TPU v7x, 128 devices: a whole 4x4x4 slice. The times are simulated.
128 devices in a mesh: ctx: 4 (over y), ch: 32 (over z, x, core).
Axes of the slice: x: 4, y: 4, z: 4, core: 2. Of those that a mesh axis runs over, the one named last changes fastest.
Arguments:
- streams: bfloat16 [16384, 3, 8192], P(('ctx', 'ch')), may hold values from -6 to 6
- load_counts: int32 [4, 32], P('ctx'), may hold values from 1 to 128, 2048 in all within a row
- seg_ids: int32 [8192], P('ctx'), may hold values from 0 to 3, never falling along the last dimension, each value on 1 to 4096 neighbouring positions
- rates: float32 [8192, 16], P('ch'), may hold values from 1.2207031e-05 to 0.05
- residues: float32 [8192, 16], P('ch'), may hold values from -1.5 to 1.5
- skip: float32 [8192], P('ch'), may hold values from 0.5 to 1.5
Outputs:
- mixed: bfloat16 [8192, 8192], P('ctx', 'ch')
Inputs may be any that keep to these rules, and one draw needn't show every extreme that they name: `load_counts`: each row sums to 2048 and its largest entry equals 128. `seg_ids`: never falls; each segment holds 1 to 4096 positions, one exactly that many.
All inputs are finite; a program needn't handle non-finite values.
Results may differ from a plain program's by a relative error of at most 0.0049.
Values may be sent and summed in bfloat16 or wider, within the bound.
No kernel may reach another device: no remote copies, remote signals or barrier semaphores. Data moves between devices by JAX's collectives and lax.ppermute only.
A program may use at most 192 MiB of HBM per device.

v0:
```python
import jax
import jax.numpy as jnp
from jax import lax
from jax.sharding import PartitionSpec as P

BLOCK = 128


def passed_along(value, axis, steps):
    count = lax.axis_size(axis)
    initial, last = (max(0, -steps), min(count, count - steps))
    return lax.ppermute(value, axis, [(source, source + steps) for source in range(initial, last)])


def chain_blocks(first_pair, second_pair):
    return (first_pair[0] * second_pair[0], second_pair[0] * first_pair[1] + second_pair[1])


def shards(streams, load_counts, seg_ids, rates, residues, skip):
    capacity = streams.shape[0]
    groups = lax.axis_size("ch")
    channels = rates.shape[0]
    modes = rates.shape[1]
    length = seg_ids.shape[0]
    arrived = lax.all_to_all(
        streams.reshape(capacity, 3, groups, channels),
        "ch",
        split_axis=2,
        concat_axis=0,
        tiled=True,
    )
    query_all = arrived[:, 0, 0]
    signal_all = (
        arrived[:, 1, 0].astype(jnp.float32) * arrived[:, 2, 0].astype(jnp.float32)
    ).astype(jnp.bfloat16)
    counts = load_counts[0]
    ending = jnp.cumsum(counts)
    position = jnp.arange(length, dtype=jnp.int32)
    passed = ending[None, :] <= position[:, None]
    source = jnp.sum(passed.astype(jnp.int32), axis=1)
    starts = jnp.sum(jnp.where(passed, counts[None, :], 0), axis=1)
    picked = source * capacity + position - starts
    query = jnp.take(query_all, picked, axis=0)
    signal = jnp.take(signal_all, picked, axis=0).astype(jnp.float32)
    rate_rows = jnp.transpose(rates)
    residue_rows = jnp.transpose(residues)
    blocks = length // BLOCK
    within = jnp.arange(BLOCK, dtype=jnp.float32)
    gain = jnp.sqrt(-jnp.expm1(-2.0 * rate_rows))
    grow = jnp.exp(within[:, None, None] * rate_rows[None]) * gain[None]
    shrink = jnp.exp(-within[:, None, None] * rate_rows[None])
    step_in = jnp.exp(-(within[:, None, None] + 1.0) * rate_rows[None])
    lifted = (signal.reshape(blocks, BLOCK, 1, channels) * grow[None]).reshape(
        blocks, BLOCK, modes * channels
    )
    doc_block = seg_ids.reshape(blocks, BLOCK)
    causal = (within[:, None] >= within[None, :])[None]
    same_doc = ((doc_block[:, :, None] == doc_block[:, None, :]) & causal).astype(jnp.float32)
    summed = jnp.einsum("bts,bsk->btk", same_doc, lifted, precision=lax.Precision.HIGHEST)
    inner = summed.reshape(blocks, BLOCK, modes, channels) * shrink[None]
    block_end = inner[:, -1]
    linked = jnp.concatenate(
        [
            jnp.zeros((1,), jnp.float32),
            (doc_block[1:, -1] == doc_block[:-1, -1]).astype(jnp.float32),
        ]
    )
    block_decay = jnp.exp(-float(BLOCK) * rate_rows)
    _, after = lax.associative_scan(
        chain_blocks, (linked[:, None, None] * block_decay[None], block_end)
    )
    block_in = jnp.concatenate([jnp.zeros((1, modes, channels), jnp.float32), after[:-1]])
    prior_doc = jnp.concatenate([doc_block[:1, 0], doc_block[:-1, -1]])
    block_flag = (doc_block == prior_doc[:, None]).astype(jnp.float32)
    span_state = after[-1]
    span_decay = jnp.exp(-float(length) * rate_rows)
    first_doc = seg_ids[0].astype(jnp.float32)
    last_doc = seg_ids[-1].astype(jnp.float32)
    whole = (seg_ids[0] == seg_ids[-1]).astype(jnp.float32)
    state_in = jnp.zeros((modes, channels), jnp.float32)
    doc_in = jnp.float32(-1.0)
    leading = lax.axis_index("ctx") == 0
    for repeat in range(lax.axis_size("ctx") - 1):
        joined = whole * ((first_doc == doc_in) | (doc_in < 0)).astype(jnp.float32)
        sending = span_state + joined * span_decay * state_in
        received, prior = passed_along((sending, last_doc), "ctx", 1)
        state_in = jnp.where(leading, jnp.zeros_like(received), received)
        doc_in = jnp.where(leading, jnp.float32(-1.0), prior)
    span_flag = (doc_block.astype(jnp.float32) == doc_in).astype(jnp.float32)
    start_decay = jnp.exp(
        -(jnp.arange(blocks, dtype=jnp.float32) * float(BLOCK))[:, None, None] * rate_rows[None]
    )
    carried = (
        block_flag[:, :, None, None] * block_in[:, None]
        + span_flag[:, :, None, None] * (start_decay * state_in[None])[:, None]
    )
    total = inner + step_in[None] * carried
    conv = jnp.sum(total * residue_rows[None, None], axis=2).reshape(length, channels)
    mixed = query.astype(jnp.float32) * (conv + skip[None, :] * signal)
    return mixed.astype(jnp.bfloat16)


def solution(mesh):
    return jax.shard_map(
        shards,
        mesh=mesh,
        in_specs=(
            P(("ctx", "ch"), None, None),
            P("ctx", None),
            P("ctx"),
            P("ch", None),
            P("ch", None),
            P("ch"),
        ),
        out_specs=P("ctx", "ch"),
        check_vma=False,
    )
```

profile of v0, /device:TPU:0, one launch (start us, length us, event | category | flops | bytes accessed | tf_op | source)
XLA Modules:
  0.0 309.7 jit_solution(7241272509679679447)
XLA Ops:
  0.0 8.5 %copy.24 = bf16[128,3,8192]{0,2,1:T(8,128)(2,1)} copy(bf16[128,3,8192]{2,0,1:T(8,128)(2,1)} %param.8) | data formatting | bytes 12582912 | tf_op args[0]
  8.5 8.7 %copy.25 = bf16[128,3,32,256]{3,0,1,2:T(8,128)(2,1)} copy(bf16[128,3,32,256]{0,3,2,1:T(8,128)(2,1)} %bitcast.61) | data formatting | bytes 12582912 | tf_op jit(solution)/shard_map/reshape | solution.py:26
  17.2 8.5 %all-to-all-start = ((bf16[128,3,32,256]{3,0,1,2:T(8,128)(2,1)}), bf16[128,3,32,256]{3,0,1,2:T(8,128)(2,1)}, u32[]{:S(2)}, u32[]{:S(2)}) async-start(bf16[128,3,32,256]{3,0,1,2:T(8,128)(2,1)} %copy.25), calls=%async_computation | async-start | bytes 12582912 | tf_op jit(solution)/shard_map/all_to_all | solution.py:25
  26.9 4.8 %collective-permute-start = (f32[]{:T(128)}, f32[]{:T(128)}, u32[]{:S(2)}, u32[]{:S(2)}) collective-permute-start(f32[]{:T(128)} %bitcast.14), channel_id=1, source_target_pairs={{0,32},{32,64},{64,96},{1,33},{33,65},{65,97},{2,34},{34,66},{66,9... | collective-permute-start | bytes 20 | tf_op jit(solution)/shard_map/ppermute | solution.py:12
  36.3 2.6 multiply_exponential_fusion
  38.9 1.6 exponential_multiply_fusion
  41.9 61.6 %all-to-all-done = bf16[128,3,32,256]{3,0,1,2:T(8,128)(2,1)} async-done(((bf16[128,3,32,256]{3,0,1,2:T(8,128)(2,1)}), bf16[128,3,32,256]{3,0,1,2:T(8,128)(2,1)}, u32[]{:S(2)}, u32[]{:S(2)}) %all-to-all-start) | async-done | bytes 6291488 | tf_op jit(solution)/shard_map/all_to_all | solution.py:25
  103.6 3.2 %copy.26 = bf16[32,128,3,1,256]{4,1,0,2,3:T(8,128)(2,1)S(1)} copy(bf16[32,128,3,1,256]{4,1,2,0,3:T(8,128)(2,1)} %bitcast.4) | data formatting | bytes 12582912 | tf_op jit(solution)/shard_map/all_to_all | solution.py:25
  106.8 2.0 fusion.3
  109.0 8.7 %gather_fusion.1 = bf16[2048,256]{1,0:T(8,128)(2,1)S(1)} fusion(bf16[4096,256]{1,0:T(8,128)(2,1)} %fusion.3, s32[2048]{0:T(1024)S(1)} %broadcast_clamp_fusion), kind=kCustom, calls=%fused_computation.1.clone | custom fusion | bytes 2105344 | tf_op jit(solution)/shard_map/jit(_take)/gather | solution.py:44
  118.0 11.1 %mul.282 = f32[16,128,16,256]{3,2,1,0:T(8,128)} broadcast(f32[16,128,256]{2,1,0:T(8,128)S(1)} %bitcast.62), dimensions={0,1,3} | broadcast | bytes 35651584 | tf_op jit(solution)/shard_map/mul | solution.py:53
  129.1 35.9 %mul.283 = f32[16,128,4096]{2,1,0:T(8,128)} reshape(f32[16,128,16,256]{3,2,1,0:T(8,128)} %mul.282) | data formatting | bytes 67108864 | tf_op jit(solution)/shard_map/mul | solution.py:53
  165.0 30.2 %fusion = f32[16,128,4096]{2,1,0:T(8,128)} fusion(f32[16,128,4096]{2,1,0:T(8,128)} %mul.283, f32[128,4096]{1,0:T(8,128)} %exponential_multiply_fusion, s32[16,128]{1,0:T(8,128)S(1)} %bitcast.68, pred[128,128]{1,0:T(8,128)(4,1)S(1)} %iota_compare_fusion.1), kind=kOutput, calls=%fused_computation.4 | convolution fusion | flops 12893814784 | bytes 69230592 | tf_op jit(solution)/shard_map/bts,bsk->btk/dot_general | solution.py:59
  195.2 19.8 %copy.29 = f32[256,8,16,256]{3,2,1,0:T(8,128)S(1)} copy(f32[256,8,16,256]{3,1,2,0:T(8,128)} %bitcast.58) | data formatting | bytes 67108864
  215.0 17.9 %bitcast_multiply_fusion = f32[16,128,16,256]{3,2,1,0:T(8,128)} fusion(f32[128,16,256]{2,1,0:T(8,128)} %get-tuple-element.24, f32[16,128,16,256]{3,2,1,0:T(8,128)S(1)} %bitcast.56), kind=kLoop, calls=%fused_computation.2 | loop fusion | flops 8388608 | bytes 69206016 | tf_op jit(solution)/shard_map/mul | solution.py:60
  232.9 4.1 %copy-done = f32[256,8,16,256]{3,2,1,0:T(8,128)} copy-done((f32[256,8,16,256]{3,2,1,0:T(8,128)}, f32[256,8,16,256]{3,2,1,0:T(8,128)S(1)}, u32[]{:S(2)}) %copy-start) | copy-done | bytes 33554456
  240.6 1.9 pad.28
  242.6 2.0 pad.29
  245.4 1.5 add.98
  246.9 1.3 pad_maximum_fusion.1
  248.2 1.5 pad.30
  249.7 3.3 %pad.31 = f32[8,16,256]{2,1,0:T(8,128)} pad(f32[4,16,256]{2,1,0:T(8,128)} %add.98, f32[]{:T(128)} %constant.14.clone.1), padding=1_0_1x0_0_0x0_0_0 | pad | bytes 196612 | tf_op jit(solution)/shard_map/pad | solution.py:69
  253.0 1.6 fusion.11
  255.6 3.5 %collective-permute-start.1 = (f32[16,256]{1,0:T(8,128)S(1)}, f32[16,256]{1,0:T(8,128)S(1)}, u32[]{:S(2)}, u32[]{:S(2)}) collective-permute-start(f32[16,256]{1,0:T(8,128)S(1)} %get-tuple-element.10), channel_id=1, source_target_pairs={{0,32},{32,64},{64,96},{1,33},{33,65},{65,97},{2,34},{34,66},{66,9... | collective-permute-start | bytes 49160 | tf_op jit(solution)/shard_map/ppermute | solution.py:12
  261.2 4.8 %collective-permute-start.2 = (f32[16,256]{1,0:T(8,128)}, f32[16,256]{1,0:T(8,128)}, u32[]{:S(2)}, u32[]{:S(2)}) collective-permute-start(f32[16,256]{1,0:T(8,128)} %bitcast_add_fusion.2), channel_id=1, source_target_pairs={{0,32},{32,64},{64,96},{1,33},{33,65},{65,97},{2,34},{34,66},{66,9... | collective-permute-start | bytes 49160 | tf_op jit(solution)/shard_map/ppermute | solution.py:12
  266.0 1.5 pad_maximum_fusion
  267.6 4.8 %pad.32 = f32[16,16,256]{2,1,0:T(8,128)} pad(f32[8,16,256]{2,1,0:T(8,128)} %pad_maximum_fusion, f32[]{:T(128)} %constant.14.clone.1), padding=0_1_1x0_0_0x0_0_0 | pad | bytes 393220 | tf_op jit(solution)/shard_map/pad | solution.py:69
  273.8 3.5 %collective-permute-start.3 = (f32[16,256]{1,0:T(8,128)}, f32[16,256]{1,0:T(8,128)}, u32[]{:S(2)}, u32[]{:S(2)}) collective-permute-start(f32[16,256]{1,0:T(8,128)} %bitcast_add_fusion.1), channel_id=1, source_target_pairs={{0,32},{32,64},{64,96},{1,33},{33,65},{65,97},{2,34},{34,66},{66,9... | collective-permute-start | bytes 49160 | tf_op jit(solution)/shard_map/ppermute | solution.py:12
  277.3 1.7 slice_add_fusion
  279.0 10.0 %gather_fusion = bf16[2048,256]{1,0:T(8,128)(2,1)} fusion(bf16[4096,256]{1,0:T(8,128)(2,1)S(1)} %slice_bitcast_fusion, s32[2048]{0:T(1024)} %copy-done.8), kind=kCustom, calls=%fused_computation.clone | custom fusion | bytes 2105344 | tf_op jit(solution)/shard_map/jit(_take)/gather | solution.py:43
  289.2 18.8 %multiply_reduce_fusion = f32[16,128,256]{2,1,0:T(8,128)S(1)} fusion(f32[16,256]{1,0:T(8,128)S(1)} %bitcast.71, f32[16,16,256]{2,1,0:T(8,128)S(1)} %exponential_multiply_fusion.1, f32[16,128]{1,0:T(8,128)S(1)} %copy-done.10, f32[16,16,256]{2,1,0:T(8,128)S(1)} %concatenate.27, f32[16,128]{1,0:T(8,128)S(1)} %copy-done.9, f32[128,16,256]{2,1,0:T(8,128)} %get-tuple-element.23, ...), kind=kLoop, calls=%fused_computation.3 | loop fusion | flops 66584576 | bytes 40402944 | tf_op jit(solution)/shard_map/reduce_sum | solution.py:98
  308.0 1.7 fusion.5
  (79 shorter events, 13.5 us)
Async XLA Ops:
  17.2 8.5 %copy-start.6 = (s32[2048]{0:T(1024)S(1)}, s32[2048]{0:T(1024)}, u32[]{:S(2)}) copy-start(s32[2048]{0:T(1024)} %param.10) | copy-start | bytes 24580
  17.2 17.0 %copy-start.4 = (f32[256,16]{0,1:T(8,128)S(1)}, f32[256,16]{0,1:T(8,128)}, u32[]{:S(2)}) copy-start(f32[256,16]{0,1:T(8,128)} %param.11) | copy-start | bytes 49156
  17.2 17.0 %copy-start.14 = (s32[1,32]{1,0:T(1,128)S(1)}, s32[1,32]{1,0:T(1,128)}, u32[]{:S(2)}) copy-start(s32[1,32]{1,0:T(1,128)} %param.9) | copy-start | bytes 388
  17.2 86.4 %all-to-all-start = ((bf16[128,3,32,256]{3,0,1,2:T(8,128)(2,1)}), bf16[128,3,32,256]{3,0,1,2:T(8,128)(2,1)}, u32[]{:S(2)}, u32[]{:S(2)}) async-start(bf16[128,3,32,256]{3,0,1,2:T(8,128)(2,1)} %copy.25), calls=%async_computation | async-start | bytes 12582912 | tf_op jit(solution)/shard_map/all_to_all | solution.py:25
  26.9 13.6 %collective-permute-start = (f32[]{:T(128)}, f32[]{:T(128)}, u32[]{:S(2)}, u32[]{:S(2)}) collective-permute-start(f32[]{:T(128)} %bitcast.14), channel_id=1, source_target_pairs={{0,32},{32,64},{64,96},{1,33},{33,65},{65,97},{2,34},{34,66},{66,9... | collective-permute-start | bytes 20 | tf_op jit(solution)/shard_map/ppermute | solution.py:12
  36.2 81.4 %copy-start.11 = (pred[2048]{0:T(1024)(128)(4,1)}, pred[2048]{0:T(1024)(128)(4,1)S(1)}, u32[]{:S(2)}) copy-start(pred[2048]{0:T(1024)(128)(4,1)S(1)} %compare_and_fusion) | copy-start | bytes 6148
  36.2 72.7 %copy-start.8 = (s32[2048]{0:T(1024)}, s32[2048]{0:T(1024)S(1)}, u32[]{:S(2)}) copy-start(s32[2048]{0:T(1024)S(1)} %broadcast_clamp_fusion) | copy-start | bytes 24580
  215.0 21.9 %copy-start = (f32[256,8,16,256]{3,2,1,0:T(8,128)}, f32[256,8,16,256]{3,2,1,0:T(8,128)S(1)}, u32[]{:S(2)}) copy-start(f32[256,8,16,256]{3,2,1,0:T(8,128)S(1)} %copy.29) | copy-start | bytes 100663296
  237.9 0.7 copy-start.2
  238.7 0.7 copy-start.5
  255.6 10.3 %copy-start.7 = (f32[1,16,256]{2,1,0:T(8,128)}, f32[1,16,256]{2,1,0:T(8,128)S(1)}, u32[]{:S(2)}) copy-start(f32[1,16,256]{2,1,0:T(8,128)S(1)} %get-tuple-element.11) | copy-start | bytes 49156
  255.6 4.9 %collective-permute-start.1 = (f32[16,256]{1,0:T(8,128)S(1)}, f32[16,256]{1,0:T(8,128)S(1)}, u32[]{:S(2)}, u32[]{:S(2)}) collective-permute-start(f32[16,256]{1,0:T(8,128)S(1)} %get-tuple-element.10), channel_id=1, source_target_pairs={{0,32},{32,64},{64,96},{1,33},{33,65},{65,97},{2,34},{34,66},{66,9... | collective-permute-start | bytes 49160 | tf_op jit(solution)/shard_map/ppermute | solution.py:12
  261.2 11.2 %collective-permute-start.2 = (f32[16,256]{1,0:T(8,128)}, f32[16,256]{1,0:T(8,128)}, u32[]{:S(2)}, u32[]{:S(2)}) collective-permute-start(f32[16,256]{1,0:T(8,128)} %bitcast_add_fusion.2), channel_id=1, source_target_pairs={{0,32},{32,64},{64,96},{1,33},{33,65},{65,97},{2,34},{34,66},{66,9... | collective-permute-start | bytes 49160 | tf_op jit(solution)/shard_map/ppermute | solution.py:12
  273.8 15.2 %collective-permute-start.3 = (f32[16,256]{1,0:T(8,128)}, f32[16,256]{1,0:T(8,128)}, u32[]{:S(2)}, u32[]{:S(2)}) collective-permute-start(f32[16,256]{1,0:T(8,128)} %bitcast_add_fusion.1), channel_id=1, source_target_pairs={{0,32},{32,64},{64,96},{1,33},{33,65},{65,97},{2,34},{34,66},{66,9... | collective-permute-start | bytes 49160 | tf_op jit(solution)/shard_map/ppermute | solution.py:12
  278.9 10.0 %copy-start.3 = (f32[15,16,256]{2,1,0:T(8,128)S(1)}, f32[15,16,256]{2,1,0:T(8,128)}, u32[]{:S(2)}) copy-start(f32[15,16,256]{2,1,0:T(8,128)} %slice_add_fusion) | copy-start | bytes 737284
  278.9 10.1 %copy-start.16 = (f32[16]{0:T(128)S(1)}, f32[16]{0:T(128)}, u32[]{:S(2)}) copy-start(f32[16]{0:T(128)} %multiply_negate_fusion) | copy-start | bytes 196
  278.9 10.2 %copy-start.9 = (f32[16,128]{1,0:T(8,128)S(1)}, f32[16,128]{1,0:T(8,128)}, u32[]{:S(2)}) copy-start(f32[16,128]{1,0:T(8,128)} %get-tuple-element.27) | copy-start | bytes 24580
  278.9 10.2 %copy-start.10 = (f32[16,128]{1,0:T(8,128)S(1)}, f32[16,128]{1,0:T(8,128)}, u32[]{:S(2)}) copy-start(f32[16,128]{1,0:T(8,128)} %get-tuple-element.28) | copy-start | bytes 24580
  278.9 10.2 %copy-start.13 = (f32[256,16]{0,1:T(8,128)S(1)}, f32[256,16]{0,1:T(8,128)}, u32[]{:S(2)}) copy-start(f32[256,16]{0,1:T(8,128)} %param.12) | copy-start | bytes 49156
  289.2 18.8 %copy-start.1 = (bf16[2048,256]{1,0:T(8,128)(2,1)S(1)}, bf16[2048,256]{1,0:T(8,128)(2,1)}, u32[]{:S(2)}) copy-start(bf16[2048,256]{1,0:T(8,128)(2,1)} %gather_fusion) | copy-start | bytes 3145732
  289.2 18.8 %copy-start.12 = (pred[2048]{0:T(1024)(128)(4,1)S(1)}, pred[2048]{0:T(1024)(128)(4,1)}, u32[]{:S(2)}) copy-start(pred[2048]{0:T(1024)(128)(4,1)} %copy-done.11) | copy-start | bytes 6148
  289.2 18.8 %copy-start.15 = (f32[256]{0:T(256)S(1)}, f32[256]{0:T(256)}, u32[]{:S(2)}) copy-start(f32[256]{0:T(256)} %param.13) | copy-start | bytes 3076
where the time goes:
time: 313 us; the launch traced here: 310 us
  local copies, waits for them, and re-layouts  128 us (41%)
  waiting for transfers between devices  62.3 us (20%)
  other arithmetic  60.2 us (19%)
  matrix products  30.2 us (10%)
  starting transfers between devices  25.1 us (8%)
  between operations  3.67 us (1%)
    all_to_all x1, waiting for transfers between devices, shards(): lax.all_to_all(streams.reshape(capacity, 3, groups, channels), 'ch', spli...  61.6 us
    mul x2, local copies, waits for them, and re-layouts, shards(): signal.reshape(blocks, BLOCK, 1, channels) * grow[None]  47 us
    unnamed x39, local copies, waits for them, and re-layouts  33.2 us
    dot_general x1, matrix products, shards(): jnp.einsum('bts,bsk->btk', same_doc, lifted, precision=lax.Precision.HIGH...  30.2 us
    reduce_sum x1, other arithmetic, shards(): jnp.sum(total * residue_rows[None, None], axis=2).reshape(length, channels)  18.8 us
    mul x1, other arithmetic, shards(): inner = summed.reshape(blocks, BLOCK, modes, channels) * shrink[None]  17.9 us
    ppermute x4, starting transfers between devices, passed_along(): lax.ppermute(value, axis, [(source, source + steps) for source in range(i...  16.6 us
    pad x6, local copies, waits for them, and re-layouts, shards(): lax.associative_scan(chain_blocks, (linked[:, None, None] * block_decay[N...  13.5 us
  transfers between devices with their start and end apart: 5, of which 2 were waited for; matrix products, arithmetic and copies ran while one was open for 9% of the time, Pallas kernels for 0%

commit v1 on v0

v1 whole, which is shorter than its diff:
```python
import functools

import jax
import jax.numpy as jnp
from jax import lax
from jax.experimental import pallas as pl
from jax.experimental.pallas import tpu as pltpu
from jax.sharding import PartitionSpec as P

BLOCK = 128
STEPS = 16
LANES = 128
SUB = 8
F32 = jnp.float32
BF16 = jnp.bfloat16


def slot_position(shape, dim):
    slot = lax.broadcasted_iota(jnp.int32, shape, dim)
    return (slot & (SUB - 1)) * STEPS + (slot >> 3)


def rotation(shift):
    place = slot_position((BLOCK, BLOCK), 0)
    row = lax.broadcasted_iota(jnp.int32, (BLOCK, BLOCK), 1)
    return jnp.where(((row + shift) & (BLOCK - 1)) == place, 1.0, 0.0).astype(BF16)


def send_signal_kernel(shift, key_ref, value_ref, out_ref):
    turn = rotation(shift[0])
    signal = (key_ref[0].astype(F32) * value_ref[0].astype(F32)).astype(BF16)
    moved = jnp.dot(turn, signal, preferred_element_type=F32).astype(BF16)
    channels = out_ref.shape[2]
    for part in range(out_ref.shape[0]):
        out_ref[part] = moved[:, part * channels : (part + 1) * channels]


def send_query_kernel(shift, query_ref, out_ref):
    turn = rotation(shift[0])
    moved = jnp.dot(turn, query_ref[0], preferred_element_type=F32).astype(BF16)
    channels = out_ref.shape[2]
    for part in range(out_ref.shape[0]):
        out_ref[part] = moved[:, part * channels : (part + 1) * channels]


def send(kernel, planes, streams, shift, groups, channels, step):
    rows = streams.shape[1]
    return pl.pallas_call(
        kernel,
        out_shape=jax.ShapeDtypeStruct((groups, rows, channels), BF16),
        grid_spec=pltpu.PrefetchScalarGridSpec(
            num_scalar_prefetch=1,
            grid=(groups // step,),
            in_specs=[
                pl.BlockSpec((1, rows, step * channels), functools.partial(lambda plane, i, s: (plane, 0, i), plane))
                for plane in planes
            ],
            out_specs=pl.BlockSpec((step, rows, channels), lambda i, s: (i, 0, 0)),
        ),
    )(shift, *[streams for _ in planes])


def segment(position, bounds):
    total = (position >= bounds[0]).astype(jnp.int32)
    for bound in bounds[1:]:
        total = total + (position >= bound).astype(jnp.int32)
    return total


def gather_block(block, starts, first, last, arrived_ref, into_ref):
    place = slot_position(into_ref.shape, 0)

    def add(source, carry):
        low = starts[source] - block * BLOCK
        high = starts[source + 1] - block * BLOCK
        here = (place >= low) & (place < high)
        into_ref[...] = jnp.where(here, arrived_ref[source].astype(F32), into_ref[...])
        return carry

    lax.fori_loop(first[block], last[block], add, 0)


def scan_kernel(per, starts, first, last, bounds, arrived_ref, decay_ref, weight_ref, leap_ref, signal_ref, ends_ref, final_ref, held, carry):
    step = pl.program_id(0)
    limits = [bounds[k] for k in range(3)]
    modes = decay_ref.shape[0]
    channels = decay_ref.shape[2]

    @pl.when(step == 0)
    def _():
        carry[...] = jnp.zeros_like(carry)

    def one(inner, unused):
        block = step * per + inner
        begin = block * BLOCK
        gather_block(block, starts, first, last, arrived_ref, held)
        signal_ref[pl.ds(inner * BLOCK, BLOCK), :] = held[...].astype(BF16)
        first_id = segment(begin, limits)
        last_id = segment(begin + BLOCK - 1, limits)
        before_id = segment(begin - 1, limits)

        @pl.when(first_id != last_id)
        def _():
            place = slot_position(held.shape, 0)
            own = segment(begin + place, limits)
            end = segment(begin + (place | (STEPS - 1)), limits)
            held[...] = jnp.where(own == end, held[...], 0.0)

        rank = lax.broadcasted_iota(jnp.int32, (SUB, LANES), 0)
        reach = segment(begin + rank * STEPS + STEPS - 1, limits) == last_id
        going = jnp.where(before_id == last_id, 1.0, 0.0)
        for tile in range(channels // LANES):
            lanes = pl.ds(tile * LANES, LANES)
            rows = [held[pl.ds(t * SUB, SUB), lanes] for t in range(STEPS)]
            for mode in range(modes):
                decay = decay_ref[mode, :, lanes]
                state = rows[0]
                for t in range(1, STEPS):
                    state = decay * state + rows[t]
                ends_ref[inner, mode, :, lanes] = state
                kept = jnp.where(reach, weight_ref[mode, :, lanes] * state, 0.0)
                carry[mode, :, lanes] = (going * leap_ref[mode, :, lanes]) * carry[mode, :, lanes] + kept
        return unused

    lax.fori_loop(0, per, one, 0)

    @pl.when(step == pl.num_programs(0) - 1)
    def _():
        final_ref[...] = jnp.sum(carry[...], axis=1)


def conv_kernel(
    per, bounds, signal_ref, ends_ref, near_ref, far_ref, farther_ref, decay_ref, one_ref, two_ref, four_ref, onward_ref, scale_ref, taps_ref, span_ref, out_ref, state
):
    step = pl.program_id(0)
    limits = [bounds[k] for k in range(3)]
    modes = decay_ref.shape[0]
    channels = decay_ref.shape[2]

    @pl.when(step == 0)
    def _():
        start_id = segment(0, limits).astype(F32)
        span = span_ref[...]

        def ids(ref):
            return ref[modes : modes + 1, :], ref[modes + 1 : modes + 2, :]

        near_first, near_last = ids(near_ref)
        far_first, far_last = ids(far_ref)
        farther_first, farther_last = ids(farther_ref)
        through_far = jnp.where((far_first == far_last) & (far_first == farther_last), 1.0, 0.0)
        through_near = jnp.where((near_first == near_last) & (near_first == far_last), 1.0, 0.0)
        entering = jnp.where(near_last == start_id, 1.0, 0.0)
        inside = far_ref[0:modes, :] + through_far * span * farther_ref[0:modes, :]
        inside = near_ref[0:modes, :] + through_near * span * inside
        inside = entering * inside
        for mode in range(modes):
            state[mode] = jnp.broadcast_to(inside[mode : mode + 1], (SUB, channels))

    rank = lax.broadcasted_iota(jnp.int32, (SUB, LANES), 0)

    def one(inner, unused):
        block = step * per + inner
        begin = block * BLOCK
        last_id = segment(begin + BLOCK - 1, limits)
        before_id = segment(jnp.maximum(begin - 1, 0), limits)
        edge = segment(begin + rank * STEPS + STEPS - 1, limits)
        single = before_id == last_id

        def tiles(masked):
            if masked:
                one_in = jnp.where((rank >= 1) & (edge == pltpu.roll(edge, 1, 0)), 1.0, 0.0)
                two_in = jnp.where((rank >= 2) & (edge == pltpu.roll(edge, 2, 0)), 1.0, 0.0)
                four_in = jnp.where((rank >= 4) & (edge == pltpu.roll(edge, 4, 0)), 1.0, 0.0)
                start_in = jnp.where(edge == before_id, 1.0, 0.0)
                prior = jnp.where(rank == 0, before_id, pltpu.roll(edge, 1, 0))
                own = [segment(begin + rank * STEPS + t, limits) for t in range(STEPS)]
                open_in = [jnp.where(o == prior, 1.0, 0.0) for o in own]
            for tile in range(channels // LANES):
                lanes = pl.ds(tile * LANES, LANES)
                rows = [
                    signal_ref[pl.ds(inner * BLOCK + t * SUB, SUB), lanes].astype(F32) for t in range(STEPS)
                ]
                local = []
                for t in range(STEPS):
                    total = taps_ref[0, :, lanes] * rows[t]
                    for u in range(t):
                        term = taps_ref[t - u, :, lanes] * rows[u]
                        if masked:
                            term = jnp.where(own[t] == own[u], term, 0.0)
                        total = total + term
                    local.append(total)
                carried = [None] * STEPS
                for mode in range(modes):
                    scan = ends_ref[inner, mode, :, lanes]
                    moved = one_ref[mode, :, lanes] * pltpu.roll(scan, 1, 0)
                    scan = scan + (moved * one_in if masked else moved)
                    moved = two_ref[mode, :, lanes] * pltpu.roll(scan, 2, 0)
                    scan = scan + (moved * two_in if masked else moved)
                    moved = four_ref[mode, :, lanes] * pltpu.roll(scan, 4, 0)
                    scan = scan + (moved * four_in if masked else moved)
                    entry = state[mode, :, lanes]
                    moved = onward_ref[mode, :, lanes] * entry
                    scan = scan + (moved * start_in if masked else moved)
                    state[mode, :, lanes] = jnp.broadcast_to(scan[SUB - 1 : SUB], (SUB, LANES))
                    running = jnp.where(rank == 0, entry, pltpu.roll(scan, 1, 0)) * scale_ref[mode, :, lanes]
                    decay = decay_ref[mode, :, lanes]
                    for t in range(STEPS):
                        running = running * decay
                        carried[t] = running if carried[t] is None else carried[t] + running
                for t in range(STEPS):
                    more = carried[t] * open_in[t] if masked else carried[t]
                    out_ref[pl.ds(inner * BLOCK + t * SUB, SUB), lanes] = local[t] + more

        @pl.when(single)
        def _():
            tiles(False)

        @pl.when(jnp.logical_not(single))
        def _():
            tiles(True)

        return unused

    lax.fori_loop(0, per, one, 0)


def mix_kernel(per, starts, first, last, arrived_ref, filtered_ref, out_ref, held):
    step = pl.program_id(0)
    place = slot_position((BLOCK, BLOCK), 1)
    row = lax.broadcasted_iota(jnp.int32, (BLOCK, BLOCK), 0)
    back = jnp.where(place == row, 1.0, 0.0).astype(BF16)

    def one(inner, unused):
        gather_block(step * per + inner, starts, first, last, arrived_ref, held)
        rows = pl.ds(inner * BLOCK, BLOCK)
        mixed = (held[...] * filtered_ref[rows, :]).astype(BF16)
        out_ref[rows, :] = jnp.dot(back, mixed, preferred_element_type=F32).astype(BF16)
        return unused

    lax.fori_loop(0, per, one, 0)


def whole(array):
    zeros = (0,) * array.ndim
    return pl.BlockSpec(array.shape, lambda i, *_: zeros)


def passed_along(value, axis, steps):
    count = lax.axis_size(axis)
    return lax.ppermute(value, axis, [(source, source + steps) for source in range(count - steps)])


def shards(streams, load_counts, seg_ids, rates, residues, skip):
    capacity = streams.shape[0]
    groups = lax.axis_size("ch")
    channels, modes = rates.shape
    length = seg_ids.shape[0]
    blocks = length // BLOCK
    per = 4
    counts = load_counts[0]
    mine = lax.axis_index("ch")
    shift = jnp.sum(jnp.where(jnp.arange(groups) < mine, counts, 0)).astype(jnp.int32)[None]
    planes = jnp.transpose(streams, (1, 0, 2))
    signal_out = send(send_signal_kernel, (1, 2), planes, shift, groups, channels, 4)
    signal_in = lax.all_to_all(signal_out, "ch", split_axis=0, concat_axis=0, tiled=True)
    query_out = send(send_query_kernel, (0,), planes, shift, groups, channels, 4)
    query_in = lax.all_to_all(query_out, "ch", split_axis=0, concat_axis=0, tiled=True)

    ending = jnp.sum(jnp.where(jnp.arange(groups)[:, None] >= jnp.arange(groups)[None, :], counts[None, :], 0), axis=1)
    starts = jnp.concatenate([jnp.zeros((1,), jnp.int32), ending]).astype(jnp.int32)
    edges = jnp.arange(blocks, dtype=jnp.int32) * BLOCK
    first = jnp.sum((ending[None, :] <= edges[:, None]).astype(jnp.int32), axis=1)
    last = jnp.sum((starts[None, :-1] < edges[:, None] + BLOCK).astype(jnp.int32), axis=1)
    bounds = jnp.sum((seg_ids[None, :] < jnp.arange(1, 4, dtype=jnp.int32)[:, None]).astype(jnp.int32), axis=1)

    rate = jnp.transpose(rates)
    gain = jnp.sqrt(-jnp.expm1(-2.0 * rate))
    scale = jnp.transpose(residues) * gain
    rank = jnp.arange(SUB, dtype=F32)[None, :, None]

    def power(exponent):
        return jnp.exp(-exponent * rate[:, None, :])

    flat = jnp.zeros((1, SUB, 1), F32)
    decay = power(1.0 + flat)
    weight = power((SUB - 1.0 - rank) * STEPS)
    leap = power(float(BLOCK) + flat)
    one_coef = jnp.where(rank >= 1, power(1.0 * STEPS + flat), 0.0)
    two_coef = jnp.where(rank >= 2, power(2.0 * STEPS + flat), 0.0)
    four_coef = jnp.where(rank >= 4, power(4.0 * STEPS + flat), 0.0)
    onward = power((rank + 1.0) * STEPS)
    scale_b = jnp.broadcast_to(scale[:, None, :], (modes, SUB, channels))
    lag = jnp.arange(STEPS, dtype=F32)[:, None, None]
    taps = jnp.sum(scale[None] * jnp.exp(-lag * rate[None]), axis=1)
    taps = taps + jnp.where(jnp.arange(STEPS)[:, None] == 0, skip[None, :], 0.0)
    taps_b = jnp.broadcast_to(taps[:, None, :], (STEPS, SUB, channels))
    span = jnp.exp(-float(length) * rate)

    coefficients = (decay, weight, leap)
    signal, ends, final = pl.pallas_call(
        functools.partial(scan_kernel, per),
        out_shape=(
            jax.ShapeDtypeStruct((length, channels), BF16),
            jax.ShapeDtypeStruct((blocks, modes, SUB, channels), F32),
            jax.ShapeDtypeStruct((modes, channels), F32),
        ),
        grid_spec=pltpu.PrefetchScalarGridSpec(
            num_scalar_prefetch=4,
            grid=(blocks // per,),
            in_specs=[whole(signal_in)] + [whole(c) for c in coefficients],
            out_specs=(
                pl.BlockSpec((per * BLOCK, channels), lambda i, *_: (i, 0)),
                pl.BlockSpec((per, modes, SUB, channels), lambda i, *_: (i, 0, 0, 0)),
                pl.BlockSpec((modes, channels), lambda i, *_: (0, 0)),
            ),
            scratch_shapes=[pltpu.VMEM((BLOCK, channels), F32), pltpu.VMEM((modes, SUB, channels), F32)],
        ),
    )(starts, first, last, bounds, signal_in, *coefficients)

    ids = jnp.stack([seg_ids[0], seg_ids[-1]]).astype(F32)
    passing = jnp.concatenate(
        [final, jnp.broadcast_to(ids[:, None], (2, channels)), jnp.zeros((SUB - 2, channels), F32)]
    )
    near = passed_along(passing, "ctx", 1)
    far = passed_along(passing, "ctx", 2)
    farther = passed_along(passing, "ctx", 3)

    resident = (near, far, farther, decay, one_coef, two_coef, four_coef, onward, scale_b, taps_b, span)
    filtered = pl.pallas_call(
        functools.partial(conv_kernel, per),
        out_shape=jax.ShapeDtypeStruct((length, channels), F32),
        grid_spec=pltpu.PrefetchScalarGridSpec(
            num_scalar_prefetch=1,
            grid=(blocks // per,),
            in_specs=[
                pl.BlockSpec((per * BLOCK, channels), lambda i, *_: (i, 0)),
                pl.BlockSpec((per, modes, SUB, channels), lambda i, *_: (i, 0, 0, 0)),
            ]
            + [whole(r) for r in resident],
            out_specs=pl.BlockSpec((per * BLOCK, channels), lambda i, *_: (i, 0)),
            scratch_shapes=[pltpu.VMEM((modes, SUB, channels), F32)],
        ),
    )(bounds, signal, ends, *resident)

    return pl.pallas_call(
        functools.partial(mix_kernel, per),
        out_shape=jax.ShapeDtypeStruct((length, channels), BF16),
        grid_spec=pltpu.PrefetchScalarGridSpec(
            num_scalar_prefetch=3,
            grid=(blocks // per,),
            in_specs=[whole(query_in), pl.BlockSpec((per * BLOCK, channels), lambda i, *_: (i, 0))],
            out_specs=pl.BlockSpec((per * BLOCK, channels), lambda i, *_: (i, 0)),
            scratch_shapes=[pltpu.VMEM((BLOCK, channels), F32)],
        ),
    )(starts, first, last, query_in, filtered)


def solution(mesh):
    return jax.shard_map(
        shards,
        mesh=mesh,
        in_specs=(
            P(("ctx", "ch"), None, None),
            P("ctx", None),
            P("ctx"),
            P("ch", None),
            P("ch", None),
            P("ch"),
        ),
        out_specs=P("ctx", "ch"),
        check_vma=False,
    )
```

time: 313 us -> 97.1 us (0.31)
  local copies, waits for them, and re-layouts: 128 us -> 6.1 us
  other arithmetic: 60.2 us -> 8.37 us
  waiting for transfers between devices: 62.3 us -> 22.1 us
  Pallas kernels: 0 us -> 36.8 us
  matrix products: 30.2 us -> 0 us
  between operations: 3.67 us -> 0.15 us
  starting transfers between devices: 25.1 us -> 21.9 us
    mul x2, local copies, waits for them, and re-layouts: 47 us -> 1.32 us  [power(): return jnp.exp(-exponent * rate[:, None, :])]
    all_to_all x1 -> x2, waiting for transfers between devices: 61.6 us -> 20.7 us  [the longest x1 20.7 us: shards(): lax.all_to_all(signal_out, 'ch', split_axis=0, concat_axis=0, tiled=True)]
    pallas_call x0 -> x5, Pallas kernels: none -> 36.8 us  [the longest x2 14.5 us: send(): pl.pallas_call(kernel, out_shape=jax.ShapeDtypeStruct((groups, rows, chan...]
    unnamed x39 -> x22, local copies, waits for them, and re-layouts: 33.2 us -> 2.69 us
    dot_general x1 -> x0, matrix products: 30.2 us -> none  [shards(): jnp.einsum('bts,bsk->btk', same_doc, lifted, precision=lax.Precision.HIGH...]
    mul x6 -> x1, other arithmetic: 19.7 us -> 0.01 us  [shards(): edges = jnp.arange(blocks, dtype=jnp.int32) * BLOCK]
    gather x2 -> x0, local copies, waits for them, and re-layouts: 18.7 us -> none  [the longest x1 10 us: shards(): query = jnp.take(query_all, picked, axis=0)]
    reduce_sum x2 -> x5, other arithmetic: 18.9 us -> 3.08 us  [the longest x1 1.29 us: shards(): jnp.sum(jnp.where(jnp.arange(groups) < mine, counts, 0)).astype(jnp.int32)]
  transfers between devices with their start and end apart: 5 -> 5, of which waited for: 2 -> 3; matrix products, arithmetic and copies ran while one was open for 9% -> 11% of each run, Pallas kernels for 0% -> 23%
where the time goes in v1:
time: 97.1 us; the launch traced here: 95.4 us
  Pallas kernels  36.8 us (38%)
  waiting for transfers between devices  22.1 us (23%)
  starting transfers between devices  21.9 us (23%)
  other arithmetic  8.37 us (9%)
  local copies, waits for them, and re-layouts  6.1 us (6%)
    all_to_all x1, waiting for transfers between devices, shards(): lax.all_to_all(signal_out, 'ch', split_axis=0, concat_axis=0, tiled=True)  20.7 us
    pallas_call x2, Pallas kernels, send(): pl.pallas_call(kernel, out_shape=jax.ShapeDtypeStruct((groups, rows, chan...  14.5 us
    ppermute x3, starting transfers between devices, passed_along(): lax.ppermute(value, axis, [(source, source + steps) for source in range(c...  9.64 us
    all_to_all x1, starting transfers between devices, shards(): lax.all_to_all(signal_out, 'ch', split_axis=0, concat_axis=0, tiled=True)  8.24 us
    pallas_call x1, Pallas kernels, shards(): pl.pallas_call(functools.partial(conv_kernel, per), out_shape=jax.ShapeDt...  8.05 us
    pallas_call x1, Pallas kernels, shards(): pl.pallas_call(functools.partial(scan_kernel, per), out_shape=(jax.ShapeD...  7.3 us
    pallas_call x1, Pallas kernels, shards(): pl.pallas_call(functools.partial(mix_kernel, per), out_shape=jax.ShapeDty...  6.94 us
    all_to_all x1, starting transfers between devices, shards(): lax.all_to_all(query_out, 'ch', split_axis=0, concat_axis=0, tiled=True)  4.01 us
  transfers between devices with their start and end apart: 5, of which 3 were waited for; matrix products, arithmetic and copies ran while one was open for 11% of the time, Pallas kernels for 23%

profile of v1, /device:TPU:0, one launch (start us, length us, event | category | flops | bytes accessed | tf_op | source)
XLA Modules:
  0.0 95.4 jit_solution(18362645752351252222)
XLA Ops:
  0.0 1.3 %fusion = s32[]{:T(128)} fusion(s32[]{:T(128)S(6)} %axis_index.12, s32[1,32]{1,0:T(1,128)} %param.7), kind=kLoop, calls=%fused_computation.21 | loop fusion | flops 95 | bytes 136 | tf_op jit(solution)/shard_map/reduce_sum | solution.py:263
  1.3 7.5 %shard_map.65 = bf16[32,128,256]{2,1,0:T(8,128)(2,1)} custom-call(s32[1]{0:T(128)} %bitcast.1.shift, bf16[3,128,8192]{2,1,0:T(8,128)(2,1)} %bitcast.15, bf16[3,128,8192]{2,1,0:T(8,128)(2,1)} %bitcast.16), custom_call_target="tpu_custom_call" | custom-call | tf_op jit(solution)/shard_map/pallas_call | solution.py:48
  8.8 8.2 %all-to-all-start.1 = ((bf16[32,128,256]{2,1,0:T(8,128)(2,1)}), bf16[32,128,256]{2,1,0:T(8,128)(2,1)S(1)}, u32[]{:S(2)}, u32[]{:S(2)}) async-start(bf16[32,128,256]{2,1,0:T(8,128)(2,1)} %shard_map.65), calls=%async_computation.1 | async-start | bytes 4194304 | tf_op jit(solution)/shard_map/all_to_all | solution.py:266
  17.1 7.0 %shard_map.64 = bf16[32,128,256]{2,1,0:T(8,128)(2,1)} custom-call(s32[1]{0:T(128)} %bitcast.1.shift, bf16[3,128,8192]{2,1,0:T(8,128)(2,1)} %bitcast.17), custom_call_target="tpu_custom_call" | custom-call | tf_op jit(solution)/shard_map/pallas_call | solution.py:48
  24.0 0.6 fusion.1
  24.7 1.3 %add_convert_fusion = f32[2]{0:T(128)S(1)} fusion(s32[1]{0:T(128)} %get-tuple-element.21, s32[1]{0:T(128)} %get-tuple-element.20), kind=kLoop, calls=%fused_computation.23 | loop fusion | flops 4 | bytes 16 | tf_op jit(solution)/shard_map/convert_element_type | solution.py:321
  26.1 0.1 pad.2.clone
  26.2 0.1 select_reduce_fusion
  26.3 20.7 %all-to-all-done.1.arrived_ref = bf16[32,128,256]{2,1,0:T(8,128)(2,1)S(1)} async-done(((bf16[32,128,256]{2,1,0:T(8,128)(2,1)}), bf16[32,128,256]{2,1,0:T(8,128)(2,1)S(1)}, u32[]{:S(2)}, u32[]{:S(2)}) %all-to-all-start.1) | async-done | bytes 2097184 | tf_op jit(solution)/shard_map/all_to_all | solution.py:266
  47.0 1.3 %copy-done.1 = bf16[32,128,256]{2,1,0:T(8,128)(2,1)} copy-done((bf16[32,128,256]{2,1,0:T(8,128)(2,1)}, bf16[32,128,256]{2,1,0:T(8,128)(2,1)S(1)}, u32[]{:S(2)}) %copy-start.1) | copy-done | bytes 2097176
  48.3 4.0 %all-to-all-start = ((bf16[32,128,256]{2,1,0:T(8,128)(2,1)}), bf16[32,128,256]{2,1,0:T(8,128)(2,1)S(1)}, u32[]{:S(2)}, u32[]{:S(2)}) async-start(bf16[32,128,256]{2,1,0:T(8,128)(2,1)} %shard_map.64), calls=%async_computation | async-start | bytes 4194304 | tf_op jit(solution)/shard_map/all_to_all | solution.py:268
  52.5 0.8 convert_reduce_fusion.bounds
  53.2 0.8 convert_reduce_fusion.1
  54.0 0.6 multiply_exponential_fusion.2
  54.6 0.1 multiply_reduce_fusion
  54.8 0.7 broadcast_select_fusion.2.one_ref
  55.5 0.8 multiply_exponential_fusion
  56.3 0.8 broadcast_select_fusion
  57.1 0.7 mul.151.decay_ref
  57.8 0.7 mul.158.leap_ref
  58.4 7.3 %shard_map.66 = (bf16[2048,256]{1,0:T(8,128)(2,1)}, f32[16,16,8,256]{3,2,1,0:T(8,128)}, f32[16,256]{1,0:T(8,128)}) custom-call(s32[33]{0:T(128)} %copy-done.8, s32[16]{0:T(128)} %get-tuple-element.27.first, s32[16]{0:T(128)} %get-tuple-element.26.last, s32[3]{0:T(128)} %convert_reduce_fusion.bounds, bf16[32,128,256]{2,1,0:T(8,128)(2,1)} %copy-done.1, ...), custom_call_target="tpu_custom_call" | custom-call | tf_op jit(solution)/shard_map/pallas_call | solution.py:301
  65.7 0.8 maximum_maximum_fusion
  66.5 3.5 %collective-permute-start = (f32[24,256]{1,0:T(8,128)S(1)}, f32[24,256]{1,0:T(8,128)S(1)}, u32[]{:S(2)}, u32[]{:S(2)}) collective-permute-start(f32[24,256]{1,0:T(8,128)S(1)} %maximum_maximum_fusion), channel_id=1, source_target_pairs={{0,32},{32,64},{64,96},{1,33},{33,65},{65,97},{2,34},{34,66},{66,9... | collective-permute-start | bytes 73736 | tf_op jit(solution)/shard_map/ppermute | solution.py:251
  70.0 4.8 %collective-permute-start.1 = (f32[24,256]{1,0:T(8,128)S(1)}, f32[24,256]{1,0:T(8,128)S(1)}, u32[]{:S(2)}, u32[]{:S(2)}) collective-permute-start(f32[24,256]{1,0:T(8,128)S(1)} %maximum_maximum_fusion), channel_id=1, source_target_pairs={{0,64},{32,96},{1,65},{33,97},{2,66},{34,98},{3,67},{35,99},{4,68}... | collective-permute-start | bytes 73736 | tf_op jit(solution)/shard_map/ppermute | solution.py:251
  74.9 1.3 %collective-permute-start.2 = (f32[24,256]{1,0:T(8,128)S(1)}, f32[24,256]{1,0:T(8,128)S(1)}, u32[]{:S(2)}, u32[]{:S(2)}) collective-permute-start(f32[24,256]{1,0:T(8,128)S(1)} %maximum_maximum_fusion), channel_id=1, source_target_pairs={{0,96},{1,97},{2,98},{3,99},{4,100},{5,101},{6,102},{7,103},{8,104... | collective-permute-start | bytes 73736 | tf_op jit(solution)/shard_map/ppermute | solution.py:251
  76.3 0.1 collective-permute-done.1.far_ref
  76.4 1.3 %collective-permute-done.2.farther_ref = f32[24,256]{1,0:T(8,128)S(1)} collective-permute-done((f32[24,256]{1,0:T(8,128)S(1)}, f32[24,256]{1,0:T(8,128)S(1)}, u32[]{:S(2)}, u32[]{:S(2)}) %collective-permute-start.2) | collective-permute-done | bytes 24608 | tf_op jit(solution)/shard_map/ppermute | solution.py:251
  77.7 0.7 broadcast_in_dim.122.taps_ref
  78.3 0.7 broadcast_in_dim.118.scale_ref
  79.0 8.0 %shard_map.67.filtered_ref = f32[2048,256]{1,0:T(8,128)} custom-call(s32[3]{0:T(128)} %convert_reduce_fusion.bounds, bf16[2048,256]{1,0:T(8,128)(2,1)} %get-tuple-element.8.signal_ref, f32[16,16,8,256]{3,2,1,0:T(8,128)} %get-tuple-element.9.ends_ref, f32[24,256]{1,0:T(8,128)} %copy-done.3, f32[24,256]{1,0:T(8,128)} %copy-done.4, f32[24,256]{1,0:T(8,128)} %copy-done.5, ...), custom_call_target="tpu_custom_call" | custom-call | tf_op jit(solution)/shard_map/pallas_call | solution.py:330
  87.1 1.3 %copy-done = bf16[32,128,256]{2,1,0:T(8,128)(2,1)} copy-done((bf16[32,128,256]{2,1,0:T(8,128)(2,1)}, bf16[32,128,256]{2,1,0:T(8,128)(2,1)S(1)}, u32[]{:S(2)}) %copy-start) | copy-done | bytes 2097176
  88.4 6.9 %shard_map.68 = bf16[2048,256]{1,0:T(8,128)(2,1)} custom-call(s32[33]{0:T(128)} %copy-done.8, s32[16]{0:T(128)} %get-tuple-element.27.first, s32[16]{0:T(128)} %get-tuple-element.26.last, bf16[32,128,256]{2,1,0:T(8,128)(2,1)} %copy-done, f32[2048,256]{1,0:T(8,128)} %shard_map.67.filtered_ref), custom_call_target="tpu_custom_call" | custom-call | tf_op jit(solution)/shard_map/pallas_call | solution.py:346
  (35 shorter events, 0.3 us)
Async XLA Ops:
  8.8 38.2 %all-to-all-start.1 = ((bf16[32,128,256]{2,1,0:T(8,128)(2,1)}), bf16[32,128,256]{2,1,0:T(8,128)(2,1)S(1)}, u32[]{:S(2)}, u32[]{:S(2)}) async-start(bf16[32,128,256]{2,1,0:T(8,128)(2,1)} %shard_map.65), calls=%async_computation.1 | async-start | bytes 4194304 | tf_op jit(solution)/shard_map/all_to_all | solution.py:266
  17.0 7.0 %copy-start.7 = (s32[2048]{0:T(1024)S(1)}, s32[2048]{0:T(1024)}, u32[]{:S(2)}) copy-start(s32[2048]{0:T(1024)} %param.8) | copy-start | bytes 24580
  17.0 9.2 %copy-start.10 = (s32[1,32]{1,0:T(1,128)S(1)}, s32[1,32]{1,0:T(1,128)}, u32[]{:S(2)}) copy-start(s32[1,32]{1,0:T(1,128)} %param.7) | copy-start | bytes 388
  26.3 27.7 %copy-start.2 = (f32[256,16]{0,1:T(8,128)S(1)}, f32[256,16]{0,1:T(8,128)}, u32[]{:S(2)}) copy-start(f32[256,16]{0,1:T(8,128)} %param.9) | copy-start | bytes 49156
  26.3 27.7 %copy-start.6 = (f32[256,16]{0,1:T(8,128)S(1)}, f32[256,16]{0,1:T(8,128)}, u32[]{:S(2)}) copy-start(f32[256,16]{0,1:T(8,128)} %param.10) | copy-start | bytes 49156
  47.0 1.3 %copy-start.1 = (bf16[32,128,256]{2,1,0:T(8,128)(2,1)}, bf16[32,128,256]{2,1,0:T(8,128)(2,1)S(1)}, u32[]{:S(2)}) copy-start(bf16[32,128,256]{2,1,0:T(8,128)(2,1)S(1)} %all-to-all-done.1.arrived_ref) | copy-start | bytes 6291460
  48.3 38.7 %all-to-all-start = ((bf16[32,128,256]{2,1,0:T(8,128)(2,1)}), bf16[32,128,256]{2,1,0:T(8,128)(2,1)S(1)}, u32[]{:S(2)}, u32[]{:S(2)}) async-start(bf16[32,128,256]{2,1,0:T(8,128)(2,1)} %shard_map.64), calls=%async_computation | async-start | bytes 4194304 | tf_op jit(solution)/shard_map/all_to_all | solution.py:268
  52.3 23.8 %copy-start.9 = (f32[256]{0:T(256)S(1)}, f32[256]{0:T(256)}, u32[]{:S(2)}) copy-start(f32[256]{0:T(256)} %param.11) | copy-start | bytes 3076
  52.4 6.0 %copy-start.8 = (s32[33]{0:T(128)}, s32[33]{0:T(128)S(1)}, u32[]{:S(2)}) copy-start(s32[33]{0:T(128)S(1)} %pad_add_fusion.starts) | copy-start | bytes 400
  66.5 9.8 %collective-permute-start = (f32[24,256]{1,0:T(8,128)S(1)}, f32[24,256]{1,0:T(8,128)S(1)}, u32[]{:S(2)}, u32[]{:S(2)}) collective-permute-start(f32[24,256]{1,0:T(8,128)S(1)} %maximum_maximum_fusion), channel_id=1, source_target_pairs={{0,32},{32,64},{64,96},{1,33},{33,65},{65,97},{2,34},{34,66},{66,9... | collective-permute-start | bytes 73736 | tf_op jit(solution)/shard_map/ppermute | solution.py:251
  70.0 6.3 %collective-permute-start.1 = (f32[24,256]{1,0:T(8,128)S(1)}, f32[24,256]{1,0:T(8,128)S(1)}, u32[]{:S(2)}, u32[]{:S(2)}) collective-permute-start(f32[24,256]{1,0:T(8,128)S(1)} %maximum_maximum_fusion), channel_id=1, source_target_pairs={{0,64},{32,96},{1,65},{33,97},{2,66},{34,98},{3,67},{35,99},{4,68}... | collective-permute-start | bytes 73736 | tf_op jit(solution)/shard_map/ppermute | solution.py:251
  74.9 2.8 %collective-permute-start.2 = (f32[24,256]{1,0:T(8,128)S(1)}, f32[24,256]{1,0:T(8,128)S(1)}, u32[]{:S(2)}, u32[]{:S(2)}) collective-permute-start(f32[24,256]{1,0:T(8,128)S(1)} %maximum_maximum_fusion), channel_id=1, source_target_pairs={{0,96},{1,97},{2,98},{3,99},{4,100},{5,101},{6,102},{7,103},{8,104... | collective-permute-start | bytes 73736 | tf_op jit(solution)/shard_map/ppermute | solution.py:251
  76.3 2.7 %copy-start.3 = (f32[24,256]{1,0:T(8,128)}, f32[24,256]{1,0:T(8,128)S(1)}, u32[]{:S(2)}) copy-start(f32[24,256]{1,0:T(8,128)S(1)} %collective-permute-done.near_ref) | copy-start | bytes 73732
  76.4 2.6 %copy-start.4 = (f32[24,256]{1,0:T(8,128)}, f32[24,256]{1,0:T(8,128)S(1)}, u32[]{:S(2)}) copy-start(f32[24,256]{1,0:T(8,128)S(1)} %collective-permute-done.1.far_ref) | copy-start | bytes 73732
  77.7 1.3 %copy-start.5 = (f32[24,256]{1,0:T(8,128)}, f32[24,256]{1,0:T(8,128)S(1)}, u32[]{:S(2)}) copy-start(f32[24,256]{1,0:T(8,128)S(1)} %collective-permute-done.2.farther_ref) | copy-start | bytes 73732
  87.1 1.3 %copy-start = (bf16[32,128,256]{2,1,0:T(8,128)(2,1)}, bf16[32,128,256]{2,1,0:T(8,128)(2,1)S(1)}, u32[]{:S(2)}) copy-start(bf16[32,128,256]{2,1,0:T(8,128)(2,1)S(1)} %all-to-all-done.arrived_ref) | copy-start | bytes 6291460

commit v2 on v1

v2 whole, which is shorter than its diff:
```python
import functools

import jax
import jax.numpy as jnp
from jax import lax
from jax.experimental import pallas as pl
from jax.experimental.pallas import tpu as pltpu
from jax.sharding import PartitionSpec as P

BLOCK = 128
STEPS = 16
LANES = 128
SUB = 8
F32 = jnp.float32
BF16 = jnp.bfloat16


def slot_position(shape, dim):
    slot = lax.broadcasted_iota(jnp.int32, shape, dim)
    return (slot & (SUB - 1)) * STEPS + (slot >> 3)


def send_signal_kernel(key_ref, value_ref, out_ref):
    signal = key_ref[0] * value_ref[0]
    channels = out_ref.shape[2]
    for part in range(out_ref.shape[0]):
        out_ref[part] = signal[:, part * channels : (part + 1) * channels]


def send_query_kernel(shift, query_ref, out_ref):
    place = lax.broadcasted_iota(jnp.int32, (BLOCK, BLOCK), 0)
    row = lax.broadcasted_iota(jnp.int32, (BLOCK, BLOCK), 1)
    turn = jnp.where(((row + shift[0]) & (BLOCK - 1)) == place, 1.0, 0.0).astype(BF16)
    moved = jnp.dot(turn, query_ref[0], preferred_element_type=F32).astype(BF16)
    channels = out_ref.shape[2]
    for part in range(out_ref.shape[0]):
        out_ref[part] = moved[:, part * channels : (part + 1) * channels]


def send(kernel, planes, streams, scalars, groups, channels, step):
    rows = streams.shape[1]
    return pl.pallas_call(
        kernel,
        out_shape=jax.ShapeDtypeStruct((groups, rows, channels), BF16),
        grid_spec=pltpu.PrefetchScalarGridSpec(
            num_scalar_prefetch=len(scalars),
            grid=(groups // step,),
            in_specs=[
                pl.BlockSpec((1, rows, step * channels), functools.partial(lambda plane, i, *_: (plane, 0, i), plane))
                for plane in planes
            ],
            out_specs=pl.BlockSpec((step, rows, channels), lambda i, *_: (i, 0, 0)),
        ),
    )(*scalars, *[streams for _ in planes])


def segment(position, bounds):
    total = (position >= bounds[0]).astype(jnp.int32)
    for bound in bounds[1:]:
        total = total + (position >= bound).astype(jnp.int32)
    return total


def scan_kernel(starts, first, last, bounds, arrived_ref, decay_ref, weight_ref, leap_ref, signal_ref, ends_ref, final_ref, carry, gap):
    limits = [bounds[k] for k in range(3)]
    blocks, modes, _, channels = ends_ref.shape
    carry[...] = jnp.zeros_like(carry)
    row = lax.broadcasted_iota(jnp.int32, (BLOCK, BLOCK), 1)
    gap[...] = slot_position((BLOCK, BLOCK), 0) - row
    rank = lax.broadcasted_iota(jnp.int32, (SUB, LANES), 0)

    def one(block, unused):
        begin = block * BLOCK

        def picked(source):
            low = starts[source] - begin
            held = starts[source + 1] - starts[source]
            here = (gap[...] == low) & (row < held)
            return jnp.dot(
                jnp.where(here, 1.0, 0.0).astype(BF16), arrived_ref[source], preferred_element_type=F32
            )

        rows_here = pl.ds(pl.multiple_of(begin, BLOCK), BLOCK)
        signal_ref[rows_here, :] = picked(first[block])

        def add(source, carried):
            signal_ref[rows_here, :] += picked(source)
            return carried

        lax.fori_loop(first[block] + 1, last[block], add, 0)
        first_id = segment(begin, limits)
        last_id = segment(begin + BLOCK - 1, limits)
        before_id = segment(begin - 1, limits)
        reach = segment(begin + rank * STEPS + STEPS - 1, limits) == last_id
        going = jnp.where(before_id == last_id, 1.0, 0.0)

        def tiles(masked):
            if masked:
                own = [segment(begin + rank * STEPS + t, limits) for t in range(STEPS)]
            for tile in range(channels // LANES):
                lanes = pl.ds(tile * LANES, LANES)
                rows = [
                    signal_ref[pl.ds(pl.multiple_of(begin + t * SUB, SUB), SUB), lanes] for t in range(STEPS)
                ]
                if masked:
                    rows = [jnp.where(o == own[-1], r, 0.0) for o, r in zip(own, rows)]
                for mode in range(modes):
                    decay = decay_ref[mode, :, lanes]
                    state = rows[0]
                    for t in range(1, STEPS):
                        state = decay * state + rows[t]
                    ends_ref[block, mode, :, lanes] = state
                    kept = weight_ref[mode, :, lanes] * state
                    if masked:
                        kept = jnp.where(reach, kept, 0.0)
                    carry[mode, :, lanes] = (going * leap_ref[mode, :, lanes]) * carry[mode, :, lanes] + kept

        @pl.when(first_id == last_id)
        def _():
            tiles(False)

        @pl.when(first_id != last_id)
        def _():
            tiles(True)

        return unused

    lax.fori_loop(0, blocks, one, 0)
    final_ref[...] = jnp.sum(carry[...], axis=1)


def conv_kernel(
    bounds, signal_ref, ends_ref, near_ref, far_ref, farther_ref, decay_ref, one_ref, two_ref, four_ref, onward_ref, scale_ref, taps_ref, span_ref, out_ref, state
):
    limits = [bounds[k] for k in range(3)]
    blocks, modes, _, channels = ends_ref.shape
    start_id = segment(0, limits).astype(F32)

    def ids(ref):
        return ref[modes : modes + 1, :], ref[modes + 1 : modes + 2, :]

    near_first, near_last = ids(near_ref)
    far_first, far_last = ids(far_ref)
    _, farther_last = ids(farther_ref)
    through_far = jnp.where((far_first == far_last) & (far_first == farther_last), 1.0, 0.0)
    through_near = jnp.where((near_first == near_last) & (near_first == far_last), 1.0, 0.0)
    entering = jnp.where(near_last == start_id, 1.0, 0.0)
    span = span_ref[...]
    inside = far_ref[0:modes, :] + through_far * span * farther_ref[0:modes, :]
    inside = near_ref[0:modes, :] + through_near * span * inside
    inside = entering * inside
    for mode in range(modes):
        state[mode] = jnp.broadcast_to(inside[mode : mode + 1], (SUB, channels))

    rank = lax.broadcasted_iota(jnp.int32, (SUB, LANES), 0)

    def one(block, unused):
        begin = block * BLOCK
        last_id = segment(begin + BLOCK - 1, limits)
        before_id = segment(jnp.maximum(begin - 1, 0), limits)
        edge = segment(begin + rank * STEPS + STEPS - 1, limits)
        single = before_id == last_id

        def tiles(masked):
            if masked:
                one_in = jnp.where((rank >= 1) & (edge == pltpu.roll(edge, 1, 0)), 1.0, 0.0)
                two_in = jnp.where((rank >= 2) & (edge == pltpu.roll(edge, 2, 0)), 1.0, 0.0)
                four_in = jnp.where((rank >= 4) & (edge == pltpu.roll(edge, 4, 0)), 1.0, 0.0)
                start_in = jnp.where(edge == before_id, 1.0, 0.0)
                prior = jnp.where(rank == 0, before_id, pltpu.roll(edge, 1, 0))
                own = [segment(begin + rank * STEPS + t, limits) for t in range(STEPS)]
                open_in = [jnp.where(o == prior, 1.0, 0.0) for o in own]
            for tile in range(channels // LANES):
                lanes = pl.ds(tile * LANES, LANES)
                rows = [
                    signal_ref[pl.ds(pl.multiple_of(begin + t * SUB, SUB), SUB), lanes] for t in range(STEPS)
                ]
                local = []
                for t in range(STEPS):
                    total = taps_ref[0, :, lanes] * rows[t]
                    for u in range(t):
                        term = taps_ref[t - u, :, lanes] * rows[u]
                        if masked:
                            term = jnp.where(own[t] == own[u], term, 0.0)
                        total = total + term
                    local.append(total)
                carried = [None] * STEPS
                for mode in range(modes):
                    scan = ends_ref[block, mode, :, lanes]
                    moved = one_ref[mode, :, lanes] * pltpu.roll(scan, 1, 0)
                    scan = scan + (moved * one_in if masked else moved)
                    moved = two_ref[mode, :, lanes] * pltpu.roll(scan, 2, 0)
                    scan = scan + (moved * two_in if masked else moved)
                    moved = four_ref[mode, :, lanes] * pltpu.roll(scan, 4, 0)
                    scan = scan + (moved * four_in if masked else moved)
                    entry = state[mode, :, lanes]
                    moved = onward_ref[mode, :, lanes] * entry
                    scan = scan + (moved * start_in if masked else moved)
                    state[mode, :, lanes] = jnp.broadcast_to(scan[SUB - 1 : SUB], (SUB, LANES))
                    running = jnp.where(rank == 0, entry, pltpu.roll(scan, 1, 0)) * scale_ref[mode, :, lanes]
                    decay = decay_ref[mode, :, lanes]
                    for t in range(STEPS):
                        running = running * decay
                        carried[t] = running if carried[t] is None else carried[t] + running
                for t in range(STEPS):
                    more = carried[t] * open_in[t] if masked else carried[t]
                    out_ref[tile, pl.ds(begin + t, SUB, stride=STEPS), :] = local[t] + more

        @pl.when(single)
        def _():
            tiles(False)

        @pl.when(jnp.logical_not(single))
        def _():
            tiles(True)

        return unused

    lax.fori_loop(0, blocks, one, 0)


def mix_kernel(starts, first, last, arrived_ref, filtered_ref, out_ref, held, ready, sems):
    pieces = sems.shape[0]
    blocks = filtered_ref.shape[1] // BLOCK
    per = blocks // pieces
    place = lax.broadcasted_iota(jnp.int32, (BLOCK, LANES), 0)
    tiles = held.shape[1] // LANES

    def one(block, unused):
        begin = pl.multiple_of(block * BLOCK, BLOCK)

        def add(source, carried):
            low = starts[source] - begin
            here = place >= low
            for tile in range(tiles):
                lanes = pl.ds(tile * LANES, LANES)
                held[:, lanes] = jnp.where(here, arrived_ref[source, :, lanes].astype(F32), held[:, lanes])
            return carried

        lax.fori_loop(first[block], last[block], add, 0)
        rows = pl.ds(begin, BLOCK)
        for tile in range(tiles):
            lanes = pl.ds(tile * LANES, LANES)
            ready[rows, lanes] = (held[:, lanes] * filtered_ref[tile, rows, :]).astype(BF16)
        return unused

    def copy(piece):
        rows = pl.ds(piece * per * BLOCK, per * BLOCK)
        return pltpu.make_async_copy(ready.at[rows, :], out_ref.at[rows, :], sems.at[piece])

    for piece in range(pieces):
        lax.fori_loop(piece * per, (piece + 1) * per, one, 0)
        copy(piece).start()
    for piece in range(pieces):
        copy(piece).wait()


def near_by(array):
    return pltpu.with_memory_space_constraint(array, pltpu.VMEM)


def local_call(kernel, outs, scalars, arrays, scratch, out_space=pltpu.VMEM):
    return pl.pallas_call(
        kernel,
        out_shape=outs,
        in_specs=[pl.BlockSpec(memory_space=pltpu.SMEM)] * len(scalars) + [pl.BlockSpec(memory_space=pltpu.VMEM)] * len(arrays),
        out_specs=jax.tree.map(lambda _: pl.BlockSpec(memory_space=out_space), outs),
        scratch_shapes=scratch,
        compiler_params=pltpu.CompilerParams(vmem_limit_bytes=24 << 20),
    )(*scalars, *[near_by(array) for array in arrays])


def passed_along(value, axis, steps):
    count = lax.axis_size(axis)
    return lax.ppermute(value, axis, [(source, source + steps) for source in range(count - steps)])


def shards(streams, load_counts, seg_ids, rates, residues, skip):
    capacity = streams.shape[0]
    groups = lax.axis_size("ch")
    channels, modes = rates.shape
    length = seg_ids.shape[0]
    blocks = length // BLOCK
    counts = load_counts[0]
    planes = jnp.transpose(streams, (1, 0, 2))
    signal_out = send(send_signal_kernel, (1, 2), planes, (), groups, channels, 8)
    signal_in = lax.all_to_all(signal_out, "ch", split_axis=0, concat_axis=0, tiled=True)
    mine = lax.axis_index("ch")
    shift = jnp.sum(jnp.where(jnp.arange(groups) < mine, counts, 0)).astype(jnp.int32)[None]
    query_out = send(send_query_kernel, (0,), planes, (shift,), groups, channels, 8)

    ending = jnp.sum(jnp.where(jnp.arange(groups)[:, None] >= jnp.arange(groups)[None, :], counts[None, :], 0), axis=1)
    starts = jnp.concatenate([jnp.zeros((1,), jnp.int32), ending]).astype(jnp.int32)
    edges = jnp.arange(blocks, dtype=jnp.int32) * BLOCK
    first = jnp.sum((ending[None, :] <= edges[:, None]).astype(jnp.int32), axis=1)
    last = jnp.sum((starts[None, :-1] < edges[:, None] + BLOCK).astype(jnp.int32), axis=1)
    bounds = jnp.sum((seg_ids[None, :] < jnp.arange(1, 4, dtype=jnp.int32)[:, None]).astype(jnp.int32), axis=1)

    rate = jnp.transpose(rates)
    gain = jnp.sqrt(-jnp.expm1(-2.0 * rate))
    scale = jnp.transpose(residues) * gain
    rank = jnp.arange(SUB, dtype=F32)[None, :, None]

    def power(exponent):
        return jnp.exp(-exponent * rate[:, None, :])

    flat = jnp.zeros((1, SUB, 1), F32)
    decay = power(1.0 + flat)
    weight = power((SUB - 1.0 - rank) * STEPS)
    leap = power(float(BLOCK) + flat)
    one_coef = jnp.where(rank >= 1, power(1.0 * STEPS + flat), 0.0)
    two_coef = jnp.where(rank >= 2, power(2.0 * STEPS + flat), 0.0)
    four_coef = jnp.where(rank >= 4, power(4.0 * STEPS + flat), 0.0)
    onward = power((rank + 1.0) * STEPS)
    scale_b = jnp.broadcast_to(scale[:, None, :], (modes, SUB, channels))
    lag = jnp.arange(STEPS, dtype=F32)[:, None, None]
    taps = jnp.sum(scale[None] * jnp.exp(-lag * rate[None]), axis=1)
    taps = taps + jnp.where(jnp.arange(STEPS)[:, None] == 0, skip[None, :], 0.0)
    taps_b = jnp.broadcast_to(taps[:, None, :], (STEPS, SUB, channels))
    span = jnp.exp(-float(length) * rate)

    prepared = (starts, first, last, bounds, decay, weight, leap, one_coef, two_coef, four_coef, onward, scale_b, taps_b, span)
    query_out, prepared = lax.optimization_barrier((query_out, prepared))
    starts, first, last, bounds, decay, weight, leap, one_coef, two_coef, four_coef, onward, scale_b, taps_b, span = prepared
    query_in = lax.all_to_all(query_out, "ch", split_axis=0, concat_axis=0, tiled=True)

    signal, ends, final = local_call(
        scan_kernel,
        (
            pltpu.VMEM((length, channels), F32),
            pltpu.VMEM((blocks, modes, SUB, channels), F32),
            pltpu.VMEM((modes, channels), F32),
        ),
        (starts, first, last, bounds),
        (signal_in, decay, weight, leap),
        [pltpu.VMEM((modes, SUB, channels), F32), pltpu.VMEM((BLOCK, BLOCK), jnp.int32)],
    )

    ids = jnp.stack([seg_ids[0], seg_ids[-1]]).astype(F32)
    passing = jnp.concatenate(
        [final, jnp.broadcast_to(ids[:, None], (2, channels)), jnp.zeros((SUB - 2, channels), F32)]
    )
    near = passed_along(passing, "ctx", 1)
    far = passed_along(passing, "ctx", 2)
    farther = passed_along(passing, "ctx", 3)

    filtered = local_call(
        conv_kernel,
        pltpu.VMEM((channels // LANES, length, LANES), F32),
        (bounds,),
        (signal, ends, near, far, farther, decay, one_coef, two_coef, four_coef, onward, scale_b, taps_b, span),
        [pltpu.VMEM((modes, SUB, channels), F32)],
    )
    pieces = 4
    return local_call(
        mix_kernel,
        jax.ShapeDtypeStruct((length, channels), BF16),
        (starts, first, last),
        (query_in, filtered),
        [
            pltpu.VMEM((BLOCK, channels), F32),
            pltpu.VMEM((length, channels), BF16),
            pltpu.SemaphoreType.DMA((pieces,)),
        ],
        pl.ANY,
    )


def solution(mesh):
    return jax.shard_map(
        shards,
        mesh=mesh,
        in_specs=(
            P(("ctx", "ch"), None, None),
            P("ctx", None),
            P("ctx"),
            P("ch", None),
            P("ch", None),
            P("ch"),
        ),
        out_specs=P("ctx", "ch"),
        check_vma=False,
    )
```

time: 97.1 us -> 81.6 us (0.84)
  Pallas kernels: 36.8 us -> 28.9 us
  local copies, waits for them, and re-layouts: 6.1 us -> 0.88 us
  other arithmetic: 8.37 us -> 3.29 us
  waiting for transfers between devices: 22.1 us -> 24.7 us
    pallas_call x2, Pallas kernels: 14.5 us -> 9.15 us  [send(): pl.pallas_call(kernel, out_shape=jax.ShapeDtypeStruct((groups, rows, chan...]
    unnamed x22 -> x10, local copies, waits for them, and re-layouts: 2.69 us -> 0.02 us
    pallas_call x3, Pallas kernels: 22.3 us -> 19.7 us  [local_call(): pl.pallas_call(kernel, out_shape=outs, in_specs=[pl.BlockSpec(memory_spac...]
    all_to_all x1, waiting for transfers between devices: 20.7 us -> 23 us  [shards(): lax.all_to_all(signal_out, 'ch', split_axis=0, concat_axis=0, tiled=True)]
    mul x2, local copies, waits for them, and re-layouts: 1.32 us -> 0.02 us  [power(): return jnp.exp(-exponent * rate[:, None, :])]
  transfers between devices with their start and end apart: 5 -> 5, of which waited for: 3 -> 4; matrix products, arithmetic and copies ran while one was open for 11% -> 5% of each run, Pallas kernels for 23% -> 26%
where the time goes in v2:
time: 81.6 us; the launch traced here: 80.7 us
  Pallas kernels  28.9 us (35%)
  waiting for transfers between devices  24.7 us (30%)
  starting transfers between devices  22.7 us (28%)
  other arithmetic  3.29 us (4%)
  local copies, waits for them, and re-layouts  0.88 us (1%)
    all_to_all x1, waiting for transfers between devices, shards(): lax.all_to_all(signal_out, 'ch', split_axis=0, concat_axis=0, tiled=True)  23 us
    pallas_call x3, Pallas kernels, local_call(): pl.pallas_call(kernel, out_shape=outs, in_specs=[pl.BlockSpec(memory_spac...  19.7 us
    ppermute x3, starting transfers between devices, passed_along(): lax.ppermute(value, axis, [(source, source + steps) for source in range(c...  9.55 us
    pallas_call x2, Pallas kernels, send(): pl.pallas_call(kernel, out_shape=jax.ShapeDtypeStruct((groups, rows, chan...  9.15 us
    all_to_all x1, starting transfers between devices, shards(): lax.all_to_all(signal_out, 'ch', split_axis=0, concat_axis=0, tiled=True)  8.38 us
    all_to_all x1, starting transfers between devices, shards(): lax.all_to_all(query_out, 'ch', split_axis=0, concat_axis=0, tiled=True)  4.77 us
  transfers between devices with their start and end apart: 5, of which 4 were waited for; matrix products, arithmetic and copies ran while one was open for 5% of the time, Pallas kernels for 26%

profile of v2, /device:TPU:0, one launch (start us, length us, event | category | flops | bytes accessed | tf_op | source)
XLA Modules:
  0.0 80.7 jit_solution(2751873223823281801)
XLA Ops:
  0.0 4.2 %shard_map.65 = bf16[32,128,256]{2,1,0:T(8,128)(2,1)} custom-call(bf16[3,128,8192]{2,1,0:T(8,128)(2,1)} %bitcast.16, bf16[3,128,8192]{2,1,0:T(8,128)(2,1)} %bitcast.17), custom_call_target="tpu_custom_call" | custom-call | tf_op jit(solution)/shard_map/pallas_call | solution.py:42
  4.2 8.4 %all-to-all-start.1 = ((bf16[32,128,256]{2,1,0:T(8,128)(2,1)}), bf16[32,128,256]{2,1,0:T(8,128)(2,1)S(1)}, u32[]{:S(2)}, u32[]{:S(2)}) async-start(bf16[32,128,256]{2,1,0:T(8,128)(2,1)} %shard_map.65), calls=%async_computation.1 | async-start | bytes 4194304 | tf_op jit(solution)/shard_map/all_to_all | solution.py:287
  12.7 0.6 fusion
  13.3 5.0 %shard_map.64 = bf16[32,128,256]{2,1,0:T(8,128)(2,1)} custom-call(s32[1]{0:T(128)} %bitcast.1.shift, bf16[3,128,8192]{2,1,0:T(8,128)(2,1)} %bitcast.18), custom_call_target="tpu_custom_call" | custom-call | tf_op jit(solution)/shard_map/pallas_call | solution.py:42
  18.3 0.1 select_reduce_fusion
  18.4 0.1 pad_add_fusion.starts
  18.5 0.0 copy-done.2
  18.5 0.2 convert_reduce_fusion.bounds
  18.7 0.2 convert_reduce_fusion.1
  18.9 0.0 copy-done
  18.9 0.1 multiply_reduce_fusion
  19.1 0.1 select_add_fusion
  19.2 0.1 broadcast_select_fusion.2.one_ref
  19.2 0.1 multiply_exponential_fusion
  19.4 0.1 broadcast_select_fusion
  19.5 23.0 %all-to-all-done.1.arrived_ref = bf16[32,128,256]{2,1,0:T(8,128)(2,1)S(1)} async-done(((bf16[32,128,256]{2,1,0:T(8,128)(2,1)}), bf16[32,128,256]{2,1,0:T(8,128)(2,1)S(1)}, u32[]{:S(2)}, u32[]{:S(2)}) %all-to-all-start.1) | async-done | bytes 2097184 | tf_op jit(solution)/shard_map/all_to_all | solution.py:287
  42.6 4.8 %all-to-all-start = ((bf16[32,128,256]{2,1,0:T(8,128)(2,1)}), bf16[32,128,256]{2,1,0:T(8,128)(2,1)}, u32[]{:S(2)}, u32[]{:S(2)}) async-start(bf16[32,128,256]{2,1,0:T(8,128)(2,1)} %shard_map.64), calls=%async_computation | async-start | bytes 4194304 | tf_op jit(solution)/shard_map/all_to_all | solution.py:325
  47.3 0.7 fusion.1
  48.0 1.4 %add_convert_fusion = f32[2]{0:T(128)S(1)} fusion(s32[1]{0:T(128)} %get-tuple-element.51, s32[1]{0:T(128)} %get-tuple-element.50), kind=kLoop, calls=%fused_computation.23 | loop fusion | flops 4 | bytes 16 | tf_op jit(solution)/shard_map/convert_element_type | solution.py:339
  49.4 0.1 pad.1.clone
  49.5 0.1 pad.2.clone
  49.6 10.6 %shard_map.66 = (f32[2048,256]{1,0:T(8,128)S(1)}, f32[16,16,8,256]{3,2,1,0:T(8,128)S(1)}, f32[16,256]{1,0:T(8,128)S(1)}) custom-call(s32[33]{0:T(128)S(1)} %pad_add_fusion.starts, s32[16]{0:T(128)S(1)} %get-tuple-element.24.first, s32[16]{0:T(128)S(1)} %get-tuple-element.25.last, s32[3]{0:T(128)S(1)} %convert_reduce_fusion.bounds, ...), custom_call_target="tpu_custom_call" | custom-call | tf_op jit(solution)/shard_map/pallas_call | solution.py:263
  60.2 0.1 maximum_maximum_fusion
  60.2 3.5 %collective-permute-start = (f32[24,256]{1,0:T(8,128)S(1)}, f32[24,256]{1,0:T(8,128)S(1)}, u32[]{:S(2)}, u32[]{:S(2)}) collective-permute-start(f32[24,256]{1,0:T(8,128)S(1)} %maximum_maximum_fusion), channel_id=1, source_target_pairs={{0,32},{32,64},{64,96},{1,33},{33,65},{65,97},{2,34},{34,66},{66,9... | collective-permute-start | bytes 73736 | tf_op jit(solution)/shard_map/ppermute | solution.py:275
  63.7 4.8 %collective-permute-start.1 = (f32[24,256]{1,0:T(8,128)S(1)}, f32[24,256]{1,0:T(8,128)S(1)}, u32[]{:S(2)}, u32[]{:S(2)}) collective-permute-start(f32[24,256]{1,0:T(8,128)S(1)} %maximum_maximum_fusion), channel_id=1, source_target_pairs={{0,64},{32,96},{1,65},{33,97},{2,66},{34,98},{3,67},{35,99},{4,68}... | collective-permute-start | bytes 73736 | tf_op jit(solution)/shard_map/ppermute | solution.py:275
  68.5 1.3 %collective-permute-start.2 = (f32[24,256]{1,0:T(8,128)S(1)}, f32[24,256]{1,0:T(8,128)S(1)}, u32[]{:S(2)}, u32[]{:S(2)}) collective-permute-start(f32[24,256]{1,0:T(8,128)S(1)} %maximum_maximum_fusion), channel_id=1, source_target_pairs={{0,96},{1,97},{2,98},{3,99},{4,100},{5,101},{6,102},{7,103},{8,104... | collective-permute-start | bytes 73736 | tf_op jit(solution)/shard_map/ppermute | solution.py:275
  69.8 0.0 collective-permute-done.near_ref
  69.8 0.2 collective-permute-done.1.far_ref
  70.0 1.3 %collective-permute-done.2.farther_ref = f32[24,256]{1,0:T(8,128)S(1)} collective-permute-done((f32[24,256]{1,0:T(8,128)S(1)}, f32[24,256]{1,0:T(8,128)S(1)}, u32[]{:S(2)}, u32[]{:S(2)}) %collective-permute-start.2) | collective-permute-done | bytes 24608 | tf_op jit(solution)/shard_map/ppermute | solution.py:275
  71.3 5.8 %shard_map.67.filtered_ref = f32[2,2048,128]{2,1,0:T(8,128)S(1)} custom-call(s32[3]{0:T(128)S(1)} %convert_reduce_fusion.bounds, f32[2048,256]{1,0:T(8,128)S(1)} %get-tuple-element.31.signal_ref, f32[16,16,8,256]{3,2,1,0:T(8,128)S(1)} %get-tuple-element.32.ends_ref, f32[24,256]{1,0:T(8,128)S(1)} %collective-permute-done.near_ref, ...), custom_call_target="tpu_custom_call" | custom-call | tf_op jit(solution)/shard_map/pallas_call | solution.py:263
  77.1 0.2 all-to-all-done.arrived_ref
  77.3 3.4 %shard_map.68 = bf16[2048,256]{1,0:T(8,128)(2,1)} custom-call(s32[33]{0:T(128)S(1)} %pad_add_fusion.starts, s32[16]{0:T(128)S(1)} %get-tuple-element.24.first, s32[16]{0:T(128)S(1)} %get-tuple-element.25.last, bf16[32,128,256]{2,1,0:T(8,128)(2,1)} %all-to-all-done.arrived_ref, f32[2,2048,128]{2,1,0:T(8,128)S(1)} %shard_map.67.filtered_ref), custom_call_target="tpu_custom_call" | custom-call | tf_op jit(solution)/shard_map/pallas_call | solution.py:263
  (23 shorter events, 0.2 us)
Async XLA Ops:
  4.2 8.5 %copy-start.4 = (s32[1,32]{1,0:T(1,128)S(1)}, s32[1,32]{1,0:T(1,128)}, u32[]{:S(2)}) copy-start(s32[1,32]{1,0:T(1,128)} %param.7) | copy-start | bytes 388
  4.2 38.4 %all-to-all-start.1 = ((bf16[32,128,256]{2,1,0:T(8,128)(2,1)}), bf16[32,128,256]{2,1,0:T(8,128)(2,1)S(1)}, u32[]{:S(2)}, u32[]{:S(2)}) async-start(bf16[32,128,256]{2,1,0:T(8,128)(2,1)} %shard_map.65), calls=%async_computation.1 | async-start | bytes 4194304 | tf_op jit(solution)/shard_map/all_to_all | solution.py:287
  13.3 5.2 %copy-start.2 = (s32[2048]{0:T(1024)S(1)}, s32[2048]{0:T(1024)}, u32[]{:S(2)}) copy-start(s32[2048]{0:T(1024)} %param.8) | copy-start | bytes 24580
  13.3 5.6 %copy-start = (f32[256,16]{0,1:T(8,128)S(1)}, f32[256,16]{0,1:T(8,128)}, u32[]{:S(2)}) copy-start(f32[256,16]{0,1:T(8,128)} %param.9) | copy-start | bytes 49156
  13.3 5.6 %copy-start.1 = (f32[256,16]{0,1:T(8,128)S(1)}, f32[256,16]{0,1:T(8,128)}, u32[]{:S(2)}) copy-start(f32[256,16]{0,1:T(8,128)} %param.10) | copy-start | bytes 49156
  13.3 5.8 %copy-start.3 = (f32[256]{0:T(256)S(1)}, f32[256]{0:T(256)}, u32[]{:S(2)}) copy-start(f32[256]{0:T(256)} %param.11) | copy-start | bytes 3076
  42.6 34.7 %all-to-all-start = ((bf16[32,128,256]{2,1,0:T(8,128)(2,1)}), bf16[32,128,256]{2,1,0:T(8,128)(2,1)}, u32[]{:S(2)}, u32[]{:S(2)}) async-start(bf16[32,128,256]{2,1,0:T(8,128)(2,1)} %shard_map.64), calls=%async_computation | async-start | bytes 4194304 | tf_op jit(solution)/shard_map/all_to_all | solution.py:325
  60.2 9.6 %collective-permute-start = (f32[24,256]{1,0:T(8,128)S(1)}, f32[24,256]{1,0:T(8,128)S(1)}, u32[]{:S(2)}, u32[]{:S(2)}) collective-permute-start(f32[24,256]{1,0:T(8,128)S(1)} %maximum_maximum_fusion), channel_id=1, source_target_pairs={{0,32},{32,64},{64,96},{1,33},{33,65},{65,97},{2,34},{34,66},{66,9... | collective-permute-start | bytes 73736 | tf_op jit(solution)/shard_map/ppermute | solution.py:275
  63.7 6.3 %collective-permute-start.1 = (f32[24,256]{1,0:T(8,128)S(1)}, f32[24,256]{1,0:T(8,128)S(1)}, u32[]{:S(2)}, u32[]{:S(2)}) collective-permute-start(f32[24,256]{1,0:T(8,128)S(1)} %maximum_maximum_fusion), channel_id=1, source_target_pairs={{0,64},{32,96},{1,65},{33,97},{2,66},{34,98},{3,67},{35,99},{4,68}... | collective-permute-start | bytes 73736 | tf_op jit(solution)/shard_map/ppermute | solution.py:275
  68.5 2.8 %collective-permute-start.2 = (f32[24,256]{1,0:T(8,128)S(1)}, f32[24,256]{1,0:T(8,128)S(1)}, u32[]{:S(2)}, u32[]{:S(2)}) collective-permute-start(f32[24,256]{1,0:T(8,128)S(1)} %maximum_maximum_fusion), channel_id=1, source_target_pairs={{0,96},{1,97},{2,98},{3,99},{4,100},{5,101},{6,102},{7,103},{8,104... | collective-permute-start | bytes 73736 | tf_op jit(solution)/shard_map/ppermute | solution.py:275

commit v3 on v2

--- a/solution.py
+++ b/solution.py
@@ -15,11 +15,6 @@
 BF16 = jnp.bfloat16
 
 
-def slot_position(shape, dim):
-    slot = lax.broadcasted_iota(jnp.int32, shape, dim)
-    return (slot & (SUB - 1)) * STEPS + (slot >> 3)
-
-
 def send_signal_kernel(key_ref, value_ref, out_ref):
     signal = key_ref[0] * value_ref[0]
     channels = out_ref.shape[2]
@@ -27,31 +22,39 @@
         out_ref[part] = signal[:, part * channels : (part + 1) * channels]
 
 
-def send_query_kernel(shift, query_ref, out_ref):
-    place = lax.broadcasted_iota(jnp.int32, (BLOCK, BLOCK), 0)
-    row = lax.broadcasted_iota(jnp.int32, (BLOCK, BLOCK), 1)
-    turn = jnp.where(((row + shift[0]) & (BLOCK - 1)) == place, 1.0, 0.0).astype(BF16)
-    moved = jnp.dot(turn, query_ref[0], preferred_element_type=F32).astype(BF16)
+def send_query_kernel(query_ref, out_ref):
     channels = out_ref.shape[2]
     for part in range(out_ref.shape[0]):
-        out_ref[part] = moved[:, part * channels : (part + 1) * channels]
-
-
-def send(kernel, planes, streams, scalars, groups, channels, step):
+        out_ref[part] = query_ref[0, :, part * channels : (part + 1) * channels]
+
+
+def send(kernel, planes, streams, groups, channels, step):
     rows = streams.shape[1]
     return pl.pallas_call(
         kernel,
         out_shape=jax.ShapeDtypeStruct((groups, rows, channels), BF16),
-        grid_spec=pltpu.PrefetchScalarGridSpec(
-            num_scalar_prefetch=len(scalars),
-            grid=(groups // step,),
-            in_specs=[
-                pl.BlockSpec((1, rows, step * channels), functools.partial(lambda plane, i, *_: (plane, 0, i), plane))
-                for plane in planes
-            ],
-            out_specs=pl.BlockSpec((step, rows, channels), lambda i, *_: (i, 0, 0)),
-        ),
-    )(*scalars, *[streams for _ in planes])
+        grid=(groups // step,),
+        in_specs=[
+            pl.BlockSpec((1, rows, step * channels), functools.partial(lambda plane, i: (plane, 0, i), plane))
+            for plane in planes
+        ],
+        out_specs=pl.BlockSpec((step, rows, channels), lambda i: (i, 0, 0)),
+    )(*[streams for _ in planes])
+
+
+def compact(starts, arrived_ref, into_ref):
+    sources, rows, channels = arrived_ref.shape
+
+    def place(source, unused):
+        begin = starts[source]
+        for part in range(0, rows, 2 * SUB):
+            for tile in range(channels // LANES):
+                piece = arrived_ref[source, pl.ds(part, 2 * SUB), pl.ds(tile * LANES, LANES)].astype(F32)
+                into_ref[tile, pl.ds(begin + part, SUB), :] = piece[:SUB]
+                into_ref[tile, pl.ds(begin + part + SUB, SUB), :] = piece[SUB:]
+        return unused
+
+    lax.fori_loop(0, sources, place, 0)
 
 
 def segment(position, bounds):
@@ -61,33 +64,15 @@
     return total
 
 
-def scan_kernel(starts, first, last, bounds, arrived_ref, decay_ref, weight_ref, leap_ref, signal_ref, ends_ref, final_ref, carry, gap):
+def scan_kernel(starts, bounds, arrived_ref, decay_ref, weight_ref, leap_ref, signal_ref, ends_ref, passing_ref, carry):
     limits = [bounds[k] for k in range(3)]
     blocks, modes, _, channels = ends_ref.shape
     carry[...] = jnp.zeros_like(carry)
-    row = lax.broadcasted_iota(jnp.int32, (BLOCK, BLOCK), 1)
-    gap[...] = slot_position((BLOCK, BLOCK), 0) - row
     rank = lax.broadcasted_iota(jnp.int32, (SUB, LANES), 0)
+    compact(starts, arrived_ref, signal_ref)
 
     def one(block, unused):
         begin = block * BLOCK
-
-        def picked(source):
-            low = starts[source] - begin
-            held = starts[source + 1] - starts[source]
-            here = (gap[...] == low) & (row < held)
-            return jnp.dot(
-                jnp.where(here, 1.0, 0.0).astype(BF16), arrived_ref[source], preferred_element_type=F32
-            )
-
-        rows_here = pl.ds(pl.multiple_of(begin, BLOCK), BLOCK)
-        signal_ref[rows_here, :] = picked(first[block])
-
-        def add(source, carried):
-            signal_ref[rows_here, :] += picked(source)
-            return carried
-
-        lax.fori_loop(first[block] + 1, last[block], add, 0)
         first_id = segment(begin, limits)
         last_id = segment(begin + BLOCK - 1, limits)
         before_id = segment(begin - 1, limits)
@@ -99,9 +84,7 @@
                 own = [segment(begin + rank * STEPS + t, limits) for t in range(STEPS)]
             for tile in range(channels // LANES):
                 lanes = pl.ds(tile * LANES, LANES)
-                rows = [
-                    signal_ref[pl.ds(pl.multiple_of(begin + t * SUB, SUB), SUB), lanes] for t in range(STEPS)
-                ]
+                rows = [signal_ref[tile, pl.ds(begin + t, SUB, stride=STEPS), :] for t in range(STEPS)]
                 if masked:
                     rows = [jnp.where(o == own[-1], r, 0.0) for o, r in zip(own, rows)]
                 for mode in range(modes):
@@ -126,7 +109,10 @@
         return unused
 
     lax.fori_loop(0, blocks, one, 0)
-    final_ref[...] = jnp.sum(carry[...], axis=1)
+    passing_ref[0:modes, :] = jnp.sum(carry[...], axis=1)
+    line = lax.broadcasted_iota(jnp.int32, (SUB, channels), 0)
+    ids = jnp.where(line == 0, segment(0, limits), segment(blocks * BLOCK - 1, limits))
+    passing_ref[modes : modes + SUB, :] = ids.astype(F32)
 
 
 def conv_kernel(
@@ -172,9 +158,7 @@
                 open_in = [jnp.where(o == prior, 1.0, 0.0) for o in own]
             for tile in range(channels // LANES):
                 lanes = pl.ds(tile * LANES, LANES)
-                rows = [
-                    signal_ref[pl.ds(pl.multiple_of(begin + t * SUB, SUB), SUB), lanes] for t in range(STEPS)
-                ]
+                rows = [signal_ref[tile, pl.ds(begin + t, SUB, stride=STEPS), :] for t in range(STEPS)]
                 local = []
                 for t in range(STEPS):
                     total = taps_ref[0, :, lanes] * rows[t]
@@ -219,29 +203,16 @@
     lax.fori_loop(0, blocks, one, 0)
 
 
-def mix_kernel(starts, first, last, arrived_ref, filtered_ref, out_ref, held, ready, sems):
+def mix_kernel(starts, arrived_ref, filtered_ref, out_ref, held, ready, sems):
     pieces = sems.shape[0]
-    blocks = filtered_ref.shape[1] // BLOCK
-    per = blocks // pieces
-    place = lax.broadcasted_iota(jnp.int32, (BLOCK, LANES), 0)
-    tiles = held.shape[1] // LANES
+    tiles, length, _ = filtered_ref.shape
+    per = length // BLOCK // pieces
+    compact(starts, arrived_ref, held)
 
     def one(block, unused):
-        begin = pl.multiple_of(block * BLOCK, BLOCK)
-
-        def add(source, carried):
-            low = starts[source] - begin
-            here = place >= low
-            for tile in range(tiles):
-                lanes = pl.ds(tile * LANES, LANES)
-                held[:, lanes] = jnp.where(here, arrived_ref[source, :, lanes].astype(F32), held[:, lanes])
-            return carried
-
-        lax.fori_loop(first[block], last[block], add, 0)
-        rows = pl.ds(begin, BLOCK)
+        rows = pl.ds(pl.multiple_of(block * BLOCK, BLOCK), BLOCK)
         for tile in range(tiles):
-            lanes = pl.ds(tile * LANES, LANES)
-            ready[rows, lanes] = (held[:, lanes] * filtered_ref[tile, rows, :]).astype(BF16)
+            ready[rows, pl.ds(tile * LANES, LANES)] = (held[tile, rows, :] * filtered_ref[tile, rows, :]).astype(BF16)
         return unused
 
     def copy(piece):
@@ -283,17 +254,12 @@
     blocks = length // BLOCK
     counts = load_counts[0]
     planes = jnp.transpose(streams, (1, 0, 2))
-    signal_out = send(send_signal_kernel, (1, 2), planes, (), groups, channels, 8)
+    signal_out = send(send_signal_kernel, (1, 2), planes, groups, channels, 8)
     signal_in = lax.all_to_all(signal_out, "ch", split_axis=0, concat_axis=0, tiled=True)
-    mine = lax.axis_index("ch")
-    shift = jnp.sum(jnp.where(jnp.arange(groups) < mine, counts, 0)).astype(jnp.int32)[None]
-    query_out = send(send_query_kernel, (0,), planes, (shift,), groups, channels, 8)
+    query_out = send(send_query_kernel, (0,), planes, groups, channels, 8)
 
     ending = jnp.sum(jnp.where(jnp.arange(groups)[:, None] >= jnp.arange(groups)[None, :], counts[None, :], 0), axis=1)
     starts = jnp.concatenate([jnp.zeros((1,), jnp.int32), ending]).astype(jnp.int32)
-    edges = jnp.arange(blocks, dtype=jnp.int32) * BLOCK
-    first = jnp.sum((ending[None, :] <= edges[:, None]).astype(jnp.int32), axis=1)
-    last = jnp.sum((starts[None, :-1] < edges[:, None] + BLOCK).astype(jnp.int32), axis=1)
     bounds = jnp.sum((seg_ids[None, :] < jnp.arange(1, 4, dtype=jnp.int32)[:, None]).astype(jnp.int32), axis=1)
 
     rate = jnp.transpose(rates)
@@ -319,26 +285,22 @@
     taps_b = jnp.broadcast_to(taps[:, None, :], (STEPS, SUB, channels))
     span = jnp.exp(-float(length) * rate)
 
-    prepared = (starts, first, last, bounds, decay, weight, leap, one_coef, two_coef, four_coef, onward, scale_b, taps_b, span)
+    prepared = (starts, bounds, decay, weight, leap, one_coef, two_coef, four_coef, onward, scale_b, taps_b, span)
     query_out, prepared = lax.optimization_barrier((query_out, prepared))
-    starts, first, last, bounds, decay, weight, leap, one_coef, two_coef, four_coef, onward, scale_b, taps_b, span = prepared
+    starts, bounds, decay, weight, leap, one_coef, two_coef, four_coef, onward, scale_b, taps_b, span = prepared
     query_in = lax.all_to_all(query_out, "ch", split_axis=0, concat_axis=0, tiled=True)
 
-    signal, ends, final = local_call(
+    padded = (channels // LANES, length + capacity, LANES)
+    signal, ends, passing = local_call(
         scan_kernel,
         (
-            pltpu.VMEM((length, channels), F32),
+            pltpu.VMEM(padded, F32),
             pltpu.VMEM((blocks, modes, SUB, channels), F32),
-            pltpu.VMEM((modes, channels), F32),
+            pltpu.VMEM((modes + SUB, channels), F32),
         ),
-        (starts, first, last, bounds),
+        (starts, bounds),
         (signal_in, decay, weight, leap),
-        [pltpu.VMEM((modes, SUB, channels), F32), pltpu.VMEM((BLOCK, BLOCK), jnp.int32)],
-    )
-
-    ids = jnp.stack([seg_ids[0], seg_ids[-1]]).astype(F32)
-    passing = jnp.concatenate(
-        [final, jnp.broadcast_to(ids[:, None], (2, channels)), jnp.zeros((SUB - 2, channels), F32)]
+        [pltpu.VMEM((modes, SUB, channels), F32)],
     )
     near = passed_along(passing, "ctx", 1)
     far = passed_along(passing, "ctx", 2)
@@ -355,10 +317,10 @@
     return local_call(
         mix_kernel,
         jax.ShapeDtypeStruct((length, channels), BF16),
-        (starts, first, last),
+        (starts,),
         (query_in, filtered),
         [
-            pltpu.VMEM((BLOCK, channels), F32),
+            pltpu.VMEM(padded, F32),
             pltpu.VMEM((length, channels), BF16),
             pltpu.SemaphoreType.DMA((pieces,)),
         ],

time: 81.6 us -> 80.7 us (0.989)
  waiting for transfers between devices: 24.7 us -> 36 us
  Pallas kernels: 28.9 us -> 20.9 us
  other arithmetic: 3.29 us -> 0.98 us
    all_to_all x1, waiting for transfers between devices: 0.22 us -> 9.55 us  [shards(): lax.all_to_all(query_out, 'ch', split_axis=0, concat_axis=0, tiled=True)]
    pallas_call x3, Pallas kernels: 19.7 us -> 12.9 us  [local_call(): pl.pallas_call(kernel, out_shape=outs, in_specs=[pl.BlockSpec(memory_spac...]
    all_to_all x1, waiting for transfers between devices: 23 us -> 25 us  [shards(): lax.all_to_all(signal_out, 'ch', split_axis=0, concat_axis=0, tiled=True)]
    convert_element_type x1 -> x0, other arithmetic: 1.41 us -> none  [shards(): ids = jnp.stack([seg_ids[0], seg_ids[-1]]).astype(F32)]
    pallas_call x2, Pallas kernels: 9.15 us -> 8 us  [send(): pl.pallas_call(kernel, out_shape=jax.ShapeDtypeStruct((groups, rows, chan...]
  transfers between devices with their start and end apart: 5 -> 5, of which waited for: 4 -> 3; matrix products, arithmetic and copies ran while one was open for 5% -> 1% of each run, Pallas kernels for 26% -> 17%
where the time goes in v3:
time: 80.7 us; the launch traced here: 80.2 us
  waiting for transfers between devices  36 us (45%)
  starting transfers between devices  22 us (27%)
  Pallas kernels  20.9 us (26%)
  other arithmetic  0.98 us (1%)
    all_to_all x1, waiting for transfers between devices, shards(): lax.all_to_all(signal_out, 'ch', split_axis=0, concat_axis=0, tiled=True)  25 us
    pallas_call x3, Pallas kernels, local_call(): pl.pallas_call(kernel, out_shape=outs, in_specs=[pl.BlockSpec(memory_spac...  12.9 us
    all_to_all x1, waiting for transfers between devices, shards(): lax.all_to_all(query_out, 'ch', split_axis=0, concat_axis=0, tiled=True)  9.55 us
    ppermute x3, starting transfers between devices, passed_along(): lax.ppermute(value, axis, [(source, source + steps) for source in range(c...  9.02 us
    all_to_all x1, starting transfers between devices, shards(): lax.all_to_all(signal_out, 'ch', split_axis=0, concat_axis=0, tiled=True)  8.25 us
    pallas_call x2, Pallas kernels, send(): pl.pallas_call(kernel, out_shape=jax.ShapeDtypeStruct((groups, rows, chan...  8 us
    all_to_all x1, starting transfers between devices, shards(): lax.all_to_all(query_out, 'ch', split_axis=0, concat_axis=0, tiled=True)  4.77 us
  transfers between devices with their start and end apart: 5, of which 3 were waited for; matrix products, arithmetic and copies ran while one was open for 1% of the time, Pallas kernels for 17%

profile of v3, /device:TPU:0, one launch (start us, length us, event | category | flops | bytes accessed | tf_op | source)
XLA Modules:
  0.0 80.2 jit_solution(4080755823112989085)
XLA Ops:
  0.0 4.2 %shard_map.65 = bf16[32,128,256]{2,1,0:T(8,128)(2,1)} custom-call(bf16[3,128,8192]{2,1,0:T(8,128)(2,1)} %bitcast.12, bf16[3,128,8192]{2,1,0:T(8,128)(2,1)} %bitcast.13), custom_call_target="tpu_custom_call" | custom-call | tf_op jit(solution)/shard_map/pallas_call | solution.py:33
  4.2 8.2 %all-to-all-start.1 = ((bf16[32,128,256]{2,1,0:T(8,128)(2,1)}), bf16[32,128,256]{2,1,0:T(8,128)(2,1)S(1)}, u32[]{:S(2)}, u32[]{:S(2)}) async-start(bf16[32,128,256]{2,1,0:T(8,128)(2,1)} %shard_map.65), calls=%async_computation.1 | async-start | bytes 4194304 | tf_op jit(solution)/shard_map/all_to_all | solution.py:258
  12.5 0.0 copy-start.4
  12.5 0.0 copy-start.2
  12.5 0.0 copy-start
  12.5 0.0 copy-start.1
  12.5 0.0 copy-start.3
  12.6 3.8 %shard_map.64 = bf16[32,128,256]{2,1,0:T(8,128)(2,1)} custom-call(bf16[3,128,8192]{2,1,0:T(8,128)(2,1)} %bitcast.14), custom_call_target="tpu_custom_call" | custom-call | tf_op jit(solution)/shard_map/pallas_call | solution.py:33
  16.4 0.0 copy-done.4
  16.4 0.1 select_reduce_fusion
  16.5 0.1 pad_add_fusion.starts
  16.6 0.0 copy-done.2
  16.6 0.2 convert_reduce_fusion.bounds
  16.8 0.0 copy-done
  16.8 0.0 copy-done.1
  16.9 0.1 multiply_reduce_fusion
  17.0 0.1 select_add_fusion
  17.1 0.1 broadcast_select_fusion.2.one_ref
  17.2 0.1 multiply_exponential_fusion
  17.3 0.1 broadcast_select_fusion
  17.5 25.0 %all-to-all-done.1.arrived_ref = bf16[32,128,256]{2,1,0:T(8,128)(2,1)S(1)} async-done(((bf16[32,128,256]{2,1,0:T(8,128)(2,1)}), bf16[32,128,256]{2,1,0:T(8,128)(2,1)S(1)}, u32[]{:S(2)}, u32[]{:S(2)}) %all-to-all-start.1) | async-done | bytes 2097184 | tf_op jit(solution)/shard_map/all_to_all | solution.py:258
  42.4 4.8 %all-to-all-start = ((bf16[32,128,256]{2,1,0:T(8,128)(2,1)}), bf16[32,128,256]{2,1,0:T(8,128)(2,1)}, u32[]{:S(2)}, u32[]{:S(2)}) async-start(bf16[32,128,256]{2,1,0:T(8,128)(2,1)} %shard_map.64), calls=%async_computation | async-start | bytes 4194304 | tf_op jit(solution)/shard_map/all_to_all | solution.py:291
  47.2 4.1 %shard_map.66 = (f32[2,2176,128]{2,1,0:T(8,128)S(1)}, f32[16,16,8,256]{3,2,1,0:T(8,128)S(1)}, f32[24,256]{1,0:T(8,128)S(1)}) custom-call(s32[33]{0:T(128)S(1)} %pad_add_fusion.starts, s32[3]{0:T(128)S(1)} %convert_reduce_fusion.bounds, bf16[32,128,256]{2,1,0:T(8,128)(2,1)S(1)} %all-to-all-done.1.arrived_ref, f32[16,8,256]{2,1,0:T(8,128)S(1)} %mul.138.decay_ref, ...), custom_call_target="tpu_custom_call" | custom-call | tf_op jit(solution)/shard_map/pallas_call | solution.py:234
  51.4 5.0 %collective-permute-start.2 = (f32[24,256]{1,0:T(8,128)S(1)}, f32[24,256]{1,0:T(8,128)S(1)}, u32[]{:S(2)}, u32[]{:S(2)}) collective-permute-start(f32[24,256]{1,0:T(8,128)S(1)} %get-tuple-element.29), channel_id=1, source_target_pairs={{0,96},{1,97},{2,98},{3,99},{4,100},{5,101},{6,102},{7,103},{8,104... | collective-permute-start | bytes 73736 | tf_op jit(solution)/shard_map/ppermute | solution.py:246
  56.3 1.3 %collective-permute-start.1 = (f32[24,256]{1,0:T(8,128)S(1)}, f32[24,256]{1,0:T(8,128)S(1)}, u32[]{:S(2)}, u32[]{:S(2)}) collective-permute-start(f32[24,256]{1,0:T(8,128)S(1)} %get-tuple-element.29), channel_id=1, source_target_pairs={{0,64},{32,96},{1,65},{33,97},{2,66},{34,98},{3,67},{35,99},{4,68}... | collective-permute-start | bytes 73736 | tf_op jit(solution)/shard_map/ppermute | solution.py:246
  57.6 2.8 %collective-permute-start = (f32[24,256]{1,0:T(8,128)S(1)}, f32[24,256]{1,0:T(8,128)S(1)}, u32[]{:S(2)}, u32[]{:S(2)}) collective-permute-start(f32[24,256]{1,0:T(8,128)S(1)} %get-tuple-element.29), channel_id=1, source_target_pairs={{0,32},{32,64},{64,96},{1,33},{33,65},{65,97},{2,34},{34,66},{66,9... | collective-permute-start | bytes 73736 | tf_op jit(solution)/shard_map/ppermute | solution.py:246
  60.4 0.0 collective-permute-done.2.farther_ref
  60.4 0.0 collective-permute-done.1.far_ref
  60.4 1.5 %collective-permute-done.near_ref = f32[24,256]{1,0:T(8,128)S(1)} collective-permute-done((f32[24,256]{1,0:T(8,128)S(1)}, f32[24,256]{1,0:T(8,128)S(1)}, u32[]{:S(2)}, u32[]{:S(2)}) %collective-permute-start) | collective-permute-done | bytes 24608 | tf_op jit(solution)/shard_map/ppermute | solution.py:246
  61.9 5.7 %shard_map.67.filtered_ref = f32[2,2048,128]{2,1,0:T(8,128)S(1)} custom-call(s32[3]{0:T(128)S(1)} %convert_reduce_fusion.bounds, f32[2,2176,128]{2,1,0:T(8,128)S(1)} %get-tuple-element.27.signal_ref, f32[16,16,8,256]{3,2,1,0:T(8,128)S(1)} %get-tuple-element.28.ends_ref, f32[24,256]{1,0:T(8,128)S(1)} %collective-permute-done.near_ref, ...), custom_call_target="tpu_custom_call" | custom-call | tf_op jit(solution)/shard_map/pallas_call | solution.py:234
  67.6 9.6 %all-to-all-done.arrived_ref = bf16[32,128,256]{2,1,0:T(8,128)(2,1)} async-done(((bf16[32,128,256]{2,1,0:T(8,128)(2,1)}), bf16[32,128,256]{2,1,0:T(8,128)(2,1)}, u32[]{:S(2)}, u32[]{:S(2)}) %all-to-all-start) | async-done | bytes 2097184 | tf_op jit(solution)/shard_map/all_to_all | solution.py:291
  77.2 3.1 %shard_map.68 = bf16[2048,256]{1,0:T(8,128)(2,1)} custom-call(s32[33]{0:T(128)S(1)} %pad_add_fusion.starts, bf16[32,128,256]{2,1,0:T(8,128)(2,1)} %all-to-all-done.arrived_ref, f32[2,2048,128]{2,1,0:T(8,128)S(1)} %shard_map.67.filtered_ref), custom_call_target="tpu_custom_call" | custom-call | tf_op jit(solution)/shard_map/pallas_call | solution.py:234
  (13 shorter events, 0.1 us)
Async XLA Ops:
  4.2 38.2 %all-to-all-start.1 = ((bf16[32,128,256]{2,1,0:T(8,128)(2,1)}), bf16[32,128,256]{2,1,0:T(8,128)(2,1)S(1)}, u32[]{:S(2)}, u32[]{:S(2)}) async-start(bf16[32,128,256]{2,1,0:T(8,128)(2,1)} %shard_map.65), calls=%async_computation.1 | async-start | bytes 4194304 | tf_op jit(solution)/shard_map/all_to_all | solution.py:258
  12.5 3.9 %copy-start.4 = (s32[1,32]{1,0:T(1,128)S(1)}, s32[1,32]{1,0:T(1,128)}, u32[]{:S(2)}) copy-start(s32[1,32]{1,0:T(1,128)} %param.7) | copy-start | bytes 388
  12.5 4.1 %copy-start.2 = (s32[2048]{0:T(1024)S(1)}, s32[2048]{0:T(1024)}, u32[]{:S(2)}) copy-start(s32[2048]{0:T(1024)} %param.8) | copy-start | bytes 24580
  12.5 4.3 %copy-start = (f32[256,16]{0,1:T(8,128)S(1)}, f32[256,16]{0,1:T(8,128)}, u32[]{:S(2)}) copy-start(f32[256,16]{0,1:T(8,128)} %param.9) | copy-start | bytes 49156
  12.5 4.3 %copy-start.1 = (f32[256,16]{0,1:T(8,128)S(1)}, f32[256,16]{0,1:T(8,128)}, u32[]{:S(2)}) copy-start(f32[256,16]{0,1:T(8,128)} %param.10) | copy-start | bytes 49156
  12.5 4.5 %copy-start.3 = (f32[256]{0:T(256)S(1)}, f32[256]{0:T(256)}, u32[]{:S(2)}) copy-start(f32[256]{0:T(256)} %param.11) | copy-start | bytes 3076
  42.4 34.7 %all-to-all-start = ((bf16[32,128,256]{2,1,0:T(8,128)(2,1)}), bf16[32,128,256]{2,1,0:T(8,128)(2,1)}, u32[]{:S(2)}, u32[]{:S(2)}) async-start(bf16[32,128,256]{2,1,0:T(8,128)(2,1)} %shard_map.64), calls=%async_computation | async-start | bytes 4194304 | tf_op jit(solution)/shard_map/all_to_all | solution.py:291
  51.4 9.0 %collective-permute-start.2 = (f32[24,256]{1,0:T(8,128)S(1)}, f32[24,256]{1,0:T(8,128)S(1)}, u32[]{:S(2)}, u32[]{:S(2)}) collective-permute-start(f32[24,256]{1,0:T(8,128)S(1)} %get-tuple-element.29), channel_id=1, source_target_pairs={{0,96},{1,97},{2,98},{3,99},{4,100},{5,101},{6,102},{7,103},{8,104... | collective-permute-start | bytes 73736 | tf_op jit(solution)/shard_map/ppermute | solution.py:246
  56.3 4.1 %collective-permute-start.1 = (f32[24,256]{1,0:T(8,128)S(1)}, f32[24,256]{1,0:T(8,128)S(1)}, u32[]{:S(2)}, u32[]{:S(2)}) collective-permute-start(f32[24,256]{1,0:T(8,128)S(1)} %get-tuple-element.29), channel_id=1, source_target_pairs={{0,64},{32,96},{1,65},{33,97},{2,66},{34,98},{3,67},{35,99},{4,68}... | collective-permute-start | bytes 73736 | tf_op jit(solution)/shard_map/ppermute | solution.py:246
  57.6 4.3 %collective-permute-start = (f32[24,256]{1,0:T(8,128)S(1)}, f32[24,256]{1,0:T(8,128)S(1)}, u32[]{:S(2)}, u32[]{:S(2)}) collective-permute-start(f32[24,256]{1,0:T(8,128)S(1)} %get-tuple-element.29), channel_id=1, source_target_pairs={{0,32},{32,64},{64,96},{1,33},{33,65},{65,97},{2,34},{34,66},{66,9... | collective-permute-start | bytes 73736 | tf_op jit(solution)/shard_map/ppermute | solution.py:246

commit v4 on v3

--- a/solution.py
+++ b/solution.py
@@ -11,45 +11,75 @@
 STEPS = 16
 LANES = 128
 SUB = 8
+TURN = 12
 F32 = jnp.float32
 BF16 = jnp.bfloat16
 
 
-def send_signal_kernel(key_ref, value_ref, out_ref):
-    signal = key_ref[0] * value_ref[0]
-    channels = out_ref.shape[2]
-    for part in range(out_ref.shape[0]):
-        out_ref[part] = signal[:, part * channels : (part + 1) * channels]
-
-
-def send_query_kernel(query_ref, out_ref):
-    channels = out_ref.shape[2]
-    for part in range(out_ref.shape[0]):
-        out_ref[part] = query_ref[0, :, part * channels : (part + 1) * channels]
-
-
-def send(kernel, planes, streams, groups, channels, step):
+def send_kernel(planes, turn, streams_ref, out_ref, *scratch):
+    held, ready, in_sems, out_sems = scratch[:-3], scratch[-3], scratch[-2], scratch[-1]
+    pieces = in_sems.shape[1]
+    groups, _, channels = out_ref.shape
+    per = groups // pieces
+    width = per * channels
+
+    def load(plane, piece):
+        columns = pl.ds(piece * width, width)
+        return pltpu.make_async_copy(
+            streams_ref.at[planes[plane], :, columns], held[plane].at[:, columns], in_sems.at[plane, piece]
+        )
+
+    def store(piece):
+        goes = (piece * per + turn) % groups
+        return pltpu.make_async_copy(ready.at[pl.ds(piece * per, per)], out_ref.at[pl.ds(goes, per)], out_sems.at[piece])
+
+    for piece in range(pieces):
+        for plane in range(len(planes)):
+            load(plane, piece).start()
+    for piece in range(pieces):
+        for plane in range(len(planes)):
+            load(plane, piece).wait()
+        for part in range(piece * per, (piece + 1) * per):
+            columns = pl.ds(part * channels, channels)
+            value = held[0][:, columns]
+            for other in held[1:]:
+                value = value * other[:, columns]
+            ready[part] = value
+        store(piece).start()
+    for piece in range(pieces):
+        store(piece).wait()
+
+
+def send(planes, streams, groups, channels, turn, pieces):
     rows = streams.shape[1]
     return pl.pallas_call(
-        kernel,
+        functools.partial(send_kernel, planes, turn),
         out_shape=jax.ShapeDtypeStruct((groups, rows, channels), BF16),
-        grid=(groups // step,),
-        in_specs=[
-            pl.BlockSpec((1, rows, step * channels), functools.partial(lambda plane, i: (plane, 0, i), plane))
-            for plane in planes
+        in_specs=[pl.BlockSpec(memory_space=pl.ANY)],
+        out_specs=pl.BlockSpec(memory_space=pl.ANY),
+        scratch_shapes=[pltpu.VMEM((rows, groups * channels), BF16) for _ in planes]
+        + [
+            pltpu.VMEM((groups, rows, channels), BF16),
+            pltpu.SemaphoreType.DMA((len(planes), pieces)),
+            pltpu.SemaphoreType.DMA((pieces,)),
         ],
-        out_specs=pl.BlockSpec((step, rows, channels), lambda i: (i, 0, 0)),
-    )(*[streams for _ in planes])
-
-
-def compact(starts, arrived_ref, into_ref):
+        compiler_params=pltpu.CompilerParams(vmem_limit_bytes=24 << 20),
+    )(streams)
+
+
+def exchange(value, order):
+    return lax.all_to_all(value, "ch", split_axis=0, concat_axis=0, axis_index_groups=[order], tiled=True)
+
+
+def compact(turn, starts, arrived_ref, into_ref):
     sources, rows, channels = arrived_ref.shape
 
     def place(source, unused):
         begin = starts[source]
+        slot = lax.rem(source + turn, sources)
         for part in range(0, rows, 2 * SUB):
             for tile in range(channels // LANES):
-                piece = arrived_ref[source, pl.ds(part, 2 * SUB), pl.ds(tile * LANES, LANES)].astype(F32)
+                piece = arrived_ref[slot, pl.ds(part, 2 * SUB), pl.ds(tile * LANES, LANES)].astype(F32)
                 into_ref[tile, pl.ds(begin + part, SUB), :] = piece[:SUB]
                 into_ref[tile, pl.ds(begin + part + SUB, SUB), :] = piece[SUB:]
         return unused
@@ -64,12 +94,12 @@
     return total
 
 
-def scan_kernel(starts, bounds, arrived_ref, decay_ref, weight_ref, leap_ref, signal_ref, ends_ref, passing_ref, carry):
+def scan_kernel(turn, starts, bounds, arrived_ref, decay_ref, weight_ref, leap_ref, signal_ref, ends_ref, passing_ref, carry):
     limits = [bounds[k] for k in range(3)]
     blocks, modes, _, channels = ends_ref.shape
     carry[...] = jnp.zeros_like(carry)
     rank = lax.broadcasted_iota(jnp.int32, (SUB, LANES), 0)
-    compact(starts, arrived_ref, signal_ref)
+    compact(turn, starts, arrived_ref, signal_ref)
 
     def one(block, unused):
         begin = block * BLOCK
@@ -203,11 +233,11 @@
     lax.fori_loop(0, blocks, one, 0)
 
 
-def mix_kernel(starts, arrived_ref, filtered_ref, out_ref, held, ready, sems):
+def mix_kernel(turn, starts, arrived_ref, filtered_ref, out_ref, held, ready, sems):
     pieces = sems.shape[0]
     tiles, length, _ = filtered_ref.shape
     per = length // BLOCK // pieces
-    compact(starts, arrived_ref, held)
+    compact(turn, starts, arrived_ref, held)
 
     def one(block, unused):
         rows = pl.ds(pl.multiple_of(block * BLOCK, BLOCK), BLOCK)
@@ -254,9 +284,9 @@
     blocks = length // BLOCK
     counts = load_counts[0]
     planes = jnp.transpose(streams, (1, 0, 2))
-    signal_out = send(send_signal_kernel, (1, 2), planes, groups, channels, 8)
-    signal_in = lax.all_to_all(signal_out, "ch", split_axis=0, concat_axis=0, tiled=True)
-    query_out = send(send_query_kernel, (0,), planes, groups, channels, 8)
+    order = [(rank - TURN) % groups for rank in range(groups)]
+    signal_in = exchange(send((1, 2), planes, groups, channels, TURN, 8), order)
+    query_out = send((0,), planes, groups, channels, TURN, 8)
 
     ending = jnp.sum(jnp.where(jnp.arange(groups)[:, None] >= jnp.arange(groups)[None, :], counts[None, :], 0), axis=1)
     starts = jnp.concatenate([jnp.zeros((1,), jnp.int32), ending]).astype(jnp.int32)
@@ -288,11 +318,11 @@
     prepared = (starts, bounds, decay, weight, leap, one_coef, two_coef, four_coef, onward, scale_b, taps_b, span)
     query_out, prepared = lax.optimization_barrier((query_out, prepared))
     starts, bounds, decay, weight, leap, one_coef, two_coef, four_coef, onward, scale_b, taps_b, span = prepared
-    query_in = lax.all_to_all(query_out, "ch", split_axis=0, concat_axis=0, tiled=True)
+    query_in = exchange(query_out, order)
 
     padded = (channels // LANES, length + capacity, LANES)
     signal, ends, passing = local_call(
-        scan_kernel,
+        functools.partial(scan_kernel, TURN),
         (
             pltpu.VMEM(padded, F32),
             pltpu.VMEM((blocks, modes, SUB, channels), F32),
@@ -315,7 +345,7 @@
     )
     pieces = 4
     return local_call(
-        mix_kernel,
+        functools.partial(mix_kernel, TURN),
         jax.ShapeDtypeStruct((length, channels), BF16),
         (starts,),
         (query_in, filtered),

time: 80.7 us -> 76.1 us (0.943); the launches traced: 80.2 us -> 74.7 us
  waiting for transfers between devices: 36 us -> 23 us
  local copies, waits for them, and re-layouts: 0.07 us -> 8.26 us
  Pallas kernels: 20.9 us -> 14.8 us
  starting transfers between devices: 22 us -> 27.4 us
    all_to_all x2, waiting for transfers between devices: 34.5 us -> 21.5 us  [exchange(): lax.all_to_all(value, 'ch', split_axis=0, concat_axis=0, axis_index_group...]
    unnamed x10 -> x18, local copies, waits for them, and re-layouts: 0.03 us -> 8.21 us
    pallas_call x2, Pallas kernels: 8 us -> 1.6 us  [send(): pl.pallas_call(functools.partial(send_kernel, planes, turn), out_shape=ja...]
    all_to_all x2, starting transfers between devices: 13 us -> 18.5 us  [exchange(): lax.all_to_all(value, 'ch', split_axis=0, concat_axis=0, axis_index_group...]
  transfers between devices with their start and end apart: 5 -> 5, of which waited for: 3 -> 3; matrix products, arithmetic and copies ran while one was open for 1% -> 1% of each run, Pallas kernels for 17% -> 14%
where the time goes in v4:
time: 76.1 us; the launch traced here: 74.7 us
  starting transfers between devices  27.4 us (36%)
  waiting for transfers between devices  23 us (30%)
  Pallas kernels  14.8 us (19%)
  local copies, waits for them, and re-layouts  8.26 us (11%)
  other arithmetic  0.98 us (1%)
    all_to_all x2, waiting for transfers between devices, exchange(): lax.all_to_all(value, 'ch', split_axis=0, concat_axis=0, axis_index_group...  21.5 us
    all_to_all x2, starting transfers between devices, exchange(): lax.all_to_all(value, 'ch', split_axis=0, concat_axis=0, axis_index_group...  18.5 us
    pallas_call x3, Pallas kernels, local_call(): pl.pallas_call(kernel, out_shape=outs, in_specs=[pl.BlockSpec(memory_spac...  13.2 us
    ppermute x3, starting transfers between devices, passed_along(): lax.ppermute(value, axis, [(source, source + steps) for source in range(c...  8.97 us
    unnamed x18, local copies, waits for them, and re-layouts  8.21 us
    pallas_call x2, Pallas kernels, send(): pl.pallas_call(functools.partial(send_kernel, planes, turn), out_shape=ja...  1.6 us
  transfers between devices with their start and end apart: 5, of which 3 were waited for; matrix products, arithmetic and copies ran while one was open for 1% of the time, Pallas kernels for 14%

profile of v4, /device:TPU:0, one launch (start us, length us, event | category | flops | bytes accessed | tf_op | source)
XLA Modules:
  0.0 74.7 jit_solution(15402054985991358866)
XLA Ops:
  0.0 2.8 %copy-done = bf16[128,3,8192]{2,0,1:T(8,128)(2,1)S(1)} copy-done((bf16[128,3,8192]{2,0,1:T(8,128)(2,1)S(1)}, bf16[128,3,8192]{2,0,1:T(8,128)(2,1)}, u32[]{:S(2)}) %copy-start) | copy-done | bytes 6291480
  2.8 1.0 %shard_map.65 = bf16[32,128,256]{2,1,0:T(8,128)(2,1)S(1)} custom-call(bf16[3,128,8192]{2,1,0:T(8,128)(2,1)S(1)} %bitcast.12), custom_call_target="tpu_custom_call" | custom-call | tf_op jit(solution)/shard_map/pallas_call | solution.py:55
  3.8 0.0 copy-start.3
  3.8 1.3 %copy-done.3 = bf16[32,128,256]{2,1,0:T(8,128)(2,1)} copy-done((bf16[32,128,256]{2,1,0:T(8,128)(2,1)}, bf16[32,128,256]{2,1,0:T(8,128)(2,1)S(1)}, u32[]{:S(2)}) %copy-start.3) | copy-done | bytes 2097176
  5.1 10.2 %all-to-all-start.1 = ((bf16[32,128,256]{2,1,0:T(8,128)(2,1)}), bf16[32,128,256]{2,1,0:T(8,128)(2,1)S(1)}, u32[]{:S(2)}, u32[]{:S(2)}) async-start(bf16[32,128,256]{2,1,0:T(8,128)(2,1)} %copy-done.3), calls=%async_computation.1 | async-start | bytes 4194304 | tf_op jit(solution)/shard_map/all_to_all | solution.py:71
  15.3 0.0 copy-start.1
  15.3 2.8 %copy-done.1 = bf16[128,3,8192]{2,0,1:T(8,128)(2,1)S(1)} copy-done((bf16[128,3,8192]{2,0,1:T(8,128)(2,1)S(1)}, bf16[128,3,8192]{2,0,1:T(8,128)(2,1)}, u32[]{:S(2)}) %copy-start.1) | copy-done | bytes 6291480
  18.1 0.0 copy-start.7
  18.1 0.6 shard_map.64
  18.7 0.0 copy-start.2
  18.7 1.3 %copy-done.2 = bf16[32,128,256]{2,1,0:T(8,128)(2,1)} copy-done((bf16[32,128,256]{2,1,0:T(8,128)(2,1)}, bf16[32,128,256]{2,1,0:T(8,128)(2,1)S(1)}, u32[]{:S(2)}) %copy-start.2) | copy-done | bytes 2097176
  20.1 0.1 select_reduce_fusion
  20.2 0.1 pad_add_fusion.starts
  20.3 0.2 convert_reduce_fusion.bounds
  20.5 0.0 copy-done.5
  20.6 0.1 multiply_reduce_fusion
  20.7 0.1 select_add_fusion
  20.8 0.1 broadcast_select_fusion.2.one_ref
  20.9 0.1 multiply_exponential_fusion
  21.0 0.1 broadcast_select_fusion
  21.2 17.9 %all-to-all-done.1.arrived_ref = bf16[32,128,256]{2,1,0:T(8,128)(2,1)S(1)} async-done(((bf16[32,128,256]{2,1,0:T(8,128)(2,1)}), bf16[32,128,256]{2,1,0:T(8,128)(2,1)S(1)}, u32[]{:S(2)}, u32[]{:S(2)}) %all-to-all-start.1) | async-done | bytes 2097184 | tf_op jit(solution)/shard_map/all_to_all | solution.py:71
  39.1 8.3 %all-to-all-start = ((bf16[32,128,256]{2,1,0:T(8,128)(2,1)}), bf16[32,128,256]{2,1,0:T(8,128)(2,1)}, u32[]{:S(2)}, u32[]{:S(2)}) async-start(bf16[32,128,256]{2,1,0:T(8,128)(2,1)} %copy-done.2), calls=%async_computation | async-start | bytes 4194304 | tf_op jit(solution)/shard_map/all_to_all | solution.py:71
  47.4 4.2 %shard_map.66 = (f32[2,2176,128]{2,1,0:T(8,128)S(1)}, f32[16,16,8,256]{3,2,1,0:T(8,128)S(1)}, f32[24,256]{1,0:T(8,128)S(1)}) custom-call(s32[33]{0:T(128)S(1)} %pad_add_fusion.starts, s32[3]{0:T(128)S(1)} %convert_reduce_fusion.bounds, bf16[32,128,256]{2,1,0:T(8,128)(2,1)S(1)} %all-to-all-done.1.arrived_ref, f32[16,8,256]{2,1,0:T(8,128)S(1)} %mul.138.decay_ref, ...), custom_call_target="tpu_custom_call" | custom-call | tf_op jit(solution)/shard_map/pallas_call | solution.py:264
  51.6 4.9 %collective-permute-start.2 = (f32[24,256]{1,0:T(8,128)S(1)}, f32[24,256]{1,0:T(8,128)S(1)}, u32[]{:S(2)}, u32[]{:S(2)}) collective-permute-start(f32[24,256]{1,0:T(8,128)S(1)} %get-tuple-element.29), channel_id=1, source_target_pairs={{0,96},{1,97},{2,98},{3,99},{4,100},{5,101},{6,102},{7,103},{8,104... | collective-permute-start | bytes 73736 | tf_op jit(solution)/shard_map/ppermute | solution.py:276
  56.6 1.3 %collective-permute-start.1 = (f32[24,256]{1,0:T(8,128)S(1)}, f32[24,256]{1,0:T(8,128)S(1)}, u32[]{:S(2)}, u32[]{:S(2)}) collective-permute-start(f32[24,256]{1,0:T(8,128)S(1)} %get-tuple-element.29), channel_id=1, source_target_pairs={{0,64},{32,96},{1,65},{33,97},{2,66},{34,98},{3,67},{35,99},{4,68}... | collective-permute-start | bytes 73736 | tf_op jit(solution)/shard_map/ppermute | solution.py:276
  57.9 2.8 %collective-permute-start = (f32[24,256]{1,0:T(8,128)S(1)}, f32[24,256]{1,0:T(8,128)S(1)}, u32[]{:S(2)}, u32[]{:S(2)}) collective-permute-start(f32[24,256]{1,0:T(8,128)S(1)} %get-tuple-element.29), channel_id=1, source_target_pairs={{0,32},{32,64},{64,96},{1,33},{33,65},{65,97},{2,34},{34,66},{66,9... | collective-permute-start | bytes 73736 | tf_op jit(solution)/shard_map/ppermute | solution.py:276
  60.6 0.0 collective-permute-done.2.farther_ref
  60.6 0.0 collective-permute-done.1.far_ref
  60.7 1.5 %collective-permute-done.near_ref = f32[24,256]{1,0:T(8,128)S(1)} collective-permute-done((f32[24,256]{1,0:T(8,128)S(1)}, f32[24,256]{1,0:T(8,128)S(1)}, u32[]{:S(2)}, u32[]{:S(2)}) %collective-permute-start) | collective-permute-done | bytes 24608 | tf_op jit(solution)/shard_map/ppermute | solution.py:276
  62.1 5.8 %shard_map.67.filtered_ref = f32[2,2048,128]{2,1,0:T(8,128)S(1)} custom-call(s32[3]{0:T(128)S(1)} %convert_reduce_fusion.bounds, f32[2,2176,128]{2,1,0:T(8,128)S(1)} %get-tuple-element.27.signal_ref, f32[16,16,8,256]{3,2,1,0:T(8,128)S(1)} %get-tuple-element.28.ends_ref, f32[24,256]{1,0:T(8,128)S(1)} %collective-permute-done.near_ref, ...), custom_call_target="tpu_custom_call" | custom-call | tf_op jit(solution)/shard_map/pallas_call | solution.py:264
  68.0 3.6 %all-to-all-done.arrived_ref = bf16[32,128,256]{2,1,0:T(8,128)(2,1)} async-done(((bf16[32,128,256]{2,1,0:T(8,128)(2,1)}), bf16[32,128,256]{2,1,0:T(8,128)(2,1)}, u32[]{:S(2)}, u32[]{:S(2)}) %all-to-all-start) | async-done | bytes 2097184 | tf_op jit(solution)/shard_map/all_to_all | solution.py:71
  71.5 3.1 %shard_map.68 = bf16[2048,256]{1,0:T(8,128)(2,1)} custom-call(s32[33]{0:T(128)S(1)} %pad_add_fusion.starts, bf16[32,128,256]{2,1,0:T(8,128)(2,1)} %all-to-all-done.arrived_ref, f32[2,2048,128]{2,1,0:T(8,128)S(1)} %shard_map.67.filtered_ref), custom_call_target="tpu_custom_call" | custom-call | tf_op jit(solution)/shard_map/pallas_call | solution.py:264
  (21 shorter events, 0.2 us)
Async XLA Ops:
  0.0 2.8 %copy-start = (bf16[128,3,8192]{2,0,1:T(8,128)(2,1)S(1)}, bf16[128,3,8192]{2,0,1:T(8,128)(2,1)}, u32[]{:S(2)}) copy-start(bf16[128,3,8192]{2,0,1:T(8,128)(2,1)} %param.6) | copy-start | bytes 18874372
  3.8 1.3 %copy-start.3 = (bf16[32,128,256]{2,1,0:T(8,128)(2,1)}, bf16[32,128,256]{2,1,0:T(8,128)(2,1)S(1)}, u32[]{:S(2)}) copy-start(bf16[32,128,256]{2,1,0:T(8,128)(2,1)S(1)} %shard_map.65) | copy-start | bytes 6291460
  5.1 34.0 %all-to-all-start.1 = ((bf16[32,128,256]{2,1,0:T(8,128)(2,1)}), bf16[32,128,256]{2,1,0:T(8,128)(2,1)S(1)}, u32[]{:S(2)}, u32[]{:S(2)}) async-start(bf16[32,128,256]{2,1,0:T(8,128)(2,1)} %copy-done.3), calls=%async_computation.1 | async-start | bytes 4194304 | tf_op jit(solution)/shard_map/all_to_all | solution.py:71
  15.3 2.8 %copy-start.1 = (bf16[128,3,8192]{2,0,1:T(8,128)(2,1)S(1)}, bf16[128,3,8192]{2,0,1:T(8,128)(2,1)}, u32[]{:S(2)}) copy-start(bf16[128,3,8192]{2,0,1:T(8,128)(2,1)} %param.6) | copy-start | bytes 18874372
  18.1 2.0 %copy-start.8 = (s32[1,32]{1,0:T(1,128)S(1)}, s32[1,32]{1,0:T(1,128)}, u32[]{:S(2)}) copy-start(s32[1,32]{1,0:T(1,128)} %param.7) | copy-start | bytes 388
  18.1 2.2 %copy-start.6 = (s32[2048]{0:T(1024)S(1)}, s32[2048]{0:T(1024)}, u32[]{:S(2)}) copy-start(s32[2048]{0:T(1024)} %param.8) | copy-start | bytes 24580
  18.1 2.4 %copy-start.4 = (f32[256,16]{0,1:T(8,128)S(1)}, f32[256,16]{0,1:T(8,128)}, u32[]{:S(2)}) copy-start(f32[256,16]{0,1:T(8,128)} %param.9) | copy-start | bytes 49156
  18.1 2.4 %copy-start.5 = (f32[256,16]{0,1:T(8,128)S(1)}, f32[256,16]{0,1:T(8,128)}, u32[]{:S(2)}) copy-start(f32[256,16]{0,1:T(8,128)} %param.10) | copy-start | bytes 49156
  18.1 2.6 %copy-start.7 = (f32[256]{0:T(256)S(1)}, f32[256]{0:T(256)}, u32[]{:S(2)}) copy-start(f32[256]{0:T(256)} %param.11) | copy-start | bytes 3076
  18.7 1.3 %copy-start.2 = (bf16[32,128,256]{2,1,0:T(8,128)(2,1)}, bf16[32,128,256]{2,1,0:T(8,128)(2,1)S(1)}, u32[]{:S(2)}) copy-start(bf16[32,128,256]{2,1,0:T(8,128)(2,1)S(1)} %shard_map.64) | copy-start | bytes 6291460
  39.1 32.5 %all-to-all-start = ((bf16[32,128,256]{2,1,0:T(8,128)(2,1)}), bf16[32,128,256]{2,1,0:T(8,128)(2,1)}, u32[]{:S(2)}, u32[]{:S(2)}) async-start(bf16[32,128,256]{2,1,0:T(8,128)(2,1)} %copy-done.2), calls=%async_computation | async-start | bytes 4194304 | tf_op jit(solution)/shard_map/all_to_all | solution.py:71
  51.6 9.0 %collective-permute-start.2 = (f32[24,256]{1,0:T(8,128)S(1)}, f32[24,256]{1,0:T(8,128)S(1)}, u32[]{:S(2)}, u32[]{:S(2)}) collective-permute-start(f32[24,256]{1,0:T(8,128)S(1)} %get-tuple-element.29), channel_id=1, source_target_pairs={{0,96},{1,97},{2,98},{3,99},{4,100},{5,101},{6,102},{7,103},{8,104... | collective-permute-start | bytes 73736 | tf_op jit(solution)/shard_map/ppermute | solution.py:276
  56.6 4.1 %collective-permute-start.1 = (f32[24,256]{1,0:T(8,128)S(1)}, f32[24,256]{1,0:T(8,128)S(1)}, u32[]{:S(2)}, u32[]{:S(2)}) collective-permute-start(f32[24,256]{1,0:T(8,128)S(1)} %get-tuple-element.29), channel_id=1, source_target_pairs={{0,64},{32,96},{1,65},{33,97},{2,66},{34,98},{3,67},{35,99},{4,68}... | collective-permute-start | bytes 73736 | tf_op jit(solution)/shard_map/ppermute | solution.py:276
  57.9 4.3 %collective-permute-start = (f32[24,256]{1,0:T(8,128)S(1)}, f32[24,256]{1,0:T(8,128)S(1)}, u32[]{:S(2)}, u32[]{:S(2)}) collective-permute-start(f32[24,256]{1,0:T(8,128)S(1)} %get-tuple-element.29), channel_id=1, source_target_pairs={{0,32},{32,64},{64,96},{1,33},{33,65},{65,97},{2,34},{34,66},{66,9... | collective-permute-start | bytes 73736 | tf_op jit(solution)/shard_map/ppermute | solution.py:276

commit v5 on v4

--- a/solution.py
+++ b/solution.py
@@ -54,9 +54,9 @@
     rows = streams.shape[1]
     return pl.pallas_call(
         functools.partial(send_kernel, planes, turn),
-        out_shape=jax.ShapeDtypeStruct((groups, rows, channels), BF16),
-        in_specs=[pl.BlockSpec(memory_space=pl.ANY)],
-        out_specs=pl.BlockSpec(memory_space=pl.ANY),
+        out_shape=pltpu.HBM((groups, rows, channels), BF16),
+        in_specs=[pl.BlockSpec(memory_space=pltpu.HBM)],
+        out_specs=pl.BlockSpec(memory_space=pltpu.HBM),
         scratch_shapes=[pltpu.VMEM((rows, groups * channels), BF16) for _ in planes]
         + [
             pltpu.VMEM((groups, rows, channels), BF16),
@@ -64,7 +64,7 @@
             pltpu.SemaphoreType.DMA((pieces,)),
         ],
         compiler_params=pltpu.CompilerParams(vmem_limit_bytes=24 << 20),
-    )(streams)
+    )(pltpu.with_memory_space_constraint(streams, pltpu.HBM))
 
 
 def exchange(value, order):

time: 76.1 us -> 74.4 us (0.978)
  local copies, waits for them, and re-layouts: 8.26 us -> 0.07 us
  Pallas kernels: 14.8 us -> 19 us
  waiting for transfers between devices: 23 us -> 25.2 us
    unnamed x18 -> x10, local copies, waits for them, and re-layouts: 8.21 us -> 0.03 us
    pallas_call x2, Pallas kernels: 1.6 us -> 5.84 us  [send(): pl.pallas_call(functools.partial(send_kernel, planes, turn), out_shape=pl...]
    all_to_all x2, waiting for transfers between devices: 21.5 us -> 23.8 us  [exchange(): lax.all_to_all(value, 'ch', split_axis=0, concat_axis=0, axis_index_group...]
  transfers between devices with their start and end apart: 5 -> 5, of which waited for: 3 -> 3; matrix products, arithmetic and copies ran while one was open for 1% -> 1% of each run, Pallas kernels for 14% -> 17%
where the time goes in v5:
time: 74.4 us; the launch traced here: 73 us
  starting transfers between devices  27.4 us (37%)
  waiting for transfers between devices  25.2 us (34%)
  Pallas kernels  19 us (26%)
  other arithmetic  0.98 us (1%)
    all_to_all x2, waiting for transfers between devices, exchange(): lax.all_to_all(value, 'ch', split_axis=0, concat_axis=0, axis_index_group...  23.8 us
    all_to_all x2, starting transfers between devices, exchange(): lax.all_to_all(value, 'ch', split_axis=0, concat_axis=0, axis_index_group...  18.5 us
    pallas_call x3, Pallas kernels, local_call(): pl.pallas_call(kernel, out_shape=outs, in_specs=[pl.BlockSpec(memory_spac...  13.2 us
    ppermute x3, starting transfers between devices, passed_along(): lax.ppermute(value, axis, [(source, source + steps) for source in range(c...  8.95 us
    pallas_call x2, Pallas kernels, send(): pl.pallas_call(functools.partial(send_kernel, planes, turn), out_shape=pl...  5.84 us
  transfers between devices with their start and end apart: 5, of which 3 were waited for; matrix products, arithmetic and copies ran while one was open for 1% of the time, Pallas kernels for 17%

profile of v5, /device:TPU:0, one launch (start us, length us, event | category | flops | bytes accessed | tf_op | source)
XLA Modules:
  0.0 73.0 jit_solution(7627139994646886164)
XLA Ops:
  0.0 3.4 %shard_map.65 = bf16[32,128,256]{2,1,0:T(8,128)(2,1)} custom-call(bf16[3,128,8192]{2,1,0:T(8,128)(2,1)} %bitcast.12), custom_call_target="tpu_custom_call" | custom-call | tf_op jit(solution)/shard_map/pallas_call | solution.py:55
  3.4 10.2 %all-to-all-start.1 = ((bf16[32,128,256]{2,1,0:T(8,128)(2,1)}), bf16[32,128,256]{2,1,0:T(8,128)(2,1)S(1)}, u32[]{:S(2)}, u32[]{:S(2)}) async-start(bf16[32,128,256]{2,1,0:T(8,128)(2,1)} %shard_map.65), calls=%async_computation.1 | async-start | bytes 4194304 | tf_op jit(solution)/shard_map/all_to_all | solution.py:71
  13.6 0.0 copy-start.4
  13.6 0.0 copy-start.2
  13.6 0.0 copy-start
  13.6 0.0 copy-start.1
  13.6 0.0 copy-start.3
  13.7 2.5 %shard_map.64 = bf16[32,128,256]{2,1,0:T(8,128)(2,1)} custom-call(bf16[3,128,8192]{2,1,0:T(8,128)(2,1)} %bitcast.13), custom_call_target="tpu_custom_call" | custom-call | tf_op jit(solution)/shard_map/pallas_call | solution.py:55
  16.2 0.0 copy-done.4
  16.2 0.1 select_reduce_fusion
  16.3 0.1 pad_add_fusion.starts
  16.4 0.0 copy-done.2
  16.4 0.2 convert_reduce_fusion.bounds
  16.6 0.0 copy-done
  16.6 0.1 multiply_reduce_fusion
  16.8 0.0 copy-done.3
  16.8 0.1 select_add_fusion
  16.9 0.1 broadcast_select_fusion.2.one_ref
  17.0 0.1 multiply_exponential_fusion
  17.1 0.1 broadcast_select_fusion
  17.2 20.1 %all-to-all-done.1.arrived_ref = bf16[32,128,256]{2,1,0:T(8,128)(2,1)S(1)} async-done(((bf16[32,128,256]{2,1,0:T(8,128)(2,1)}), bf16[32,128,256]{2,1,0:T(8,128)(2,1)S(1)}, u32[]{:S(2)}, u32[]{:S(2)}) %all-to-all-start.1) | async-done | bytes 2097184 | tf_op jit(solution)/shard_map/all_to_all | solution.py:71
  37.4 8.3 %all-to-all-start = ((bf16[32,128,256]{2,1,0:T(8,128)(2,1)}), bf16[32,128,256]{2,1,0:T(8,128)(2,1)}, u32[]{:S(2)}, u32[]{:S(2)}) async-start(bf16[32,128,256]{2,1,0:T(8,128)(2,1)} %shard_map.64), calls=%async_computation | async-start | bytes 4194304 | tf_op jit(solution)/shard_map/all_to_all | solution.py:71
  45.7 4.2 %shard_map.66 = (f32[2,2176,128]{2,1,0:T(8,128)S(1)}, f32[16,16,8,256]{3,2,1,0:T(8,128)S(1)}, f32[24,256]{1,0:T(8,128)S(1)}) custom-call(s32[33]{0:T(128)S(1)} %pad_add_fusion.starts, s32[3]{0:T(128)S(1)} %convert_reduce_fusion.bounds, bf16[32,128,256]{2,1,0:T(8,128)(2,1)S(1)} %all-to-all-done.1.arrived_ref, f32[16,8,256]{2,1,0:T(8,128)S(1)} %mul.138.decay_ref, ...), custom_call_target="tpu_custom_call" | custom-call | tf_op jit(solution)/shard_map/pallas_call | solution.py:264
  50.0 4.9 %collective-permute-start.2 = (f32[24,256]{1,0:T(8,128)S(1)}, f32[24,256]{1,0:T(8,128)S(1)}, u32[]{:S(2)}, u32[]{:S(2)}) collective-permute-start(f32[24,256]{1,0:T(8,128)S(1)} %get-tuple-element.29), channel_id=1, source_target_pairs={{0,96},{1,97},{2,98},{3,99},{4,100},{5,101},{6,102},{7,103},{8,104... | collective-permute-start | bytes 73736 | tf_op jit(solution)/shard_map/ppermute | solution.py:276
  54.9 1.3 %collective-permute-start.1 = (f32[24,256]{1,0:T(8,128)S(1)}, f32[24,256]{1,0:T(8,128)S(1)}, u32[]{:S(2)}, u32[]{:S(2)}) collective-permute-start(f32[24,256]{1,0:T(8,128)S(1)} %get-tuple-element.29), channel_id=1, source_target_pairs={{0,64},{32,96},{1,65},{33,97},{2,66},{34,98},{3,67},{35,99},{4,68}... | collective-permute-start | bytes 73736 | tf_op jit(solution)/shard_map/ppermute | solution.py:276
  56.2 2.8 %collective-permute-start = (f32[24,256]{1,0:T(8,128)S(1)}, f32[24,256]{1,0:T(8,128)S(1)}, u32[]{:S(2)}, u32[]{:S(2)}) collective-permute-start(f32[24,256]{1,0:T(8,128)S(1)} %get-tuple-element.29), channel_id=1, source_target_pairs={{0,32},{32,64},{64,96},{1,33},{33,65},{65,97},{2,34},{34,66},{66,9... | collective-permute-start | bytes 73736 | tf_op jit(solution)/shard_map/ppermute | solution.py:276
  58.9 0.0 collective-permute-done.2.farther_ref
  58.9 0.0 collective-permute-done.1.far_ref
  58.9 1.5 %collective-permute-done.near_ref = f32[24,256]{1,0:T(8,128)S(1)} collective-permute-done((f32[24,256]{1,0:T(8,128)S(1)}, f32[24,256]{1,0:T(8,128)S(1)}, u32[]{:S(2)}, u32[]{:S(2)}) %collective-permute-start) | collective-permute-done | bytes 24608 | tf_op jit(solution)/shard_map/ppermute | solution.py:276
  60.4 5.8 %shard_map.67.filtered_ref = f32[2,2048,128]{2,1,0:T(8,128)S(1)} custom-call(s32[3]{0:T(128)S(1)} %convert_reduce_fusion.bounds, f32[2,2176,128]{2,1,0:T(8,128)S(1)} %get-tuple-element.27.signal_ref, f32[16,16,8,256]{3,2,1,0:T(8,128)S(1)} %get-tuple-element.28.ends_ref, f32[24,256]{1,0:T(8,128)S(1)} %collective-permute-done.near_ref, ...), custom_call_target="tpu_custom_call" | custom-call | tf_op jit(solution)/shard_map/pallas_call | solution.py:264
  66.2 3.6 %all-to-all-done.arrived_ref = bf16[32,128,256]{2,1,0:T(8,128)(2,1)} async-done(((bf16[32,128,256]{2,1,0:T(8,128)(2,1)}), bf16[32,128,256]{2,1,0:T(8,128)(2,1)}, u32[]{:S(2)}, u32[]{:S(2)}) %all-to-all-start) | async-done | bytes 2097184 | tf_op jit(solution)/shard_map/all_to_all | solution.py:71
  69.9 3.1 %shard_map.68 = bf16[2048,256]{1,0:T(8,128)(2,1)} custom-call(s32[33]{0:T(128)S(1)} %pad_add_fusion.starts, bf16[32,128,256]{2,1,0:T(8,128)(2,1)} %all-to-all-done.arrived_ref, f32[2,2048,128]{2,1,0:T(8,128)S(1)} %shard_map.67.filtered_ref), custom_call_target="tpu_custom_call" | custom-call | tf_op jit(solution)/shard_map/pallas_call | solution.py:264
  (13 shorter events, 0.1 us)
Async XLA Ops:
  3.4 34.0 %all-to-all-start.1 = ((bf16[32,128,256]{2,1,0:T(8,128)(2,1)}), bf16[32,128,256]{2,1,0:T(8,128)(2,1)S(1)}, u32[]{:S(2)}, u32[]{:S(2)}) async-start(bf16[32,128,256]{2,1,0:T(8,128)(2,1)} %shard_map.65), calls=%async_computation.1 | async-start | bytes 4194304 | tf_op jit(solution)/shard_map/all_to_all | solution.py:71
  13.6 2.6 %copy-start.4 = (s32[1,32]{1,0:T(1,128)S(1)}, s32[1,32]{1,0:T(1,128)}, u32[]{:S(2)}) copy-start(s32[1,32]{1,0:T(1,128)} %param.7) | copy-start | bytes 388
  13.6 2.8 %copy-start.2 = (s32[2048]{0:T(1024)S(1)}, s32[2048]{0:T(1024)}, u32[]{:S(2)}) copy-start(s32[2048]{0:T(1024)} %param.8) | copy-start | bytes 24580
  13.6 3.0 %copy-start = (f32[256,16]{0,1:T(8,128)S(1)}, f32[256,16]{0,1:T(8,128)}, u32[]{:S(2)}) copy-start(f32[256,16]{0,1:T(8,128)} %param.9) | copy-start | bytes 49156
  13.6 3.0 %copy-start.1 = (f32[256,16]{0,1:T(8,128)S(1)}, f32[256,16]{0,1:T(8,128)}, u32[]{:S(2)}) copy-start(f32[256,16]{0,1:T(8,128)} %param.10) | copy-start | bytes 49156
  13.6 3.1 %copy-start.3 = (f32[256]{0:T(256)S(1)}, f32[256]{0:T(256)}, u32[]{:S(2)}) copy-start(f32[256]{0:T(256)} %param.11) | copy-start | bytes 3076
  37.4 32.5 %all-to-all-start = ((bf16[32,128,256]{2,1,0:T(8,128)(2,1)}), bf16[32,128,256]{2,1,0:T(8,128)(2,1)}, u32[]{:S(2)}, u32[]{:S(2)}) async-start(bf16[32,128,256]{2,1,0:T(8,128)(2,1)} %shard_map.64), calls=%async_computation | async-start | bytes 4194304 | tf_op jit(solution)/shard_map/all_to_all | solution.py:71
  50.0 9.0 %collective-permute-start.2 = (f32[24,256]{1,0:T(8,128)S(1)}, f32[24,256]{1,0:T(8,128)S(1)}, u32[]{:S(2)}, u32[]{:S(2)}) collective-permute-start(f32[24,256]{1,0:T(8,128)S(1)} %get-tuple-element.29), channel_id=1, source_target_pairs={{0,96},{1,97},{2,98},{3,99},{4,100},{5,101},{6,102},{7,103},{8,104... | collective-permute-start | bytes 73736 | tf_op jit(solution)/shard_map/ppermute | solution.py:276
  54.9 4.1 %collective-permute-start.1 = (f32[24,256]{1,0:T(8,128)S(1)}, f32[24,256]{1,0:T(8,128)S(1)}, u32[]{:S(2)}, u32[]{:S(2)}) collective-permute-start(f32[24,256]{1,0:T(8,128)S(1)} %get-tuple-element.29), channel_id=1, source_target_pairs={{0,64},{32,96},{1,65},{33,97},{2,66},{34,98},{3,67},{35,99},{4,68}... | collective-permute-start | bytes 73736 | tf_op jit(solution)/shard_map/ppermute | solution.py:276
  56.2 4.3 %collective-permute-start = (f32[24,256]{1,0:T(8,128)S(1)}, f32[24,256]{1,0:T(8,128)S(1)}, u32[]{:S(2)}, u32[]{:S(2)}) collective-permute-start(f32[24,256]{1,0:T(8,128)S(1)} %get-tuple-element.29), channel_id=1, source_target_pairs={{0,32},{32,64},{64,96},{1,33},{33,65},{65,97},{2,34},{34,66},{66,9... | collective-permute-start | bytes 73736 | tf_op jit(solution)/shard_map/ppermute | solution.py:276

commit v6 on v5

--- a/solution.py
+++ b/solution.py
@@ -11,17 +11,19 @@
 STEPS = 16
 LANES = 128
 SUB = 8
-TURN = 12
+SIGNAL_TURN = 12
+QUERY_TURN = 12
+LOADS = 4
+STORES = 8
 F32 = jnp.float32
 BF16 = jnp.bfloat16
 
 
 def send_kernel(planes, turn, streams_ref, out_ref, *scratch):
     held, ready, in_sems, out_sems = scratch[:-3], scratch[-3], scratch[-2], scratch[-1]
-    pieces = in_sems.shape[1]
     groups, _, channels = out_ref.shape
-    per = groups // pieces
-    width = per * channels
+    width = groups * channels // LOADS
+    per = groups // STORES
 
     def load(plane, piece):
         columns = pl.ds(piece * width, width)
@@ -33,12 +35,13 @@
         goes = (piece * per + turn) % groups
         return pltpu.make_async_copy(ready.at[pl.ds(piece * per, per)], out_ref.at[pl.ds(goes, per)], out_sems.at[piece])
 
-    for piece in range(pieces):
+    for piece in range(LOADS):
         for plane in range(len(planes)):
             load(plane, piece).start()
-    for piece in range(pieces):
-        for plane in range(len(planes)):
-            load(plane, piece).wait()
+    for piece in range(STORES):
+        if piece % (STORES // LOADS) == 0:
+            for plane in range(len(planes)):
+                load(plane, piece // (STORES // LOADS)).wait()
         for part in range(piece * per, (piece + 1) * per):
             columns = pl.ds(part * channels, channels)
             value = held[0][:, columns]
@@ -46,11 +49,11 @@
                 value = value * other[:, columns]
             ready[part] = value
         store(piece).start()
-    for piece in range(pieces):
+    for piece in range(STORES):
         store(piece).wait()
 
 
-def send(planes, streams, groups, channels, turn, pieces):
+def send(planes, streams, groups, channels, turn):
     rows = streams.shape[1]
     return pl.pallas_call(
         functools.partial(send_kernel, planes, turn),
@@ -60,18 +63,20 @@
         scratch_shapes=[pltpu.VMEM((rows, groups * channels), BF16) for _ in planes]
         + [
             pltpu.VMEM((groups, rows, channels), BF16),
-            pltpu.SemaphoreType.DMA((len(planes), pieces)),
-            pltpu.SemaphoreType.DMA((pieces,)),
+            pltpu.SemaphoreType.DMA((len(planes), LOADS)),
+            pltpu.SemaphoreType.DMA((STORES,)),
         ],
         compiler_params=pltpu.CompilerParams(vmem_limit_bytes=24 << 20),
     )(pltpu.with_memory_space_constraint(streams, pltpu.HBM))
 
 
-def exchange(value, order):
+def exchange(value, turn):
+    groups = value.shape[0]
+    order = [(rank - turn) % groups for rank in range(groups)]
     return lax.all_to_all(value, "ch", split_axis=0, concat_axis=0, axis_index_groups=[order], tiled=True)
 
 
-def compact(turn, starts, arrived_ref, into_ref):
+def compact(turn, starts, arrived_ref, into_ref, first, last):
     sources, rows, channels = arrived_ref.shape
 
     def place(source, unused):
@@ -84,7 +89,7 @@
                 into_ref[tile, pl.ds(begin + part + SUB, SUB), :] = piece[SUB:]
         return unused
 
-    lax.fori_loop(0, sources, place, 0)
+    lax.fori_loop(first, last, place, 0)
 
 
 def segment(position, bounds):
@@ -99,7 +104,7 @@
     blocks, modes, _, channels = ends_ref.shape
     carry[...] = jnp.zeros_like(carry)
     rank = lax.broadcasted_iota(jnp.int32, (SUB, LANES), 0)
-    compact(turn, starts, arrived_ref, signal_ref)
+    compact(turn, starts, arrived_ref, signal_ref, 0, arrived_ref.shape[0])
 
     def one(block, unused):
         begin = block * BLOCK
@@ -233,39 +238,51 @@
     lax.fori_loop(0, blocks, one, 0)
 
 
-def mix_kernel(turn, starts, arrived_ref, filtered_ref, out_ref, held, ready, sems):
-    pieces = sems.shape[0]
+def mix_kernel(turn, starts, arrived_ref, filtered_ref, out_ref, landed, held, ready, in_sems, out_sems):
     tiles, length, _ = filtered_ref.shape
-    per = length // BLOCK // pieces
-    compact(turn, starts, arrived_ref, held)
-
-    def one(block, unused):
+    pieces = in_sems.shape[0]
+    sources = arrived_ref.shape[0]
+    per = sources // pieces
+
+    def load(piece):
+        slots = pl.ds((piece * per + turn) % sources, per)
+        return pltpu.make_async_copy(arrived_ref.at[slots], landed.at[slots], in_sems.at[piece])
+
+    def store(block):
+        rows = pl.ds(pl.multiple_of(block * BLOCK, BLOCK), BLOCK)
+        return pltpu.make_async_copy(ready.at[rows, :], out_ref.at[rows, :], out_sems.at[block])
+
+    def finish(block, unused):
         rows = pl.ds(pl.multiple_of(block * BLOCK, BLOCK), BLOCK)
         for tile in range(tiles):
             ready[rows, pl.ds(tile * LANES, LANES)] = (held[tile, rows, :] * filtered_ref[tile, rows, :]).astype(BF16)
+        store(block).start()
         return unused
 
-    def copy(piece):
-        rows = pl.ds(piece * per * BLOCK, per * BLOCK)
-        return pltpu.make_async_copy(ready.at[rows, :], out_ref.at[rows, :], sems.at[piece])
-
     for piece in range(pieces):
-        lax.fori_loop(piece * per, (piece + 1) * per, one, 0)
-        copy(piece).start()
+        load(piece).start()
+    complete = 0
     for piece in range(pieces):
-        copy(piece).wait()
+        load(piece).wait()
+        compact(turn, starts, landed, held, piece * per, (piece + 1) * per)
+        reached = starts[(piece + 1) * per] >> 7
+        lax.fori_loop(complete, reached, finish, 0)
+        complete = reached
+    for block in range(length // BLOCK):
+        store(block).wait()
 
 
 def near_by(array):
     return pltpu.with_memory_space_constraint(array, pltpu.VMEM)
 
 
-def local_call(kernel, outs, scalars, arrays, scratch, out_space=pltpu.VMEM):
+def local_call(kernel, outs, scalars, arrays, scratch):
+    spaces = (pltpu.SMEM,) * len(scalars) + (pltpu.VMEM,) * len(arrays)
     return pl.pallas_call(
         kernel,
         out_shape=outs,
-        in_specs=[pl.BlockSpec(memory_space=pltpu.SMEM)] * len(scalars) + [pl.BlockSpec(memory_space=pltpu.VMEM)] * len(arrays),
-        out_specs=jax.tree.map(lambda _: pl.BlockSpec(memory_space=out_space), outs),
+        in_specs=[pl.BlockSpec(memory_space=space) for space in spaces],
+        out_specs=jax.tree.map(lambda _: pl.BlockSpec(memory_space=pltpu.VMEM), outs),
         scratch_shapes=scratch,
         compiler_params=pltpu.CompilerParams(vmem_limit_bytes=24 << 20),
     )(*scalars, *[near_by(array) for array in arrays])
@@ -284,9 +301,8 @@
     blocks = length // BLOCK
     counts = load_counts[0]
     planes = jnp.transpose(streams, (1, 0, 2))
-    order = [(rank - TURN) % groups for rank in range(groups)]
-    signal_in = exchange(send((1, 2), planes, groups, channels, TURN, 8), order)
-    query_out = send((0,), planes, groups, channels, TURN, 8)
+    signal_in = exchange(send((1, 2), planes, groups, channels, SIGNAL_TURN), SIGNAL_TURN)
+    query_out = send((0,), planes, groups, channels, QUERY_TURN)
 
     ending = jnp.sum(jnp.where(jnp.arange(groups)[:, None] >= jnp.arange(groups)[None, :], counts[None, :], 0), axis=1)
     starts = jnp.concatenate([jnp.zeros((1,), jnp.int32), ending]).astype(jnp.int32)
@@ -318,11 +334,11 @@
     prepared = (starts, bounds, decay, weight, leap, one_coef, two_coef, four_coef, onward, scale_b, taps_b, span)
     query_out, prepared = lax.optimization_barrier((query_out, prepared))
     starts, bounds, decay, weight, leap, one_coef, two_coef, four_coef, onward, scale_b, taps_b, span = prepared
-    query_in = exchange(query_out, order)
+    query_in = exchange(query_out, QUERY_TURN)
 
     padded = (channels // LANES, length + capacity, LANES)
     signal, ends, passing = local_call(
-        functools.partial(scan_kernel, TURN),
+        functools.partial(scan_kernel, SIGNAL_TURN),
         (
             pltpu.VMEM(padded, F32),
             pltpu.VMEM((blocks, modes, SUB, channels), F32),
@@ -343,19 +359,21 @@
         (signal, ends, near, far, farther, decay, one_coef, two_coef, four_coef, onward, scale_b, taps_b, span),
         [pltpu.VMEM((modes, SUB, channels), F32)],
     )
-    pieces = 4
-    return local_call(
-        functools.partial(mix_kernel, TURN),
-        jax.ShapeDtypeStruct((length, channels), BF16),
-        (starts,),
-        (query_in, filtered),
-        [
+    pieces = 8
+    return pl.pallas_call(
+        functools.partial(mix_kernel, QUERY_TURN),
+        out_shape=pltpu.HBM((length, channels), BF16),
+        in_specs=[pl.BlockSpec(memory_space=space) for space in (pltpu.SMEM, pltpu.HBM, pltpu.VMEM)],
+        out_specs=pl.BlockSpec(memory_space=pltpu.HBM),
+        scratch_shapes=[
+            pltpu.VMEM((groups, capacity, channels), BF16),
             pltpu.VMEM(padded, F32),
             pltpu.VMEM((length, channels), BF16),
             pltpu.SemaphoreType.DMA((pieces,)),
+            pltpu.SemaphoreType.DMA((blocks,)),
         ],
-        pl.ANY,
-    )
+        compiler_params=pltpu.CompilerParams(vmem_limit_bytes=24 << 20),
+    )(starts, pltpu.with_memory_space_constraint(query_in, pltpu.HBM), near_by(filtered))
 
 
 def solution(mesh):

time: 74.4 us -> 74.1 us (level)
    pallas_call x3 -> x2, Pallas kernels: 13.2 us -> 10 us  [local_call(): pl.pallas_call(kernel, out_shape=outs, in_specs=[pl.BlockSpec(memory_spac...]
    pallas_call x0 -> x1, Pallas kernels: none -> 3.08 us  [shards(): pl.pallas_call(functools.partial(mix_kernel, QUERY_TURN), out_shape=pltpu...]
where the time goes in v6:
time: 74.1 us; the launch traced here: 72.7 us
  starting transfers between devices  27.5 us (37%)
  waiting for transfers between devices  25.2 us (34%)
  Pallas kernels  18.8 us (25%)
  other arithmetic  0.98 us (1%)
    all_to_all x2, waiting for transfers between devices, exchange(): lax.all_to_all(value, 'ch', split_axis=0, concat_axis=0, axis_index_group...  23.7 us
    all_to_all x2, starting transfers between devices, exchange(): lax.all_to_all(value, 'ch', split_axis=0, concat_axis=0, axis_index_group...  18.5 us
    pallas_call x2, Pallas kernels, local_call(): pl.pallas_call(kernel, out_shape=outs, in_specs=[pl.BlockSpec(memory_spac...  10 us
    ppermute x3, starting transfers between devices, passed_along(): lax.ppermute(value, axis, [(source, source + steps) for source in range(c...  8.97 us
    pallas_call x2, Pallas kernels, send(): pl.pallas_call(functools.partial(send_kernel, planes, turn), out_shape=pl...  5.69 us
    pallas_call x1, Pallas kernels, shards(): pl.pallas_call(functools.partial(mix_kernel, QUERY_TURN), out_shape=pltpu...  3.08 us
    ppermute x3, waiting for transfers between devices, passed_along(): lax.ppermute(value, axis, [(source, source + steps) for source in range(c...  1.49 us
  transfers between devices with their start and end apart: 5, of which 3 were waited for; matrix products, arithmetic and copies ran while one was open for 1% of the time, Pallas kernels for 17%

profile of v6, /device:TPU:0, one launch (start us, length us, event | category | flops | bytes accessed | tf_op | source)
XLA Modules:
  0.0 72.7 jit_solution(8416439427319625010)
XLA Ops:
  0.0 3.2 %shard_map.65 = bf16[32,128,256]{2,1,0:T(8,128)(2,1)} custom-call(bf16[3,128,8192]{2,1,0:T(8,128)(2,1)} %bitcast.12), custom_call_target="tpu_custom_call" | custom-call | tf_op jit(solution)/shard_map/pallas_call | solution.py:58
  3.2 10.2 %all-to-all-start.1 = ((bf16[32,128,256]{2,1,0:T(8,128)(2,1)}), bf16[32,128,256]{2,1,0:T(8,128)(2,1)S(1)}, u32[]{:S(2)}, u32[]{:S(2)}) async-start(bf16[32,128,256]{2,1,0:T(8,128)(2,1)} %shard_map.65), calls=%async_computation.1 | async-start | bytes 4194304 | tf_op jit(solution)/shard_map/all_to_all | solution.py:76
  13.4 0.0 copy-start.4
  13.4 0.0 copy-start.2
  13.4 0.0 copy-start
  13.4 0.0 copy-start.1
  13.4 0.0 copy-start.3
  13.5 2.5 %shard_map.64 = bf16[32,128,256]{2,1,0:T(8,128)(2,1)} custom-call(bf16[3,128,8192]{2,1,0:T(8,128)(2,1)} %bitcast.13), custom_call_target="tpu_custom_call" | custom-call | tf_op jit(solution)/shard_map/pallas_call | solution.py:58
  16.0 0.0 copy-done.4
  16.0 0.1 select_reduce_fusion
  16.1 0.1 pad_add_fusion.starts
  16.2 0.0 copy-done.2
  16.2 0.2 convert_reduce_fusion.bounds
  16.4 0.0 copy-done
  16.4 0.0 copy-done.1
  16.5 0.1 multiply_reduce_fusion
  16.7 0.1 select_add_fusion
  16.7 0.1 broadcast_select_fusion.2.one_ref
  16.8 0.1 multiply_exponential_fusion
  16.9 0.1 broadcast_select_fusion
  17.1 20.1 %all-to-all-done.1.arrived_ref = bf16[32,128,256]{2,1,0:T(8,128)(2,1)S(1)} async-done(((bf16[32,128,256]{2,1,0:T(8,128)(2,1)}), bf16[32,128,256]{2,1,0:T(8,128)(2,1)S(1)}, u32[]{:S(2)}, u32[]{:S(2)}) %all-to-all-start.1) | async-done | bytes 2097184 | tf_op jit(solution)/shard_map/all_to_all | solution.py:76
  37.2 8.3 %all-to-all-start = ((bf16[32,128,256]{2,1,0:T(8,128)(2,1)}), bf16[32,128,256]{2,1,0:T(8,128)(2,1)}, u32[]{:S(2)}, u32[]{:S(2)}) async-start(bf16[32,128,256]{2,1,0:T(8,128)(2,1)} %shard_map.64), calls=%async_computation | async-start | bytes 4194304 | tf_op jit(solution)/shard_map/all_to_all | solution.py:76
  45.5 4.2 %shard_map.66 = (f32[2,2176,128]{2,1,0:T(8,128)S(1)}, f32[16,16,8,256]{3,2,1,0:T(8,128)S(1)}, f32[24,256]{1,0:T(8,128)S(1)}) custom-call(s32[33]{0:T(128)S(1)} %pad_add_fusion.starts, s32[3]{0:T(128)S(1)} %convert_reduce_fusion.bounds, bf16[32,128,256]{2,1,0:T(8,128)(2,1)S(1)} %all-to-all-done.1.arrived_ref, f32[16,8,256]{2,1,0:T(8,128)S(1)} %mul.138.decay_ref, ...), custom_call_target="tpu_custom_call" | custom-call | tf_op jit(solution)/shard_map/pallas_call | solution.py:281
  49.8 4.9 %collective-permute-start.2 = (f32[24,256]{1,0:T(8,128)S(1)}, f32[24,256]{1,0:T(8,128)S(1)}, u32[]{:S(2)}, u32[]{:S(2)}) collective-permute-start(f32[24,256]{1,0:T(8,128)S(1)} %get-tuple-element.29), channel_id=1, source_target_pairs={{0,96},{1,97},{2,98},{3,99},{4,100},{5,101},{6,102},{7,103},{8,104... | collective-permute-start | bytes 73736 | tf_op jit(solution)/shard_map/ppermute | solution.py:293
  54.7 1.3 %collective-permute-start.1 = (f32[24,256]{1,0:T(8,128)S(1)}, f32[24,256]{1,0:T(8,128)S(1)}, u32[]{:S(2)}, u32[]{:S(2)}) collective-permute-start(f32[24,256]{1,0:T(8,128)S(1)} %get-tuple-element.29), channel_id=1, source_target_pairs={{0,64},{32,96},{1,65},{33,97},{2,66},{34,98},{3,67},{35,99},{4,68}... | collective-permute-start | bytes 73736 | tf_op jit(solution)/shard_map/ppermute | solution.py:293
  56.0 2.8 %collective-permute-start = (f32[24,256]{1,0:T(8,128)S(1)}, f32[24,256]{1,0:T(8,128)S(1)}, u32[]{:S(2)}, u32[]{:S(2)}) collective-permute-start(f32[24,256]{1,0:T(8,128)S(1)} %get-tuple-element.29), channel_id=1, source_target_pairs={{0,32},{32,64},{64,96},{1,33},{33,65},{65,97},{2,34},{34,66},{66,9... | collective-permute-start | bytes 73736 | tf_op jit(solution)/shard_map/ppermute | solution.py:293
  58.7 0.0 collective-permute-done.2.farther_ref
  58.8 0.0 collective-permute-done.1.far_ref
  58.8 1.5 %collective-permute-done.near_ref = f32[24,256]{1,0:T(8,128)S(1)} collective-permute-done((f32[24,256]{1,0:T(8,128)S(1)}, f32[24,256]{1,0:T(8,128)S(1)}, u32[]{:S(2)}, u32[]{:S(2)}) %collective-permute-start) | collective-permute-done | bytes 24608 | tf_op jit(solution)/shard_map/ppermute | solution.py:293
  60.3 5.8 %shard_map.67.filtered_ref = f32[2,2048,128]{2,1,0:T(8,128)S(1)} custom-call(s32[3]{0:T(128)S(1)} %convert_reduce_fusion.bounds, f32[2,2176,128]{2,1,0:T(8,128)S(1)} %get-tuple-element.27.signal_ref, f32[16,16,8,256]{3,2,1,0:T(8,128)S(1)} %get-tuple-element.28.ends_ref, f32[24,256]{1,0:T(8,128)S(1)} %collective-permute-done.near_ref, ...), custom_call_target="tpu_custom_call" | custom-call | tf_op jit(solution)/shard_map/pallas_call | solution.py:281
  66.1 3.6 %all-to-all-done.arrived_ref = bf16[32,128,256]{2,1,0:T(8,128)(2,1)} async-done(((bf16[32,128,256]{2,1,0:T(8,128)(2,1)}), bf16[32,128,256]{2,1,0:T(8,128)(2,1)}, u32[]{:S(2)}, u32[]{:S(2)}) %all-to-all-start) | async-done | bytes 2097184 | tf_op jit(solution)/shard_map/all_to_all | solution.py:76
  69.7 3.1 %shard_map.68 = bf16[2048,256]{1,0:T(8,128)(2,1)} custom-call(s32[33]{0:T(128)S(1)} %pad_add_fusion.starts, bf16[32,128,256]{2,1,0:T(8,128)(2,1)} %all-to-all-done.arrived_ref, f32[2,2048,128]{2,1,0:T(8,128)S(1)} %shard_map.67.filtered_ref), custom_call_target="tpu_custom_call" | custom-call | tf_op jit(solution)/shard_map/pallas_call | solution.py:363
  (13 shorter events, 0.1 us)
Async XLA Ops:
  3.2 34.0 %all-to-all-start.1 = ((bf16[32,128,256]{2,1,0:T(8,128)(2,1)}), bf16[32,128,256]{2,1,0:T(8,128)(2,1)S(1)}, u32[]{:S(2)}, u32[]{:S(2)}) async-start(bf16[32,128,256]{2,1,0:T(8,128)(2,1)} %shard_map.65), calls=%async_computation.1 | async-start | bytes 4194304 | tf_op jit(solution)/shard_map/all_to_all | solution.py:76
  13.4 2.6 %copy-start.4 = (s32[1,32]{1,0:T(1,128)S(1)}, s32[1,32]{1,0:T(1,128)}, u32[]{:S(2)}) copy-start(s32[1,32]{1,0:T(1,128)} %param.7) | copy-start | bytes 388
  13.4 2.8 %copy-start.2 = (s32[2048]{0:T(1024)S(1)}, s32[2048]{0:T(1024)}, u32[]{:S(2)}) copy-start(s32[2048]{0:T(1024)} %param.8) | copy-start | bytes 24580
  13.4 3.0 %copy-start = (f32[256,16]{0,1:T(8,128)S(1)}, f32[256,16]{0,1:T(8,128)}, u32[]{:S(2)}) copy-start(f32[256,16]{0,1:T(8,128)} %param.9) | copy-start | bytes 49156
  13.4 3.0 %copy-start.1 = (f32[256,16]{0,1:T(8,128)S(1)}, f32[256,16]{0,1:T(8,128)}, u32[]{:S(2)}) copy-start(f32[256,16]{0,1:T(8,128)} %param.10) | copy-start | bytes 49156
  13.4 3.2 %copy-start.3 = (f32[256]{0:T(256)S(1)}, f32[256]{0:T(256)}, u32[]{:S(2)}) copy-start(f32[256]{0:T(256)} %param.11) | copy-start | bytes 3076
  37.2 32.5 %all-to-all-start = ((bf16[32,128,256]{2,1,0:T(8,128)(2,1)}), bf16[32,128,256]{2,1,0:T(8,128)(2,1)}, u32[]{:S(2)}, u32[]{:S(2)}) async-start(bf16[32,128,256]{2,1,0:T(8,128)(2,1)} %shard_map.64), calls=%async_computation | async-start | bytes 4194304 | tf_op jit(solution)/shard_map/all_to_all | solution.py:76
  49.8 9.0 %collective-permute-start.2 = (f32[24,256]{1,0:T(8,128)S(1)}, f32[24,256]{1,0:T(8,128)S(1)}, u32[]{:S(2)}, u32[]{:S(2)}) collective-permute-start(f32[24,256]{1,0:T(8,128)S(1)} %get-tuple-element.29), channel_id=1, source_target_pairs={{0,96},{1,97},{2,98},{3,99},{4,100},{5,101},{6,102},{7,103},{8,104... | collective-permute-start | bytes 73736 | tf_op jit(solution)/shard_map/ppermute | solution.py:293
  54.7 4.1 %collective-permute-start.1 = (f32[24,256]{1,0:T(8,128)S(1)}, f32[24,256]{1,0:T(8,128)S(1)}, u32[]{:S(2)}, u32[]{:S(2)}) collective-permute-start(f32[24,256]{1,0:T(8,128)S(1)} %get-tuple-element.29), channel_id=1, source_target_pairs={{0,64},{32,96},{1,65},{33,97},{2,66},{34,98},{3,67},{35,99},{4,68}... | collective-permute-start | bytes 73736 | tf_op jit(solution)/shard_map/ppermute | solution.py:293
  56.0 4.3 %collective-permute-start = (f32[24,256]{1,0:T(8,128)S(1)}, f32[24,256]{1,0:T(8,128)S(1)}, u32[]{:S(2)}, u32[]{:S(2)}) collective-permute-start(f32[24,256]{1,0:T(8,128)S(1)} %get-tuple-element.29), channel_id=1, source_target_pairs={{0,32},{32,64},{64,96},{1,33},{33,65},{65,97},{2,34},{34,66},{66,9... | collective-permute-start | bytes 73736 | tf_op jit(solution)/shard_map/ppermute | solution.py:293

commit v7 on v6

--- a/solution.py
+++ b/solution.py
@@ -15,6 +15,7 @@
 QUERY_TURN = 12
 LOADS = 4
 STORES = 8
+PIECES = 8
 F32 = jnp.float32
 BF16 = jnp.bfloat16
 
@@ -67,7 +68,7 @@
             pltpu.SemaphoreType.DMA((STORES,)),
         ],
         compiler_params=pltpu.CompilerParams(vmem_limit_bytes=24 << 20),
-    )(pltpu.with_memory_space_constraint(streams, pltpu.HBM))
+    )(far_off(streams))
 
 
 def exchange(value, turn):
@@ -238,7 +239,7 @@
     lax.fori_loop(0, blocks, one, 0)
 
 
-def mix_kernel(turn, starts, arrived_ref, filtered_ref, out_ref, landed, held, ready, in_sems, out_sems):
+def mix_kernel(turn, starts_ref, arrived_ref, filtered_ref, out_ref, starts, landed, held, ready, table_sem, in_sems, out_sems):
     tiles, length, _ = filtered_ref.shape
     pieces = in_sems.shape[0]
     sources = arrived_ref.shape[0]
@@ -259,8 +260,11 @@
         store(block).start()
         return unused
 
+    table = pltpu.make_async_copy(starts_ref, starts, table_sem)
+    table.start()
     for piece in range(pieces):
         load(piece).start()
+    table.wait()
     complete = 0
     for piece in range(pieces):
         load(piece).wait()
@@ -274,6 +278,10 @@
 
 def near_by(array):
     return pltpu.with_memory_space_constraint(array, pltpu.VMEM)
+
+
+def far_off(array):
+    return pltpu.with_memory_space_constraint(array, pltpu.HBM)
 
 
 def local_call(kernel, outs, scalars, arrays, scratch):
@@ -305,7 +313,8 @@
     query_out = send((0,), planes, groups, channels, QUERY_TURN)
 
     ending = jnp.sum(jnp.where(jnp.arange(groups)[:, None] >= jnp.arange(groups)[None, :], counts[None, :], 0), axis=1)
-    starts = jnp.concatenate([jnp.zeros((1,), jnp.int32), ending]).astype(jnp.int32)
+    starts = jnp.concatenate([jnp.zeros((1,), jnp.int32), ending, jnp.zeros((BLOCK - 1 - groups,), jnp.int32)])
+    starts = starts.astype(jnp.int32)
     bounds = jnp.sum((seg_ids[None, :] < jnp.arange(1, 4, dtype=jnp.int32)[:, None]).astype(jnp.int32), axis=1)
 
     rate = jnp.transpose(rates)
@@ -359,21 +368,23 @@
         (signal, ends, near, far, farther, decay, one_coef, two_coef, four_coef, onward, scale_b, taps_b, span),
         [pltpu.VMEM((modes, SUB, channels), F32)],
     )
-    pieces = 8
+    pieces = PIECES
     return pl.pallas_call(
         functools.partial(mix_kernel, QUERY_TURN),
         out_shape=pltpu.HBM((length, channels), BF16),
-        in_specs=[pl.BlockSpec(memory_space=space) for space in (pltpu.SMEM, pltpu.HBM, pltpu.VMEM)],
+        in_specs=[pl.BlockSpec(memory_space=space) for space in (pltpu.HBM, pltpu.HBM, pltpu.VMEM)],
         out_specs=pl.BlockSpec(memory_space=pltpu.HBM),
         scratch_shapes=[
+            pltpu.SMEM(starts.shape, jnp.int32),
             pltpu.VMEM((groups, capacity, channels), BF16),
             pltpu.VMEM(padded, F32),
             pltpu.VMEM((length, channels), BF16),
+            pltpu.SemaphoreType.DMA,
             pltpu.SemaphoreType.DMA((pieces,)),
             pltpu.SemaphoreType.DMA((blocks,)),
         ],
         compiler_params=pltpu.CompilerParams(vmem_limit_bytes=24 << 20),
-    )(starts, pltpu.with_memory_space_constraint(query_in, pltpu.HBM), near_by(filtered))
+    )(far_off(starts), far_off(query_in), near_by(filtered))
 
 
 def solution(mesh):

time: 74.1 us -> 73.6 us (level)
  transfers between devices with their start and end apart: 5 -> 5, of which waited for: 3 -> 3; matrix products, arithmetic and copies ran while one was open for 1% -> 1% of each run, Pallas kernels for 17% -> 18%
where the time goes in v7:
time: 73.6 us; the launch traced here: 72.2 us
  starting transfers between devices  27.5 us (37%)
  waiting for transfers between devices  24.9 us (34%)
  Pallas kernels  18.5 us (25%)
  other arithmetic  0.98 us (1%)
    all_to_all x2, waiting for transfers between devices, exchange(): lax.all_to_all(value, 'ch', split_axis=0, concat_axis=0, axis_index_group...  23.5 us
    all_to_all x2, starting transfers between devices, exchange(): lax.all_to_all(value, 'ch', split_axis=0, concat_axis=0, axis_index_group...  18.5 us
    pallas_call x2, Pallas kernels, local_call(): pl.pallas_call(kernel, out_shape=outs, in_specs=[pl.BlockSpec(memory_spac...  10.3 us
    ppermute x3, starting transfers between devices, passed_along(): lax.ppermute(value, axis, [(source, source + steps) for source in range(c...  8.97 us
    pallas_call x2, Pallas kernels, send(): pl.pallas_call(functools.partial(send_kernel, planes, turn), out_shape=pl...  5.68 us
    pallas_call x1, Pallas kernels, shards(): pl.pallas_call(functools.partial(mix_kernel, QUERY_TURN), out_shape=pltpu...  2.55 us
    ppermute x3, waiting for transfers between devices, passed_along(): lax.ppermute(value, axis, [(source, source + steps) for source in range(c...  1.49 us
  transfers between devices with their start and end apart: 5, of which 3 were waited for; matrix products, arithmetic and copies ran while one was open for 1% of the time, Pallas kernels for 18%

profile of v7, /device:TPU:0, one launch (start us, length us, event | category | flops | bytes accessed | tf_op | source)
XLA Modules:
  0.0 72.2 jit_solution(2192978605153942529)
XLA Ops:
  0.0 3.2 %shard_map.65 = bf16[32,128,256]{2,1,0:T(8,128)(2,1)} custom-call(bf16[3,128,8192]{2,1,0:T(8,128)(2,1)} %bitcast.12), custom_call_target="tpu_custom_call" | custom-call | tf_op jit(solution)/shard_map/pallas_call | solution.py:59
  3.2 10.2 %all-to-all-start.1 = ((bf16[32,128,256]{2,1,0:T(8,128)(2,1)}), bf16[32,128,256]{2,1,0:T(8,128)(2,1)S(1)}, u32[]{:S(2)}, u32[]{:S(2)}) async-start(bf16[32,128,256]{2,1,0:T(8,128)(2,1)} %shard_map.65), calls=%async_computation.1 | async-start | bytes 4194304 | tf_op jit(solution)/shard_map/all_to_all | solution.py:77
  13.4 0.0 copy-start.5
  13.4 0.0 copy-start.3
  13.4 0.0 copy-start.1
  13.4 0.0 copy-start.2
  13.4 0.0 copy-start.4
  13.5 2.5 %shard_map.64 = bf16[32,128,256]{2,1,0:T(8,128)(2,1)} custom-call(bf16[3,128,8192]{2,1,0:T(8,128)(2,1)} %bitcast.13), custom_call_target="tpu_custom_call" | custom-call | tf_op jit(solution)/shard_map/pallas_call | solution.py:59
  16.0 0.0 copy-done.5
  16.0 0.1 select_reduce_fusion
  16.1 0.1 pad_add_fusion.starts.starts_ref
  16.2 0.0 copy-done.3
  16.2 0.2 convert_reduce_fusion.bounds
  16.4 0.0 copy-done.1
  16.4 0.0 copy-done.2
  16.5 0.1 multiply_reduce_fusion
  16.7 0.1 select_add_fusion
  16.7 0.1 broadcast_select_fusion.2.one_ref
  16.8 0.1 multiply_exponential_fusion
  16.9 0.1 broadcast_select_fusion
  17.1 20.1 %all-to-all-done.1.arrived_ref = bf16[32,128,256]{2,1,0:T(8,128)(2,1)S(1)} async-done(((bf16[32,128,256]{2,1,0:T(8,128)(2,1)}), bf16[32,128,256]{2,1,0:T(8,128)(2,1)S(1)}, u32[]{:S(2)}, u32[]{:S(2)}) %all-to-all-start.1) | async-done | bytes 2097184 | tf_op jit(solution)/shard_map/all_to_all | solution.py:77
  37.2 8.3 %all-to-all-start = ((bf16[32,128,256]{2,1,0:T(8,128)(2,1)}), bf16[32,128,256]{2,1,0:T(8,128)(2,1)}, u32[]{:S(2)}, u32[]{:S(2)}) async-start(bf16[32,128,256]{2,1,0:T(8,128)(2,1)} %shard_map.64), calls=%async_computation | async-start | bytes 4194304 | tf_op jit(solution)/shard_map/all_to_all | solution.py:77
  45.5 4.3 %shard_map.66 = (f32[2,2176,128]{2,1,0:T(8,128)S(1)}, f32[16,16,8,256]{3,2,1,0:T(8,128)S(1)}, f32[24,256]{1,0:T(8,128)S(1)}) custom-call(s32[128]{0:T(128)S(1)} %pad_add_fusion.starts.starts_ref, s32[3]{0:T(128)S(1)} %convert_reduce_fusion.bounds, bf16[32,128,256]{2,1,0:T(8,128)(2,1)S(1)} %all-to-all-done.1.arrived_ref, f32[16,8,256]{2,1,0:T(8,128)S(1)} %mul.138.decay_ref, ...), custom_call_target="tpu_custom_call" | custom-call | tf_op jit(solution)/shard_map/pallas_call | solution.py:289
  49.8 4.9 %collective-permute-start.2 = (f32[24,256]{1,0:T(8,128)S(1)}, f32[24,256]{1,0:T(8,128)S(1)}, u32[]{:S(2)}, u32[]{:S(2)}) collective-permute-start(f32[24,256]{1,0:T(8,128)S(1)} %get-tuple-element.29), channel_id=1, source_target_pairs={{0,96},{1,97},{2,98},{3,99},{4,100},{5,101},{6,102},{7,103},{8,104... | collective-permute-start | bytes 73736 | tf_op jit(solution)/shard_map/ppermute | solution.py:301
  54.7 1.3 %collective-permute-start.1 = (f32[24,256]{1,0:T(8,128)S(1)}, f32[24,256]{1,0:T(8,128)S(1)}, u32[]{:S(2)}, u32[]{:S(2)}) collective-permute-start(f32[24,256]{1,0:T(8,128)S(1)} %get-tuple-element.29), channel_id=1, source_target_pairs={{0,64},{32,96},{1,65},{33,97},{2,66},{34,98},{3,67},{35,99},{4,68}... | collective-permute-start | bytes 73736 | tf_op jit(solution)/shard_map/ppermute | solution.py:301
  56.0 2.8 %collective-permute-start = (f32[24,256]{1,0:T(8,128)S(1)}, f32[24,256]{1,0:T(8,128)S(1)}, u32[]{:S(2)}, u32[]{:S(2)}) collective-permute-start(f32[24,256]{1,0:T(8,128)S(1)} %get-tuple-element.29), channel_id=1, source_target_pairs={{0,32},{32,64},{64,96},{1,33},{33,65},{65,97},{2,34},{34,66},{66,9... | collective-permute-start | bytes 73736 | tf_op jit(solution)/shard_map/ppermute | solution.py:301
  58.8 0.0 collective-permute-done.2.farther_ref
  58.8 0.0 collective-permute-done.1.far_ref
  58.8 1.5 %collective-permute-done.near_ref = f32[24,256]{1,0:T(8,128)S(1)} collective-permute-done((f32[24,256]{1,0:T(8,128)S(1)}, f32[24,256]{1,0:T(8,128)S(1)}, u32[]{:S(2)}, u32[]{:S(2)}) %collective-permute-start) | collective-permute-done | bytes 24608 | tf_op jit(solution)/shard_map/ppermute | solution.py:301
  60.3 6.0 %shard_map.67.filtered_ref = f32[2,2048,128]{2,1,0:T(8,128)S(1)} custom-call(s32[3]{0:T(128)S(1)} %convert_reduce_fusion.bounds, f32[2,2176,128]{2,1,0:T(8,128)S(1)} %get-tuple-element.27.signal_ref, f32[16,16,8,256]{3,2,1,0:T(8,128)S(1)} %get-tuple-element.28.ends_ref, f32[24,256]{1,0:T(8,128)S(1)} %collective-permute-done.near_ref, ...), custom_call_target="tpu_custom_call" | custom-call | tf_op jit(solution)/shard_map/pallas_call | solution.py:289
  66.3 3.4 %all-to-all-done.arrived_ref = bf16[32,128,256]{2,1,0:T(8,128)(2,1)} async-done(((bf16[32,128,256]{2,1,0:T(8,128)(2,1)}), bf16[32,128,256]{2,1,0:T(8,128)(2,1)}, u32[]{:S(2)}, u32[]{:S(2)}) %all-to-all-start) | async-done | bytes 2097184 | tf_op jit(solution)/shard_map/all_to_all | solution.py:77
  69.7 2.5 %shard_map.68 = bf16[2048,256]{1,0:T(8,128)(2,1)} custom-call(s32[128]{0:T(128)} %copy-done, bf16[32,128,256]{2,1,0:T(8,128)(2,1)} %all-to-all-done.arrived_ref, f32[2,2048,128]{2,1,0:T(8,128)S(1)} %shard_map.67.filtered_ref), custom_call_target="tpu_custom_call" | custom-call | tf_op jit(solution)/shard_map/pallas_call | solution.py:372
  (16 shorter events, 0.1 us)
Async XLA Ops:
  3.2 34.0 %all-to-all-start.1 = ((bf16[32,128,256]{2,1,0:T(8,128)(2,1)}), bf16[32,128,256]{2,1,0:T(8,128)(2,1)S(1)}, u32[]{:S(2)}, u32[]{:S(2)}) async-start(bf16[32,128,256]{2,1,0:T(8,128)(2,1)} %shard_map.65), calls=%async_computation.1 | async-start | bytes 4194304 | tf_op jit(solution)/shard_map/all_to_all | solution.py:77
  13.4 2.6 %copy-start.5 = (s32[1,32]{1,0:T(1,128)S(1)}, s32[1,32]{1,0:T(1,128)}, u32[]{:S(2)}) copy-start(s32[1,32]{1,0:T(1,128)} %param.7) | copy-start | bytes 388
  13.4 2.8 %copy-start.3 = (s32[2048]{0:T(1024)S(1)}, s32[2048]{0:T(1024)}, u32[]{:S(2)}) copy-start(s32[2048]{0:T(1024)} %param.8) | copy-start | bytes 24580
  13.4 3.0 %copy-start.1 = (f32[256,16]{0,1:T(8,128)S(1)}, f32[256,16]{0,1:T(8,128)}, u32[]{:S(2)}) copy-start(f32[256,16]{0,1:T(8,128)} %param.9) | copy-start | bytes 49156
  13.4 3.0 %copy-start.2 = (f32[256,16]{0,1:T(8,128)S(1)}, f32[256,16]{0,1:T(8,128)}, u32[]{:S(2)}) copy-start(f32[256,16]{0,1:T(8,128)} %param.10) | copy-start | bytes 49156
  13.4 3.2 %copy-start.4 = (f32[256]{0:T(256)S(1)}, f32[256]{0:T(256)}, u32[]{:S(2)}) copy-start(f32[256]{0:T(256)} %param.11) | copy-start | bytes 3076
  16.2 29.3 %copy-start = (s32[128]{0:T(128)}, s32[128]{0:T(128)S(1)}, u32[]{:S(2)}) copy-start(s32[128]{0:T(128)S(1)} %pad_add_fusion.starts.starts_ref) | copy-start | bytes 1540
  37.2 32.5 %all-to-all-start = ((bf16[32,128,256]{2,1,0:T(8,128)(2,1)}), bf16[32,128,256]{2,1,0:T(8,128)(2,1)}, u32[]{:S(2)}, u32[]{:S(2)}) async-start(bf16[32,128,256]{2,1,0:T(8,128)(2,1)} %shard_map.64), calls=%async_computation | async-start | bytes 4194304 | tf_op jit(solution)/shard_map/all_to_all | solution.py:77
  49.8 9.0 %collective-permute-start.2 = (f32[24,256]{1,0:T(8,128)S(1)}, f32[24,256]{1,0:T(8,128)S(1)}, u32[]{:S(2)}, u32[]{:S(2)}) collective-permute-start(f32[24,256]{1,0:T(8,128)S(1)} %get-tuple-element.29), channel_id=1, source_target_pairs={{0,96},{1,97},{2,98},{3,99},{4,100},{5,101},{6,102},{7,103},{8,104... | collective-permute-start | bytes 73736 | tf_op jit(solution)/shard_map/ppermute | solution.py:301
  54.7 4.1 %collective-permute-start.1 = (f32[24,256]{1,0:T(8,128)S(1)}, f32[24,256]{1,0:T(8,128)S(1)}, u32[]{:S(2)}, u32[]{:S(2)}) collective-permute-start(f32[24,256]{1,0:T(8,128)S(1)} %get-tuple-element.29), channel_id=1, source_target_pairs={{0,64},{32,96},{1,65},{33,97},{2,66},{34,98},{3,67},{35,99},{4,68}... | collective-permute-start | bytes 73736 | tf_op jit(solution)/shard_map/ppermute | solution.py:301
  56.0 4.3 %collective-permute-start = (f32[24,256]{1,0:T(8,128)S(1)}, f32[24,256]{1,0:T(8,128)S(1)}, u32[]{:S(2)}, u32[]{:S(2)}) collective-permute-start(f32[24,256]{1,0:T(8,128)S(1)} %get-tuple-element.29), channel_id=1, source_target_pairs={{0,32},{32,64},{64,96},{1,33},{33,65},{65,97},{2,34},{34,66},{66,9... | collective-permute-start | bytes 73736 | tf_op jit(solution)/shard_map/ppermute | solution.py:301

commit v8 on v7

--- a/solution.py
+++ b/solution.py
@@ -11,20 +11,19 @@
 STEPS = 16
 LANES = 128
 SUB = 8
-SIGNAL_TURN = 12
-QUERY_TURN = 12
+SIGNAL_CHIPS = (10, 11, 12, 13, 14, 15, 0, 1, 2, 3, 4, 5, 6, 7, 8, 9)
+QUERY_CHIPS = (10, 11, 14, 15, 12, 9, 13, 1, 7, 3, 0, 5, 2, 4, 8, 6)
 LOADS = 4
-STORES = 8
-PIECES = 8
 F32 = jnp.float32
 BF16 = jnp.bfloat16
 
 
-def send_kernel(planes, turn, streams_ref, out_ref, *scratch):
+def send_kernel(planes, chips, streams_ref, out_ref, *scratch):
     held, ready, in_sems, out_sems = scratch[:-3], scratch[-3], scratch[-2], scratch[-1]
     groups, _, channels = out_ref.shape
     width = groups * channels // LOADS
-    per = groups // STORES
+    per = groups // len(chips)
+    each = len(chips) // LOADS
 
     def load(plane, piece):
         columns = pl.ds(piece * width, width)
@@ -33,16 +32,16 @@
         )
 
     def store(piece):
-        goes = (piece * per + turn) % groups
-        return pltpu.make_async_copy(ready.at[pl.ds(piece * per, per)], out_ref.at[pl.ds(goes, per)], out_sems.at[piece])
+        goes = pl.ds(chips.index(piece) * per, per)
+        return pltpu.make_async_copy(ready.at[pl.ds(piece * per, per)], out_ref.at[goes], out_sems.at[piece])
 
     for piece in range(LOADS):
         for plane in range(len(planes)):
             load(plane, piece).start()
-    for piece in range(STORES):
-        if piece % (STORES // LOADS) == 0:
+    for piece in range(len(chips)):
+        if piece % each == 0:
             for plane in range(len(planes)):
-                load(plane, piece // (STORES // LOADS)).wait()
+                load(plane, piece // each).wait()
         for part in range(piece * per, (piece + 1) * per):
             columns = pl.ds(part * channels, channels)
             value = held[0][:, columns]
@@ -50,14 +49,14 @@
                 value = value * other[:, columns]
             ready[part] = value
         store(piece).start()
-    for piece in range(STORES):
+    for piece in range(len(chips)):
         store(piece).wait()
 
 
-def send(planes, streams, groups, channels, turn):
+def send(planes, streams, groups, channels, chips):
     rows = streams.shape[1]
     return pl.pallas_call(
-        functools.partial(send_kernel, planes, turn),
+        functools.partial(send_kernel, planes, chips),
         out_shape=pltpu.HBM((groups, rows, channels), BF16),
         in_specs=[pl.BlockSpec(memory_space=pltpu.HBM)],
         out_specs=pl.BlockSpec(memory_space=pltpu.HBM),
@@ -65,32 +64,34 @@
         + [
             pltpu.VMEM((groups, rows, channels), BF16),
             pltpu.SemaphoreType.DMA((len(planes), LOADS)),
-            pltpu.SemaphoreType.DMA((STORES,)),
+            pltpu.SemaphoreType.DMA((len(chips),)),
         ],
         compiler_params=pltpu.CompilerParams(vmem_limit_bytes=24 << 20),
     )(far_off(streams))
 
 
-def exchange(value, turn):
-    groups = value.shape[0]
-    order = [(rank - turn) % groups for rank in range(groups)]
+def exchange(value, chips):
+    per = value.shape[0] // len(chips)
+    order = [chip * per + core for chip in chips for core in range(per)]
     return lax.all_to_all(value, "ch", split_axis=0, concat_axis=0, axis_index_groups=[order], tiled=True)
 
 
-def compact(turn, starts, arrived_ref, into_ref, first, last):
-    sources, rows, channels = arrived_ref.shape
-
-    def place(source, unused):
-        begin = starts[source]
-        slot = lax.rem(source + turn, sources)
-        for part in range(0, rows, 2 * SUB):
-            for tile in range(channels // LANES):
-                piece = arrived_ref[slot, pl.ds(part, 2 * SUB), pl.ds(tile * LANES, LANES)].astype(F32)
-                into_ref[tile, pl.ds(begin + part, SUB), :] = piece[:SUB]
-                into_ref[tile, pl.ds(begin + part + SUB, SUB), :] = piece[SUB:]
-        return unused
-
-    lax.fori_loop(first, last, place, 0)
+def compact(chips, starts, arrived_ref, into_ref, first, last):
+    groups, rows, channels = arrived_ref.shape
+    per = groups // len(chips)
+    for chip in range(first, last):
+        slots = chips.index(chip) * per
+
+        def place(core, unused, chip=chip, slots=slots):
+            begin = starts[chip * per + core]
+            for part in range(0, rows, 2 * SUB):
+                for tile in range(channels // LANES):
+                    piece = arrived_ref[slots + core, pl.ds(part, 2 * SUB), pl.ds(tile * LANES, LANES)].astype(F32)
+                    into_ref[tile, pl.ds(begin + part, SUB), :] = piece[:SUB]
+                    into_ref[tile, pl.ds(begin + part + SUB, SUB), :] = piece[SUB:]
+            return unused
+
+        lax.fori_loop(0, per, place, 0)
 
 
 def segment(position, bounds):
@@ -100,12 +101,12 @@
     return total
 
 
-def scan_kernel(turn, starts, bounds, arrived_ref, decay_ref, weight_ref, leap_ref, signal_ref, ends_ref, passing_ref, carry):
+def scan_kernel(chips, starts, bounds, arrived_ref, decay_ref, weight_ref, leap_ref, signal_ref, ends_ref, passing_ref, carry):
     limits = [bounds[k] for k in range(3)]
     blocks, modes, _, channels = ends_ref.shape
     carry[...] = jnp.zeros_like(carry)
     rank = lax.broadcasted_iota(jnp.int32, (SUB, LANES), 0)
-    compact(turn, starts, arrived_ref, signal_ref, 0, arrived_ref.shape[0])
+    compact(chips, starts, arrived_ref, signal_ref, 0, len(chips))
 
     def one(block, unused):
         begin = block * BLOCK
@@ -239,14 +240,14 @@
     lax.fori_loop(0, blocks, one, 0)
 
 
-def mix_kernel(turn, starts_ref, arrived_ref, filtered_ref, out_ref, starts, landed, held, ready, table_sem, in_sems, out_sems):
+def mix_kernel(chips, starts_ref, arrived_ref, filtered_ref, out_ref, starts, landed, held, ready, table_sem, in_sems, out_sems):
     tiles, length, _ = filtered_ref.shape
     pieces = in_sems.shape[0]
     sources = arrived_ref.shape[0]
     per = sources // pieces
 
     def load(piece):
-        slots = pl.ds((piece * per + turn) % sources, per)
+        slots = pl.ds(chips.index(piece) * per, per)
         return pltpu.make_async_copy(arrived_ref.at[slots], landed.at[slots], in_sems.at[piece])
 
     def store(block):
@@ -268,7 +269,7 @@
     complete = 0
     for piece in range(pieces):
         load(piece).wait()
-        compact(turn, starts, landed, held, piece * per, (piece + 1) * per)
+        compact(chips, starts, landed, held, piece, piece + 1)
         reached = starts[(piece + 1) * per] >> 7
         lax.fori_loop(complete, reached, finish, 0)
         complete = reached
@@ -309,8 +310,8 @@
     blocks = length // BLOCK
     counts = load_counts[0]
     planes = jnp.transpose(streams, (1, 0, 2))
-    signal_in = exchange(send((1, 2), planes, groups, channels, SIGNAL_TURN), SIGNAL_TURN)
-    query_out = send((0,), planes, groups, channels, QUERY_TURN)
+    signal_in = exchange(send((1, 2), planes, groups, channels, SIGNAL_CHIPS), SIGNAL_CHIPS)
+    query_out = send((0,), planes, groups, channels, QUERY_CHIPS)
 
     ending = jnp.sum(jnp.where(jnp.arange(groups)[:, None] >= jnp.arange(groups)[None, :], counts[None, :], 0), axis=1)
     starts = jnp.concatenate([jnp.zeros((1,), jnp.int32), ending, jnp.zeros((BLOCK - 1 - groups,), jnp.int32)])
@@ -343,11 +344,11 @@
     prepared = (starts, bounds, decay, weight, leap, one_coef, two_coef, four_coef, onward, scale_b, taps_b, span)
     query_out, prepared = lax.optimization_barrier((query_out, prepared))
     starts, bounds, decay, weight, leap, one_coef, two_coef, four_coef, onward, scale_b, taps_b, span = prepared
-    query_in = exchange(query_out, QUERY_TURN)
+    query_in = exchange(query_out, QUERY_CHIPS)
 
     padded = (channels // LANES, length + capacity, LANES)
     signal, ends, passing = local_call(
-        functools.partial(scan_kernel, SIGNAL_TURN),
+        functools.partial(scan_kernel, SIGNAL_CHIPS),
         (
             pltpu.VMEM(padded, F32),
             pltpu.VMEM((blocks, modes, SUB, channels), F32),
@@ -368,9 +369,9 @@
         (signal, ends, near, far, farther, decay, one_coef, two_coef, four_coef, onward, scale_b, taps_b, span),
         [pltpu.VMEM((modes, SUB, channels), F32)],
     )
-    pieces = PIECES
+    pieces = len(QUERY_CHIPS)
     return pl.pallas_call(
-        functools.partial(mix_kernel, QUERY_TURN),
+        functools.partial(mix_kernel, QUERY_CHIPS),
         out_shape=pltpu.HBM((length, channels), BF16),
         in_specs=[pl.BlockSpec(memory_space=space) for space in (pltpu.HBM, pltpu.HBM, pltpu.VMEM)],
         out_specs=pl.BlockSpec(memory_space=pltpu.HBM),

time: 73.6 us -> 73.4 us (level)
  transfers between devices with their start and end apart: 5 -> 5, of which waited for: 3 -> 3; matrix products, arithmetic and copies ran while one was open for 1% -> 1% of each run, Pallas kernels for 18% -> 17%
where the time goes in v8:
time: 73.4 us; the launch traced here: 72.7 us
  starting transfers between devices  27.5 us (37%)
  waiting for transfers between devices  25.3 us (34%)
  Pallas kernels  18.6 us (25%)
  other arithmetic  0.98 us (1%)
    all_to_all x2, waiting for transfers between devices, exchange(): lax.all_to_all(value, 'ch', split_axis=0, concat_axis=0, axis_index_group...  23.8 us
    all_to_all x2, starting transfers between devices, exchange(): lax.all_to_all(value, 'ch', split_axis=0, concat_axis=0, axis_index_group...  18.5 us
    pallas_call x2, Pallas kernels, local_call(): pl.pallas_call(kernel, out_shape=outs, in_specs=[pl.BlockSpec(memory_spac...  10.1 us
    ppermute x3, starting transfers between devices, passed_along(): lax.ppermute(value, axis, [(source, source + steps) for source in range(c...  8.97 us
    pallas_call x2, Pallas kernels, send(): pl.pallas_call(functools.partial(send_kernel, planes, chips), out_shape=p...  5.86 us
    pallas_call x1, Pallas kernels, shards(): pl.pallas_call(functools.partial(mix_kernel, QUERY_CHIPS), out_shape=pltp...  2.63 us
    ppermute x3, waiting for transfers between devices, passed_along(): lax.ppermute(value, axis, [(source, source + steps) for source in range(c...  1.49 us
  transfers between devices with their start and end apart: 5, of which 3 were waited for; matrix products, arithmetic and copies ran while one was open for 1% of the time, Pallas kernels for 17%

profile of v8, /device:TPU:0, one launch (start us, length us, event | category | flops | bytes accessed | tf_op | source)
XLA Modules:
  0.0 72.7 jit_solution(8569656648749998009)
XLA Ops:
  0.0 3.3 %shard_map.65 = bf16[32,128,256]{2,1,0:T(8,128)(2,1)} custom-call(bf16[3,128,8192]{2,1,0:T(8,128)(2,1)} %bitcast.12), custom_call_target="tpu_custom_call" | custom-call | tf_op jit(solution)/shard_map/pallas_call | solution.py:58
  3.3 10.2 %all-to-all-start.1 = ((bf16[32,128,256]{2,1,0:T(8,128)(2,1)}), bf16[32,128,256]{2,1,0:T(8,128)(2,1)S(1)}, u32[]{:S(2)}, u32[]{:S(2)}) async-start(bf16[32,128,256]{2,1,0:T(8,128)(2,1)} %shard_map.65), calls=%async_computation.1 | async-start | bytes 4194304 | tf_op jit(solution)/shard_map/all_to_all | solution.py:76
  13.5 0.0 copy-start.5
  13.5 0.0 copy-start.3
  13.5 0.0 copy-start.1
  13.5 0.0 copy-start.2
  13.5 0.0 copy-start.4
  13.6 2.6 %shard_map.64 = bf16[32,128,256]{2,1,0:T(8,128)(2,1)} custom-call(bf16[3,128,8192]{2,1,0:T(8,128)(2,1)} %bitcast.13), custom_call_target="tpu_custom_call" | custom-call | tf_op jit(solution)/shard_map/pallas_call | solution.py:58
  16.2 0.0 copy-done.5
  16.2 0.1 select_reduce_fusion
  16.3 0.1 pad_add_fusion.starts.starts_ref
  16.4 0.0 copy-done.3
  16.4 0.2 convert_reduce_fusion.bounds
  16.7 0.1 multiply_reduce_fusion
  16.8 0.0 copy-done.4
  16.8 0.1 select_add_fusion
  16.9 0.1 broadcast_select_fusion.2.one_ref
  17.0 0.1 multiply_exponential_fusion
  17.1 0.1 broadcast_select_fusion
  17.3 20.0 %all-to-all-done.1.arrived_ref = bf16[32,128,256]{2,1,0:T(8,128)(2,1)S(1)} async-done(((bf16[32,128,256]{2,1,0:T(8,128)(2,1)}), bf16[32,128,256]{2,1,0:T(8,128)(2,1)S(1)}, u32[]{:S(2)}, u32[]{:S(2)}) %all-to-all-start.1) | async-done | bytes 2097184 | tf_op jit(solution)/shard_map/all_to_all | solution.py:76
  37.3 8.3 %all-to-all-start = ((bf16[32,128,256]{2,1,0:T(8,128)(2,1)}), bf16[32,128,256]{2,1,0:T(8,128)(2,1)}, u32[]{:S(2)}, u32[]{:S(2)}) async-start(bf16[32,128,256]{2,1,0:T(8,128)(2,1)} %shard_map.64), calls=%async_computation | async-start | bytes 4194304 | tf_op jit(solution)/shard_map/all_to_all | solution.py:76
  45.6 0.0 copy-done
  45.6 4.2 %shard_map.66 = (f32[2,2176,128]{2,1,0:T(8,128)S(1)}, f32[16,16,8,256]{3,2,1,0:T(8,128)S(1)}, f32[24,256]{1,0:T(8,128)S(1)}) custom-call(s32[128]{0:T(128)S(1)} %pad_add_fusion.starts.starts_ref, s32[3]{0:T(128)S(1)} %convert_reduce_fusion.bounds, bf16[32,128,256]{2,1,0:T(8,128)(2,1)S(1)} %all-to-all-done.1.arrived_ref, f32[16,8,256]{2,1,0:T(8,128)S(1)} %mul.138.decay_ref, ...), custom_call_target="tpu_custom_call" | custom-call | tf_op jit(solution)/shard_map/pallas_call | solution.py:290
  49.8 4.9 %collective-permute-start.2 = (f32[24,256]{1,0:T(8,128)S(1)}, f32[24,256]{1,0:T(8,128)S(1)}, u32[]{:S(2)}, u32[]{:S(2)}) collective-permute-start(f32[24,256]{1,0:T(8,128)S(1)} %get-tuple-element.29), channel_id=1, source_target_pairs={{0,96},{1,97},{2,98},{3,99},{4,100},{5,101},{6,102},{7,103},{8,104... | collective-permute-start | bytes 73736 | tf_op jit(solution)/shard_map/ppermute | solution.py:302
  54.8 1.3 %collective-permute-start.1 = (f32[24,256]{1,0:T(8,128)S(1)}, f32[24,256]{1,0:T(8,128)S(1)}, u32[]{:S(2)}, u32[]{:S(2)}) collective-permute-start(f32[24,256]{1,0:T(8,128)S(1)} %get-tuple-element.29), channel_id=1, source_target_pairs={{0,64},{32,96},{1,65},{33,97},{2,66},{34,98},{3,67},{35,99},{4,68}... | collective-permute-start | bytes 73736 | tf_op jit(solution)/shard_map/ppermute | solution.py:302
  56.1 2.8 %collective-permute-start = (f32[24,256]{1,0:T(8,128)S(1)}, f32[24,256]{1,0:T(8,128)S(1)}, u32[]{:S(2)}, u32[]{:S(2)}) collective-permute-start(f32[24,256]{1,0:T(8,128)S(1)} %get-tuple-element.29), channel_id=1, source_target_pairs={{0,32},{32,64},{64,96},{1,33},{33,65},{65,97},{2,34},{34,66},{66,9... | collective-permute-start | bytes 73736 | tf_op jit(solution)/shard_map/ppermute | solution.py:302
  58.8 0.0 collective-permute-done.2.farther_ref
  58.9 0.0 collective-permute-done.1.far_ref
  58.9 1.5 %collective-permute-done.near_ref = f32[24,256]{1,0:T(8,128)S(1)} collective-permute-done((f32[24,256]{1,0:T(8,128)S(1)}, f32[24,256]{1,0:T(8,128)S(1)}, u32[]{:S(2)}, u32[]{:S(2)}) %collective-permute-start) | collective-permute-done | bytes 24608 | tf_op jit(solution)/shard_map/ppermute | solution.py:302
  60.3 5.8 %shard_map.67.filtered_ref = f32[2,2048,128]{2,1,0:T(8,128)S(1)} custom-call(s32[3]{0:T(128)S(1)} %convert_reduce_fusion.bounds, f32[2,2176,128]{2,1,0:T(8,128)S(1)} %get-tuple-element.27.signal_ref, f32[16,16,8,256]{3,2,1,0:T(8,128)S(1)} %get-tuple-element.28.ends_ref, f32[24,256]{1,0:T(8,128)S(1)} %collective-permute-done.near_ref, ...), custom_call_target="tpu_custom_call" | custom-call | tf_op jit(solution)/shard_map/pallas_call | solution.py:290
  66.2 3.8 %all-to-all-done.arrived_ref = bf16[32,128,256]{2,1,0:T(8,128)(2,1)} async-done(((bf16[32,128,256]{2,1,0:T(8,128)(2,1)}), bf16[32,128,256]{2,1,0:T(8,128)(2,1)}, u32[]{:S(2)}, u32[]{:S(2)}) %all-to-all-start) | async-done | bytes 2097184 | tf_op jit(solution)/shard_map/all_to_all | solution.py:76
  70.0 2.6 %shard_map.68 = bf16[2048,256]{1,0:T(8,128)(2,1)} custom-call(s32[128]{0:T(128)} %copy-done, bf16[32,128,256]{2,1,0:T(8,128)(2,1)} %all-to-all-done.arrived_ref, f32[2,2048,128]{2,1,0:T(8,128)S(1)} %shard_map.67.filtered_ref), custom_call_target="tpu_custom_call" | custom-call | tf_op jit(solution)/shard_map/pallas_call | solution.py:373
  (16 shorter events, 0.1 us)
Async XLA Ops:
  3.3 34.0 %all-to-all-start.1 = ((bf16[32,128,256]{2,1,0:T(8,128)(2,1)}), bf16[32,128,256]{2,1,0:T(8,128)(2,1)S(1)}, u32[]{:S(2)}, u32[]{:S(2)}) async-start(bf16[32,128,256]{2,1,0:T(8,128)(2,1)} %shard_map.65), calls=%async_computation.1 | async-start | bytes 4194304 | tf_op jit(solution)/shard_map/all_to_all | solution.py:76
  13.5 2.7 %copy-start.5 = (s32[1,32]{1,0:T(1,128)S(1)}, s32[1,32]{1,0:T(1,128)}, u32[]{:S(2)}) copy-start(s32[1,32]{1,0:T(1,128)} %param.7) | copy-start | bytes 388
  13.5 2.9 %copy-start.3 = (s32[2048]{0:T(1024)S(1)}, s32[2048]{0:T(1024)}, u32[]{:S(2)}) copy-start(s32[2048]{0:T(1024)} %param.8) | copy-start | bytes 24580
  13.5 3.1 %copy-start.1 = (f32[256,16]{0,1:T(8,128)S(1)}, f32[256,16]{0,1:T(8,128)}, u32[]{:S(2)}) copy-start(f32[256,16]{0,1:T(8,128)} %param.9) | copy-start | bytes 49156
  13.5 3.1 %copy-start.2 = (f32[256,16]{0,1:T(8,128)S(1)}, f32[256,16]{0,1:T(8,128)}, u32[]{:S(2)}) copy-start(f32[256,16]{0,1:T(8,128)} %param.10) | copy-start | bytes 49156
  13.5 3.3 %copy-start.4 = (f32[256]{0:T(256)S(1)}, f32[256]{0:T(256)}, u32[]{:S(2)}) copy-start(f32[256]{0:T(256)} %param.11) | copy-start | bytes 3076
  16.4 29.2 %copy-start = (s32[128]{0:T(128)}, s32[128]{0:T(128)S(1)}, u32[]{:S(2)}) copy-start(s32[128]{0:T(128)S(1)} %pad_add_fusion.starts.starts_ref) | copy-start | bytes 1540
  37.3 32.8 %all-to-all-start = ((bf16[32,128,256]{2,1,0:T(8,128)(2,1)}), bf16[32,128,256]{2,1,0:T(8,128)(2,1)}, u32[]{:S(2)}, u32[]{:S(2)}) async-start(bf16[32,128,256]{2,1,0:T(8,128)(2,1)} %shard_map.64), calls=%async_computation | async-start | bytes 4194304 | tf_op jit(solution)/shard_map/all_to_all | solution.py:76
  49.8 9.0 %collective-permute-start.2 = (f32[24,256]{1,0:T(8,128)S(1)}, f32[24,256]{1,0:T(8,128)S(1)}, u32[]{:S(2)}, u32[]{:S(2)}) collective-permute-start(f32[24,256]{1,0:T(8,128)S(1)} %get-tuple-element.29), channel_id=1, source_target_pairs={{0,96},{1,97},{2,98},{3,99},{4,100},{5,101},{6,102},{7,103},{8,104... | collective-permute-start | bytes 73736 | tf_op jit(solution)/shard_map/ppermute | solution.py:302
  54.8 4.1 %collective-permute-start.1 = (f32[24,256]{1,0:T(8,128)S(1)}, f32[24,256]{1,0:T(8,128)S(1)}, u32[]{:S(2)}, u32[]{:S(2)}) collective-permute-start(f32[24,256]{1,0:T(8,128)S(1)} %get-tuple-element.29), channel_id=1, source_target_pairs={{0,64},{32,96},{1,65},{33,97},{2,66},{34,98},{3,67},{35,99},{4,68}... | collective-permute-start | bytes 73736 | tf_op jit(solution)/shard_map/ppermute | solution.py:302
  56.1 4.3 %collective-permute-start = (f32[24,256]{1,0:T(8,128)S(1)}, f32[24,256]{1,0:T(8,128)S(1)}, u32[]{:S(2)}, u32[]{:S(2)}) collective-permute-start(f32[24,256]{1,0:T(8,128)S(1)} %get-tuple-element.29), channel_id=1, source_target_pairs={{0,32},{32,64},{64,96},{1,33},{33,65},{65,97},{2,34},{34,66},{66,9... | collective-permute-start | bytes 73736 | tf_op jit(solution)/shard_map/ppermute | solution.py:302

commit v9 on v8

--- a/solution.py
+++ b/solution.py
@@ -31,9 +31,15 @@
             streams_ref.at[planes[plane], :, columns], held[plane].at[:, columns], in_sems.at[plane, piece]
         )
 
-    def store(piece):
-        goes = pl.ds(chips.index(piece) * per, per)
-        return pltpu.make_async_copy(ready.at[pl.ds(piece * per, per)], out_ref.at[goes], out_sems.at[piece])
+    runs = []
+    for piece in range(len(chips)):
+        joined = piece % 2 == 1 and chips.index(piece) == chips.index(piece - 1) + 1
+        runs = runs[:-1] + [(piece - 1, 2)] if joined else runs + [(piece, 1)]
+
+    def store(run):
+        piece, count = runs[run]
+        goes = pl.ds(chips.index(piece) * per, count * per)
+        return pltpu.make_async_copy(ready.at[pl.ds(piece * per, count * per)], out_ref.at[goes], out_sems.at[run])
 
     for piece in range(LOADS):
         for plane in range(len(planes)):
@@ -48,9 +54,11 @@
             for other in held[1:]:
                 value = value * other[:, columns]
             ready[part] = value
-        store(piece).start()
-    for piece in range(len(chips)):
-        store(piece).wait()
+        for run, (begin, count) in enumerate(runs):
+            if begin + count == piece + 1:
+                store(run).start()
+    for run in range(len(runs)):
+        store(run).wait()
 
 
 def send(planes, streams, groups, channels, chips):

time: 73.4 us -> 73.4 us (level)
  transfers between devices with their start and end apart: 5 -> 5, of which waited for: 3 -> 3; matrix products, arithmetic and copies ran while one was open for 1% -> 1% of each run, Pallas kernels for 17% -> 18%
where the time goes in v9:
time: 73.4 us; the launch traced here: 72.6 us
  starting transfers between devices  27.5 us (37%)
  waiting for transfers between devices  25.2 us (34%)
  Pallas kernels  18.7 us (25%)
  other arithmetic  0.98 us (1%)
    all_to_all x2, waiting for transfers between devices, exchange(): lax.all_to_all(value, 'ch', split_axis=0, concat_axis=0, axis_index_group...  23.7 us
    all_to_all x2, starting transfers between devices, exchange(): lax.all_to_all(value, 'ch', split_axis=0, concat_axis=0, axis_index_group...  18.5 us
    pallas_call x2, Pallas kernels, local_call(): pl.pallas_call(kernel, out_shape=outs, in_specs=[pl.BlockSpec(memory_spac...  10.2 us
    ppermute x3, starting transfers between devices, passed_along(): lax.ppermute(value, axis, [(source, source + steps) for source in range(c...  8.97 us
    pallas_call x2, Pallas kernels, send(): pl.pallas_call(functools.partial(send_kernel, planes, chips), out_shape=p...  5.83 us
    pallas_call x1, Pallas kernels, shards(): pl.pallas_call(functools.partial(mix_kernel, QUERY_CHIPS), out_shape=pltp...  2.63 us
    ppermute x3, waiting for transfers between devices, passed_along(): lax.ppermute(value, axis, [(source, source + steps) for source in range(c...  1.49 us
  transfers between devices with their start and end apart: 5, of which 3 were waited for; matrix products, arithmetic and copies ran while one was open for 1% of the time, Pallas kernels for 18%

profile of v9, /device:TPU:0, one launch (start us, length us, event | category | flops | bytes accessed | tf_op | source)
XLA Modules:
  0.0 72.6 jit_solution(15634427869993680993)
XLA Ops:
  0.0 3.2 %shard_map.65 = bf16[32,128,256]{2,1,0:T(8,128)(2,1)} custom-call(bf16[3,128,8192]{2,1,0:T(8,128)(2,1)} %bitcast.12), custom_call_target="tpu_custom_call" | custom-call | tf_op jit(solution)/shard_map/pallas_call | solution.py:66
  3.2 10.2 %all-to-all-start.1 = ((bf16[32,128,256]{2,1,0:T(8,128)(2,1)}), bf16[32,128,256]{2,1,0:T(8,128)(2,1)S(1)}, u32[]{:S(2)}, u32[]{:S(2)}) async-start(bf16[32,128,256]{2,1,0:T(8,128)(2,1)} %shard_map.65), calls=%async_computation.1 | async-start | bytes 4194304 | tf_op jit(solution)/shard_map/all_to_all | solution.py:84
  13.5 0.0 copy-start.5
  13.5 0.0 copy-start.3
  13.5 0.0 copy-start.1
  13.5 0.0 copy-start.2
  13.5 0.0 copy-start.4
  13.5 2.6 %shard_map.64 = bf16[32,128,256]{2,1,0:T(8,128)(2,1)} custom-call(bf16[3,128,8192]{2,1,0:T(8,128)(2,1)} %bitcast.13), custom_call_target="tpu_custom_call" | custom-call | tf_op jit(solution)/shard_map/pallas_call | solution.py:66
  16.2 0.0 copy-done.5
  16.2 0.1 select_reduce_fusion
  16.3 0.1 pad_add_fusion.starts.starts_ref
  16.4 0.0 copy-done.3
  16.4 0.2 convert_reduce_fusion.bounds
  16.6 0.0 copy-done.1
  16.6 0.0 copy-done.2
  16.6 0.1 multiply_reduce_fusion
  16.8 0.1 select_add_fusion
  16.9 0.1 broadcast_select_fusion.2.one_ref
  17.0 0.1 multiply_exponential_fusion
  17.1 0.1 broadcast_select_fusion
  17.2 20.0 %all-to-all-done.1.arrived_ref = bf16[32,128,256]{2,1,0:T(8,128)(2,1)S(1)} async-done(((bf16[32,128,256]{2,1,0:T(8,128)(2,1)}), bf16[32,128,256]{2,1,0:T(8,128)(2,1)S(1)}, u32[]{:S(2)}, u32[]{:S(2)}) %all-to-all-start.1) | async-done | bytes 2097184 | tf_op jit(solution)/shard_map/all_to_all | solution.py:84
  37.2 8.3 %all-to-all-start = ((bf16[32,128,256]{2,1,0:T(8,128)(2,1)}), bf16[32,128,256]{2,1,0:T(8,128)(2,1)}, u32[]{:S(2)}, u32[]{:S(2)}) async-start(bf16[32,128,256]{2,1,0:T(8,128)(2,1)} %shard_map.64), calls=%async_computation | async-start | bytes 4194304 | tf_op jit(solution)/shard_map/all_to_all | solution.py:84
  45.6 4.2 %shard_map.66 = (f32[2,2176,128]{2,1,0:T(8,128)S(1)}, f32[16,16,8,256]{3,2,1,0:T(8,128)S(1)}, f32[24,256]{1,0:T(8,128)S(1)}) custom-call(s32[128]{0:T(128)S(1)} %pad_add_fusion.starts.starts_ref, s32[3]{0:T(128)S(1)} %convert_reduce_fusion.bounds, bf16[32,128,256]{2,1,0:T(8,128)(2,1)S(1)} %all-to-all-done.1.arrived_ref, f32[16,8,256]{2,1,0:T(8,128)S(1)} %mul.138.decay_ref, ...), custom_call_target="tpu_custom_call" | custom-call | tf_op jit(solution)/shard_map/pallas_call | solution.py:298
  49.8 4.9 %collective-permute-start.2 = (f32[24,256]{1,0:T(8,128)S(1)}, f32[24,256]{1,0:T(8,128)S(1)}, u32[]{:S(2)}, u32[]{:S(2)}) collective-permute-start(f32[24,256]{1,0:T(8,128)S(1)} %get-tuple-element.29), channel_id=1, source_target_pairs={{0,96},{1,97},{2,98},{3,99},{4,100},{5,101},{6,102},{7,103},{8,104... | collective-permute-start | bytes 73736 | tf_op jit(solution)/shard_map/ppermute | solution.py:310
  54.8 1.3 %collective-permute-start.1 = (f32[24,256]{1,0:T(8,128)S(1)}, f32[24,256]{1,0:T(8,128)S(1)}, u32[]{:S(2)}, u32[]{:S(2)}) collective-permute-start(f32[24,256]{1,0:T(8,128)S(1)} %get-tuple-element.29), channel_id=1, source_target_pairs={{0,64},{32,96},{1,65},{33,97},{2,66},{34,98},{3,67},{35,99},{4,68}... | collective-permute-start | bytes 73736 | tf_op jit(solution)/shard_map/ppermute | solution.py:310
  56.1 2.8 %collective-permute-start = (f32[24,256]{1,0:T(8,128)S(1)}, f32[24,256]{1,0:T(8,128)S(1)}, u32[]{:S(2)}, u32[]{:S(2)}) collective-permute-start(f32[24,256]{1,0:T(8,128)S(1)} %get-tuple-element.29), channel_id=1, source_target_pairs={{0,32},{32,64},{64,96},{1,33},{33,65},{65,97},{2,34},{34,66},{66,9... | collective-permute-start | bytes 73736 | tf_op jit(solution)/shard_map/ppermute | solution.py:310
  58.8 0.0 collective-permute-done.2.farther_ref
  58.8 0.0 collective-permute-done.1.far_ref
  58.9 1.5 %collective-permute-done.near_ref = f32[24,256]{1,0:T(8,128)S(1)} collective-permute-done((f32[24,256]{1,0:T(8,128)S(1)}, f32[24,256]{1,0:T(8,128)S(1)}, u32[]{:S(2)}, u32[]{:S(2)}) %collective-permute-start) | collective-permute-done | bytes 24608 | tf_op jit(solution)/shard_map/ppermute | solution.py:310
  60.3 6.0 %shard_map.67.filtered_ref = f32[2,2048,128]{2,1,0:T(8,128)S(1)} custom-call(s32[3]{0:T(128)S(1)} %convert_reduce_fusion.bounds, f32[2,2176,128]{2,1,0:T(8,128)S(1)} %get-tuple-element.27.signal_ref, f32[16,16,8,256]{3,2,1,0:T(8,128)S(1)} %get-tuple-element.28.ends_ref, f32[24,256]{1,0:T(8,128)S(1)} %collective-permute-done.near_ref, ...), custom_call_target="tpu_custom_call" | custom-call | tf_op jit(solution)/shard_map/pallas_call | solution.py:298
  66.3 3.7 %all-to-all-done.arrived_ref = bf16[32,128,256]{2,1,0:T(8,128)(2,1)} async-done(((bf16[32,128,256]{2,1,0:T(8,128)(2,1)}), bf16[32,128,256]{2,1,0:T(8,128)(2,1)}, u32[]{:S(2)}, u32[]{:S(2)}) %all-to-all-start) | async-done | bytes 2097184 | tf_op jit(solution)/shard_map/all_to_all | solution.py:84
  70.0 2.6 %shard_map.68 = bf16[2048,256]{1,0:T(8,128)(2,1)} custom-call(s32[128]{0:T(128)} %copy-done, bf16[32,128,256]{2,1,0:T(8,128)(2,1)} %all-to-all-done.arrived_ref, f32[2,2048,128]{2,1,0:T(8,128)S(1)} %shard_map.67.filtered_ref), custom_call_target="tpu_custom_call" | custom-call | tf_op jit(solution)/shard_map/pallas_call | solution.py:381
  (16 shorter events, 0.1 us)
Async XLA Ops:
  3.2 34.0 %all-to-all-start.1 = ((bf16[32,128,256]{2,1,0:T(8,128)(2,1)}), bf16[32,128,256]{2,1,0:T(8,128)(2,1)S(1)}, u32[]{:S(2)}, u32[]{:S(2)}) async-start(bf16[32,128,256]{2,1,0:T(8,128)(2,1)} %shard_map.65), calls=%async_computation.1 | async-start | bytes 4194304 | tf_op jit(solution)/shard_map/all_to_all | solution.py:84
  13.5 2.7 %copy-start.5 = (s32[1,32]{1,0:T(1,128)S(1)}, s32[1,32]{1,0:T(1,128)}, u32[]{:S(2)}) copy-start(s32[1,32]{1,0:T(1,128)} %param.7) | copy-start | bytes 388
  13.5 2.9 %copy-start.3 = (s32[2048]{0:T(1024)S(1)}, s32[2048]{0:T(1024)}, u32[]{:S(2)}) copy-start(s32[2048]{0:T(1024)} %param.8) | copy-start | bytes 24580
  13.5 3.1 %copy-start.1 = (f32[256,16]{0,1:T(8,128)S(1)}, f32[256,16]{0,1:T(8,128)}, u32[]{:S(2)}) copy-start(f32[256,16]{0,1:T(8,128)} %param.9) | copy-start | bytes 49156
  13.5 3.1 %copy-start.2 = (f32[256,16]{0,1:T(8,128)S(1)}, f32[256,16]{0,1:T(8,128)}, u32[]{:S(2)}) copy-start(f32[256,16]{0,1:T(8,128)} %param.10) | copy-start | bytes 49156
  13.5 3.3 %copy-start.4 = (f32[256]{0:T(256)S(1)}, f32[256]{0:T(256)}, u32[]{:S(2)}) copy-start(f32[256]{0:T(256)} %param.11) | copy-start | bytes 3076
  16.4 29.2 %copy-start = (s32[128]{0:T(128)}, s32[128]{0:T(128)S(1)}, u32[]{:S(2)}) copy-start(s32[128]{0:T(128)S(1)} %pad_add_fusion.starts.starts_ref) | copy-start | bytes 1540
  37.2 32.8 %all-to-all-start = ((bf16[32,128,256]{2,1,0:T(8,128)(2,1)}), bf16[32,128,256]{2,1,0:T(8,128)(2,1)}, u32[]{:S(2)}, u32[]{:S(2)}) async-start(bf16[32,128,256]{2,1,0:T(8,128)(2,1)} %shard_map.64), calls=%async_computation | async-start | bytes 4194304 | tf_op jit(solution)/shard_map/all_to_all | solution.py:84
  49.8 9.0 %collective-permute-start.2 = (f32[24,256]{1,0:T(8,128)S(1)}, f32[24,256]{1,0:T(8,128)S(1)}, u32[]{:S(2)}, u32[]{:S(2)}) collective-permute-start(f32[24,256]{1,0:T(8,128)S(1)} %get-tuple-element.29), channel_id=1, source_target_pairs={{0,96},{1,97},{2,98},{3,99},{4,100},{5,101},{6,102},{7,103},{8,104... | collective-permute-start | bytes 73736 | tf_op jit(solution)/shard_map/ppermute | solution.py:310
  54.8 4.1 %collective-permute-start.1 = (f32[24,256]{1,0:T(8,128)S(1)}, f32[24,256]{1,0:T(8,128)S(1)}, u32[]{:S(2)}, u32[]{:S(2)}) collective-permute-start(f32[24,256]{1,0:T(8,128)S(1)} %get-tuple-element.29), channel_id=1, source_target_pairs={{0,64},{32,96},{1,65},{33,97},{2,66},{34,98},{3,67},{35,99},{4,68}... | collective-permute-start | bytes 73736 | tf_op jit(solution)/shard_map/ppermute | solution.py:310
  56.1 4.3 %collective-permute-start = (f32[24,256]{1,0:T(8,128)S(1)}, f32[24,256]{1,0:T(8,128)S(1)}, u32[]{:S(2)}, u32[]{:S(2)}) collective-permute-start(f32[24,256]{1,0:T(8,128)S(1)} %get-tuple-element.29), channel_id=1, source_target_pairs={{0,32},{32,64},{64,96},{1,33},{33,65},{65,97},{2,34},{34,66},{66,9... | collective-permute-start | bytes 73736 | tf_op jit(solution)/shard_map/ppermute | solution.py:310

commit v10 on v9

--- a/solution.py
+++ b/solution.py
@@ -255,7 +255,8 @@
     per = sources // pieces
 
     def load(piece):
-        slots = pl.ds(chips.index(piece) * per, per)
+        joined = piece + 1 < pieces and piece % 2 == 0 and chips.index(piece + 1) == chips.index(piece) + 1
+        slots = pl.ds(chips.index(piece) * per, per * (2 if joined else 1))
         return pltpu.make_async_copy(arrived_ref.at[slots], landed.at[slots], in_sems.at[piece])
 
     def store(block):
@@ -271,12 +272,14 @@
 
     table = pltpu.make_async_copy(starts_ref, starts, table_sem)
     table.start()
-    for piece in range(pieces):
+    heads = [p for p in range(pieces) if p % 2 == 0 or chips.index(p) != chips.index(p - 1) + 1]
+    for piece in heads:
         load(piece).start()
     table.wait()
     complete = 0
     for piece in range(pieces):
-        load(piece).wait()
+        if piece in heads:
+            load(piece).wait()
         compact(chips, starts, landed, held, piece, piece + 1)
         reached = starts[(piece + 1) * per] >> 7
         lax.fori_loop(complete, reached, finish, 0)

time: 73.4 us -> 73.4 us (level)
  no operation moved by 1% of the time
where the time goes in v10:
time: 73.4 us; the launch traced here: 72.7 us
  starting transfers between devices  27.5 us (37%)
  waiting for transfers between devices  25.2 us (34%)
  Pallas kernels  18.7 us (25%)
  other arithmetic  0.98 us (1%)
    all_to_all x2, waiting for transfers between devices, exchange(): lax.all_to_all(value, 'ch', split_axis=0, concat_axis=0, axis_index_group...  23.7 us
    all_to_all x2, starting transfers between devices, exchange(): lax.all_to_all(value, 'ch', split_axis=0, concat_axis=0, axis_index_group...  18.5 us
    pallas_call x2, Pallas kernels, local_call(): pl.pallas_call(kernel, out_shape=outs, in_specs=[pl.BlockSpec(memory_spac...  10.2 us
    ppermute x3, starting transfers between devices, passed_along(): lax.ppermute(value, axis, [(source, source + steps) for source in range(c...  8.97 us
    pallas_call x2, Pallas kernels, send(): pl.pallas_call(functools.partial(send_kernel, planes, chips), out_shape=p...  5.83 us
    pallas_call x1, Pallas kernels, shards(): pl.pallas_call(functools.partial(mix_kernel, QUERY_CHIPS), out_shape=pltp...  2.64 us
    ppermute x3, waiting for transfers between devices, passed_along(): lax.ppermute(value, axis, [(source, source + steps) for source in range(c...  1.49 us
  transfers between devices with their start and end apart: 5, of which 3 were waited for; matrix products, arithmetic and copies ran while one was open for 1% of the time, Pallas kernels for 18%

profile of v10, /device:TPU:0, one launch (start us, length us, event | category | flops | bytes accessed | tf_op | source)
XLA Modules:
  0.0 72.7 jit_solution(11267860450940918997)
XLA Ops:
  0.0 3.2 %shard_map.65 = bf16[32,128,256]{2,1,0:T(8,128)(2,1)} custom-call(bf16[3,128,8192]{2,1,0:T(8,128)(2,1)} %bitcast.12), custom_call_target="tpu_custom_call" | custom-call | tf_op jit(solution)/shard_map/pallas_call | solution.py:66
  3.2 10.2 %all-to-all-start.1 = ((bf16[32,128,256]{2,1,0:T(8,128)(2,1)}), bf16[32,128,256]{2,1,0:T(8,128)(2,1)S(1)}, u32[]{:S(2)}, u32[]{:S(2)}) async-start(bf16[32,128,256]{2,1,0:T(8,128)(2,1)} %shard_map.65), calls=%async_computation.1 | async-start | bytes 4194304 | tf_op jit(solution)/shard_map/all_to_all | solution.py:84
  13.5 0.0 copy-start.5
  13.5 0.0 copy-start.3
  13.5 0.0 copy-start.1
  13.5 0.0 copy-start.2
  13.5 0.0 copy-start.4
  13.5 2.6 %shard_map.64 = bf16[32,128,256]{2,1,0:T(8,128)(2,1)} custom-call(bf16[3,128,8192]{2,1,0:T(8,128)(2,1)} %bitcast.13), custom_call_target="tpu_custom_call" | custom-call | tf_op jit(solution)/shard_map/pallas_call | solution.py:66
  16.2 0.0 copy-done.5
  16.2 0.1 select_reduce_fusion
  16.3 0.1 pad_add_fusion.starts.starts_ref
  16.4 0.0 copy-done.3
  16.4 0.2 convert_reduce_fusion.bounds
  16.6 0.0 copy-done.1
  16.6 0.0 copy-done.2
  16.6 0.1 multiply_reduce_fusion
  16.8 0.1 select_add_fusion
  16.9 0.1 broadcast_select_fusion.2.one_ref
  17.0 0.1 multiply_exponential_fusion
  17.1 0.1 broadcast_select_fusion
  17.2 20.0 %all-to-all-done.1.arrived_ref = bf16[32,128,256]{2,1,0:T(8,128)(2,1)S(1)} async-done(((bf16[32,128,256]{2,1,0:T(8,128)(2,1)}), bf16[32,128,256]{2,1,0:T(8,128)(2,1)S(1)}, u32[]{:S(2)}, u32[]{:S(2)}) %all-to-all-start.1) | async-done | bytes 2097184 | tf_op jit(solution)/shard_map/all_to_all | solution.py:84
  37.2 8.3 %all-to-all-start = ((bf16[32,128,256]{2,1,0:T(8,128)(2,1)}), bf16[32,128,256]{2,1,0:T(8,128)(2,1)}, u32[]{:S(2)}, u32[]{:S(2)}) async-start(bf16[32,128,256]{2,1,0:T(8,128)(2,1)} %shard_map.64), calls=%async_computation | async-start | bytes 4194304 | tf_op jit(solution)/shard_map/all_to_all | solution.py:84
  45.6 4.2 %shard_map.66 = (f32[2,2176,128]{2,1,0:T(8,128)S(1)}, f32[16,16,8,256]{3,2,1,0:T(8,128)S(1)}, f32[24,256]{1,0:T(8,128)S(1)}) custom-call(s32[128]{0:T(128)S(1)} %pad_add_fusion.starts.starts_ref, s32[3]{0:T(128)S(1)} %convert_reduce_fusion.bounds, bf16[32,128,256]{2,1,0:T(8,128)(2,1)S(1)} %all-to-all-done.1.arrived_ref, f32[16,8,256]{2,1,0:T(8,128)S(1)} %mul.138.decay_ref, ...), custom_call_target="tpu_custom_call" | custom-call | tf_op jit(solution)/shard_map/pallas_call | solution.py:301
  49.8 4.9 %collective-permute-start.2 = (f32[24,256]{1,0:T(8,128)S(1)}, f32[24,256]{1,0:T(8,128)S(1)}, u32[]{:S(2)}, u32[]{:S(2)}) collective-permute-start(f32[24,256]{1,0:T(8,128)S(1)} %get-tuple-element.29), channel_id=1, source_target_pairs={{0,96},{1,97},{2,98},{3,99},{4,100},{5,101},{6,102},{7,103},{8,104... | collective-permute-start | bytes 73736 | tf_op jit(solution)/shard_map/ppermute | solution.py:313
  54.8 1.3 %collective-permute-start.1 = (f32[24,256]{1,0:T(8,128)S(1)}, f32[24,256]{1,0:T(8,128)S(1)}, u32[]{:S(2)}, u32[]{:S(2)}) collective-permute-start(f32[24,256]{1,0:T(8,128)S(1)} %get-tuple-element.29), channel_id=1, source_target_pairs={{0,64},{32,96},{1,65},{33,97},{2,66},{34,98},{3,67},{35,99},{4,68}... | collective-permute-start | bytes 73736 | tf_op jit(solution)/shard_map/ppermute | solution.py:313
  56.1 2.8 %collective-permute-start = (f32[24,256]{1,0:T(8,128)S(1)}, f32[24,256]{1,0:T(8,128)S(1)}, u32[]{:S(2)}, u32[]{:S(2)}) collective-permute-start(f32[24,256]{1,0:T(8,128)S(1)} %get-tuple-element.29), channel_id=1, source_target_pairs={{0,32},{32,64},{64,96},{1,33},{33,65},{65,97},{2,34},{34,66},{66,9... | collective-permute-start | bytes 73736 | tf_op jit(solution)/shard_map/ppermute | solution.py:313
  58.8 0.0 collective-permute-done.2.farther_ref
  58.8 0.0 collective-permute-done.1.far_ref
  58.9 1.5 %collective-permute-done.near_ref = f32[24,256]{1,0:T(8,128)S(1)} collective-permute-done((f32[24,256]{1,0:T(8,128)S(1)}, f32[24,256]{1,0:T(8,128)S(1)}, u32[]{:S(2)}, u32[]{:S(2)}) %collective-permute-start) | collective-permute-done | bytes 24608 | tf_op jit(solution)/shard_map/ppermute | solution.py:313
  60.3 6.0 %shard_map.67.filtered_ref = f32[2,2048,128]{2,1,0:T(8,128)S(1)} custom-call(s32[3]{0:T(128)S(1)} %convert_reduce_fusion.bounds, f32[2,2176,128]{2,1,0:T(8,128)S(1)} %get-tuple-element.27.signal_ref, f32[16,16,8,256]{3,2,1,0:T(8,128)S(1)} %get-tuple-element.28.ends_ref, f32[24,256]{1,0:T(8,128)S(1)} %collective-permute-done.near_ref, ...), custom_call_target="tpu_custom_call" | custom-call | tf_op jit(solution)/shard_map/pallas_call | solution.py:301
  66.3 3.7 %all-to-all-done.arrived_ref = bf16[32,128,256]{2,1,0:T(8,128)(2,1)} async-done(((bf16[32,128,256]{2,1,0:T(8,128)(2,1)}), bf16[32,128,256]{2,1,0:T(8,128)(2,1)}, u32[]{:S(2)}, u32[]{:S(2)}) %all-to-all-start) | async-done | bytes 2097184 | tf_op jit(solution)/shard_map/all_to_all | solution.py:84
  70.0 2.6 %shard_map.68 = bf16[2048,256]{1,0:T(8,128)(2,1)} custom-call(s32[128]{0:T(128)} %copy-done, bf16[32,128,256]{2,1,0:T(8,128)(2,1)} %all-to-all-done.arrived_ref, f32[2,2048,128]{2,1,0:T(8,128)S(1)} %shard_map.67.filtered_ref), custom_call_target="tpu_custom_call" | custom-call | tf_op jit(solution)/shard_map/pallas_call | solution.py:384
  (16 shorter events, 0.1 us)
Async XLA Ops:
  3.2 34.0 %all-to-all-start.1 = ((bf16[32,128,256]{2,1,0:T(8,128)(2,1)}), bf16[32,128,256]{2,1,0:T(8,128)(2,1)S(1)}, u32[]{:S(2)}, u32[]{:S(2)}) async-start(bf16[32,128,256]{2,1,0:T(8,128)(2,1)} %shard_map.65), calls=%async_computation.1 | async-start | bytes 4194304 | tf_op jit(solution)/shard_map/all_to_all | solution.py:84
  13.5 2.7 %copy-start.5 = (s32[1,32]{1,0:T(1,128)S(1)}, s32[1,32]{1,0:T(1,128)}, u32[]{:S(2)}) copy-start(s32[1,32]{1,0:T(1,128)} %param.7) | copy-start | bytes 388
  13.5 2.9 %copy-start.3 = (s32[2048]{0:T(1024)S(1)}, s32[2048]{0:T(1024)}, u32[]{:S(2)}) copy-start(s32[2048]{0:T(1024)} %param.8) | copy-start | bytes 24580
  13.5 3.1 %copy-start.1 = (f32[256,16]{0,1:T(8,128)S(1)}, f32[256,16]{0,1:T(8,128)}, u32[]{:S(2)}) copy-start(f32[256,16]{0,1:T(8,128)} %param.9) | copy-start | bytes 49156
  13.5 3.1 %copy-start.2 = (f32[256,16]{0,1:T(8,128)S(1)}, f32[256,16]{0,1:T(8,128)}, u32[]{:S(2)}) copy-start(f32[256,16]{0,1:T(8,128)} %param.10) | copy-start | bytes 49156
  13.5 3.3 %copy-start.4 = (f32[256]{0:T(256)S(1)}, f32[256]{0:T(256)}, u32[]{:S(2)}) copy-start(f32[256]{0:T(256)} %param.11) | copy-start | bytes 3076
  16.4 29.2 %copy-start = (s32[128]{0:T(128)}, s32[128]{0:T(128)S(1)}, u32[]{:S(2)}) copy-start(s32[128]{0:T(128)S(1)} %pad_add_fusion.starts.starts_ref) | copy-start | bytes 1540
  37.2 32.8 %all-to-all-start = ((bf16[32,128,256]{2,1,0:T(8,128)(2,1)}), bf16[32,128,256]{2,1,0:T(8,128)(2,1)}, u32[]{:S(2)}, u32[]{:S(2)}) async-start(bf16[32,128,256]{2,1,0:T(8,128)(2,1)} %shard_map.64), calls=%async_computation | async-start | bytes 4194304 | tf_op jit(solution)/shard_map/all_to_all | solution.py:84
  49.8 9.0 %collective-permute-start.2 = (f32[24,256]{1,0:T(8,128)S(1)}, f32[24,256]{1,0:T(8,128)S(1)}, u32[]{:S(2)}, u32[]{:S(2)}) collective-permute-start(f32[24,256]{1,0:T(8,128)S(1)} %get-tuple-element.29), channel_id=1, source_target_pairs={{0,96},{1,97},{2,98},{3,99},{4,100},{5,101},{6,102},{7,103},{8,104... | collective-permute-start | bytes 73736 | tf_op jit(solution)/shard_map/ppermute | solution.py:313
  54.8 4.1 %collective-permute-start.1 = (f32[24,256]{1,0:T(8,128)S(1)}, f32[24,256]{1,0:T(8,128)S(1)}, u32[]{:S(2)}, u32[]{:S(2)}) collective-permute-start(f32[24,256]{1,0:T(8,128)S(1)} %get-tuple-element.29), channel_id=1, source_target_pairs={{0,64},{32,96},{1,65},{33,97},{2,66},{34,98},{3,67},{35,99},{4,68}... | collective-permute-start | bytes 73736 | tf_op jit(solution)/shard_map/ppermute | solution.py:313
  56.1 4.3 %collective-permute-start = (f32[24,256]{1,0:T(8,128)S(1)}, f32[24,256]{1,0:T(8,128)S(1)}, u32[]{:S(2)}, u32[]{:S(2)}) collective-permute-start(f32[24,256]{1,0:T(8,128)S(1)} %get-tuple-element.29), channel_id=1, source_target_pairs={{0,32},{32,64},{64,96},{1,33},{33,65},{65,97},{2,34},{34,66},{66,9... | collective-permute-start | bytes 73736 | tf_op jit(solution)/shard_map/ppermute | solution.py:313
